TPU v7x, 256 devices: a whole 4x4x8 slice. The times are simulated.
256 devices in a mesh: seq: 32 (over z, y_hi, core), tp: 8 (over x, y_lo).
Axes of the slice: x: 4, y: 4 (y_hi: 2, y_lo: 2; y = y_hi * 2 + y_lo), z: 8, core: 2. Of those that a mesh axis runs over, the one named last changes fastest.
Arguments:
- stream: bfloat16 [8192, 2048], P('seq', 'tp'), may hold values from -16 to 16
- frames: int32 [8192], P('seq'), may hold values from 0 to 63, never falling along the last dimension, each value on 1 to 256 neighbouring positions
- fidelity: int32 [8192, 1], P('seq'), may hold values from 0 to 15; in each aligned block of 256 rows (0 to 255, 256 to 511, ...) at most 32 rows name the same one
- w_query: bfloat16 [2048, 2048], P(None, 'tp'), may hold values from -2 to 2
- w_key: bfloat16 [2048, 2048], P(None, 'tp'), may hold values from -2 to 2
- w_value: bfloat16 [2048, 2048], P(None, 'tp'), may hold values from -0.125 to 0.125
- w_output: bfloat16 [2048, 2048], P('tp'), may hold values from -0.125 to 0.125
- norm_gain: float32 [2048], replicated, may hold values from 0.1 to 1.9
- expert_gate: bfloat16 [32, 2048, 2816], P('seq', None, 'tp'), may hold values from -0.125 to 0.125
- expert_up: bfloat16 [32, 2048, 2816], P('seq', None, 'tp'), may hold values from -0.125 to 0.125
- expert_down: bfloat16 [32, 2816, 2048], P('seq', 'tp'), may hold values from -0.078125 to 0.078125
Outputs:
- result: bfloat16 [8192, 2048], P('seq', 'tp')
Inputs may be any that keep to these rules, and one draw needn't show every extreme that they name: `frames`: frame numbers never fall along the tokens; a frame holds 1 to 256 tokens, one exactly 256. `fidelity`: among the tokens of one index of seq (aligned blocks of 256 rows) no expert is named more than 32 times, a bound that some block reaches; every expert is named by some token.
All inputs are finite; a program needn't handle non-finite values.
Results may differ from a plain program's by a relative error of at most 0.02.
Values may be sent and summed in bfloat16 or wider, within the bound.
No kernel may reach another device: no remote copies, remote signals or barrier semaphores. Data moves between devices by JAX's collectives and lax.ppermute only.
A program may use at most 128 MiB of HBM per device.

v0:
```python
import functools
import math

import jax
import jax.numpy as jnp
import numpy as np
from jax import lax
from jax.experimental import pallas as pl
from jax.experimental.pallas import tpu as pltpu
from jax.sharding import Mesh, PartitionSpec as P

HEAD = 128
EXPERTS = 16
CAP = 32
BLK = 256
NEG = -1e30
NORM_EPS = 1e-05
SEQ = ("z", "yh", "c")
CHIPS = ("z", "yh")
TP = ("x", "yl")
NEAR = ((0, 0), (1, 0), (3, 1), (3, 0), (1, 1), (0, 1))
FAR = ((2, 0), (2, 1))
F32 = jnp.float32
BF16 = jnp.bfloat16

VMEM = pl.BlockSpec(memory_space=pltpu.VMEM)
HBM = pl.BlockSpec(memory_space=pltpu.HBM)


def nt_dot(a, b):
    return lax.dot_general(a, b, (((1,), (1,)), ((), ())), preferred_element_type=F32)


def tn_dot(a, b):
    return lax.dot_general(a, b, (((0,), (0,)), ((), ())), preferred_element_type=F32)


def vmem(mib):
    return pltpu.CompilerParams(vmem_limit_bytes=mib << 20)


def source_rows(dx, dy):
    x, yl = lax.axis_index("x"), lax.axis_index("yl")
    source = ((x + 4 - dx) % 4) * 2 + (yl + dy) % 2
    return pl.ds(pl.multiple_of(source * BLK, BLK), BLK)


def fetch_kernel(wk, wv, wq, out, sem):
    copies = [
        pltpu.make_async_copy(src, out.at[:, pl.ds(i * BLK, BLK)], sem.at[i])
        for i, src in enumerate((wk, wv, wq))
    ]
    for copy in copies:
        copy.start()
    for copy in copies:
        copy.wait()


def fetch(*weights):
    return pl.pallas_call(
        fetch_kernel,
        out_shape=jax.ShapeDtypeStruct((2048, 3 * BLK), BF16),
        in_specs=[HBM] * 3,
        out_specs=VMEM,
        scratch_shapes=[pltpu.SemaphoreType.DMA((3,))],
        cost_estimate=pl.CostEstimate(flops=0, bytes_accessed=6 << 20, transcendentals=0),
        compiler_params=vmem(8),
        name="fetch",
    )(*weights)


def near_kernel(*refs):
    blocks = refs[:6]
    weights, acc, rest = refs[6:]

    def some(i, carry):
        cols = pl.ds(pl.multiple_of(i * BLK, BLK), BLK)
        total = None
        for block, shift in zip(blocks, NEAR):
            term = jnp.dot(block[...], weights[source_rows(*shift), cols], preferred_element_type=F32)
            total = term if total is None else total + term
        acc[:, cols] = total
        for j, shift in enumerate(FAR):
            rest[j * BLK : (j + 1) * BLK, cols] = weights[source_rows(*shift), cols]
        return carry

    lax.fori_loop(0, 3, some, 0)


def project_near(blocks, weights):
    return pl.pallas_call(
        near_kernel,
        out_shape=(
            jax.ShapeDtypeStruct((BLK, 3 * BLK), F32),
            jax.ShapeDtypeStruct((2 * BLK, 3 * BLK), BF16),
        ),
        in_specs=[VMEM] * 7,
        out_specs=(VMEM,) * 2,
        cost_estimate=pl.CostEstimate(
            flops=2 * BLK * 1536 * 768, bytes_accessed=5 << 20, transcendentals=0
        ),
        compiler_params=vmem(20),
        name="project_near",
    )(*blocks, weights)


def far_kernel(acc, rest, b0, b1, frames, own, other):
    first = lax.axis_index("c") == 0

    def some(i, carry):
        cols = pl.ds(pl.multiple_of(i * BLK, BLK), BLK)
        total = acc[:, cols]
        for j, block in enumerate((b0, b1)):
            total = total + jnp.dot(
                block[...], rest[j * BLK : (j + 1) * BLK, cols], preferred_element_type=F32
            )
        left, right = total[:, :HEAD], total[:, HEAD:]
        cols = pl.ds(pl.multiple_of(i * HEAD, HEAD), HEAD)
        own[:BLK, cols] = jnp.where(first, left, right).astype(BF16)
        other[:BLK, cols] = jnp.where(first, right, left).astype(BF16)
        return carry

    lax.fori_loop(0, 3, some, 0)
    tail = jnp.broadcast_to(frames[...], (16, BLK)).astype(BF16)
    for out in (own, other):
        out[BLK:, : 2 * HEAD] = tail
        out[BLK:, 2 * HEAD :] = tail[:, :HEAD]


def project_far(acc, rest, b0, b1, frames):
    packet = jax.ShapeDtypeStruct((BLK + 16, 3 * HEAD), BF16)
    return pl.pallas_call(
        far_kernel,
        out_shape=(packet, packet),
        in_specs=[VMEM] * 5,
        out_specs=(VMEM,) * 2,
        cost_estimate=pl.CostEstimate(
            flops=2 * BLK * 512 * 768, bytes_accessed=2 << 20, transcendentals=0
        ),
        compiler_params=vmem(16),
        name="project_far",
    )(acc, rest, b0, b1, frames)


def join_kernel(own, got, kv, q):
    row = lax.broadcasted_iota(jnp.int32, (16, BLK), 0)
    both = [ref[BLK:, : 2 * HEAD].astype(F32) for ref in (own, got)]
    tail = jnp.where(row == 0, both[0], both[1])
    for i, ref in enumerate((own, got)):
        rows = slice(i * BLK, (i + 1) * BLK)
        kv[rows, :] = ref[:BLK, : 2 * HEAD]
        q[rows, :] = ref[:BLK, 2 * HEAD :]
    kv[2 * BLK :, :] = tail.astype(BF16)
    row = lax.broadcasted_iota(jnp.int32, (16, HEAD), 0)
    parts = [b[:, h * HEAD : (h + 1) * HEAD] for b in both for h in range(2)]
    lines = jnp.where(row == 0, parts[0], jnp.where(row == 1, parts[1], jnp.where(row == 2, parts[2], parts[3])))
    q[2 * BLK :, :] = lines.astype(BF16)


def join(own, got):
    return pl.pallas_call(
        join_kernel,
        out_shape=(
            jax.ShapeDtypeStruct((2 * BLK + 16, 2 * HEAD), BF16),
            jax.ShapeDtypeStruct((2 * BLK + 16, HEAD), BF16),
        ),
        in_specs=[VMEM] * 2,
        out_specs=(VMEM,) * 2,
        cost_estimate=pl.CostEstimate(flops=BLK * BLK, bytes_accessed=1 << 19, transcendentals=0),
        compiler_params=vmem(8),
        name="join",
    )(own, got)


def visit(q_s, f_s, m_s, l_s, acc_s, kv, masked):
    scale = 1.0 / math.sqrt(HEAD)
    if masked:
        lines = [jnp.broadcast_to(kv[r : r + 1, :].astype(F32), (HEAD, BLK)) for r in (2 * BLK, 2 * BLK + 1)]
        frames = jnp.concatenate([jnp.transpose(line)[:, :1] for line in lines], axis=0)

    def part(i, carry):
        lanes = pl.ds(pl.multiple_of(i * BLK, BLK), BLK)
        s = nt_dot(kv[: 2 * BLK, :HEAD], q_s[lanes, :]) * scale
        if masked:
            allowed = frames <= f_s[:, lanes]
            s = jnp.where(allowed, s, NEG)
        old = m_s[:, lanes]
        top = jnp.maximum(old, jnp.max(s, axis=0, keepdims=True))
        decay = jnp.exp(old - top)
        p = jnp.exp(s - top)
        if masked:
            p = jnp.where(allowed, p, 0.0)
        m_s[:, lanes] = top
        l_s[:, lanes] = l_s[:, lanes] * decay + jnp.sum(p, axis=0, keepdims=True)
        acc_s[:, lanes] = acc_s[:, lanes] * decay + tn_dot(kv[: 2 * BLK, HEAD:], p.astype(BF16))
        return carry

    lax.fori_loop(0, 4, part, 0)


def local_kernel(mine, theirs, kv, q_s, f_s, m_s, l_s, acc_s):
    for g, q in enumerate((mine, theirs)):
        q_s[g * 2 * BLK : (g + 1) * 2 * BLK, :] = q[: 2 * BLK, :]
        for i in range(4):
            lanes = slice((g * 4 + i) * HEAD, (g * 4 + i + 1) * HEAD)
            f_s[:, lanes] = q[2 * BLK + i : 2 * BLK + i + 1, :].astype(F32)
    m_s[...] = jnp.full_like(m_s, NEG)
    l_s[...] = jnp.zeros_like(l_s)
    acc_s[...] = jnp.zeros_like(acc_s)
    visit(q_s, f_s, m_s, l_s, acc_s, kv, True)


STATE = (
    jax.ShapeDtypeStruct((4 * BLK, HEAD), BF16),
    jax.ShapeDtypeStruct((1, 4 * BLK), F32),
    jax.ShapeDtypeStruct((1, 4 * BLK), F32),
    jax.ShapeDtypeStruct((1, 4 * BLK), F32),
    jax.ShapeDtypeStruct((HEAD, 4 * BLK), F32),
)


def visit_cost(blocks):
    work = 1024 * BLK * blocks
    return pl.CostEstimate(flops=4 * work * HEAD, bytes_accessed=2 << 20, transcendentals=work)


def local(mine, theirs, kv):
    return pl.pallas_call(
        local_kernel,
        out_shape=STATE,
        in_specs=[VMEM] * 3,
        out_specs=(VMEM,) * 5,
        cost_estimate=visit_cost(4),
        compiler_params=vmem(24),
        name="local",
    )(mine, theirs, kv)


def step_kernel(k, q_s, f_s, m_i, l_i, acc_i, f, b, m_s, l_s, acc_s, kv):
    z = lax.axis_index("z")
    m_s[...] = m_i[...]
    l_s[...] = l_i[...]
    acc_s[...] = acc_i[...]
    wrapped = z + k >= 8
    if k == 1:
        wrapped = wrapped | (lax.axis_index("yh") == 0)

    def side(j, carry):
        @pl.when((j == 0) & (z >= k))
        def _():
            kv[...] = f[...]

        @pl.when((j == 1) & wrapped)
        def _():
            kv[...] = b[...]

        @pl.when(((j == 0) & (z >= k)) | ((j == 1) & wrapped))
        def _():
            visit(q_s, f_s, m_s, l_s, acc_s, kv, k == 1)

        return carry

    lax.fori_loop(0, 2, side, 0)


def step(k, state, f, b):
    m, l, acc = pl.pallas_call(
        functools.partial(step_kernel, k),
        out_shape=STATE[2:],
        in_specs=[VMEM] * 7,
        out_specs=(VMEM,) * 3,
        scratch_shapes=[pltpu.VMEM(f.shape, BF16)],
        cost_estimate=visit_cost(4),
        compiler_params=vmem(24),
        name="step",
    )(*state, f, b)
    return state[0], state[1], m, l, acc


def last_kernel(q_s, f_s, m_i, l_i, acc_i, kv, mine, theirs, m_s, l_s, acc_s):
    m_s[...] = m_i[...]
    l_s[...] = l_i[...]
    acc_s[...] = acc_i[...]

    @pl.when(lax.axis_index("z") >= 4)
    def _():
        visit(q_s, f_s, m_s, l_s, acc_s, kv, False)

    for g, out in enumerate((mine, theirs)):
        lanes = slice(g * 2 * BLK, (g + 1) * 2 * BLK)
        total = l_s[:, lanes]
        some = total > 0.0
        safe = jnp.where(some, total, 1.0)
        out[:HEAD, :] = (acc_s[:, lanes] * (1.0 / safe)).astype(BF16)
        log = jnp.where(some, m_s[:, lanes] + jnp.log(safe), NEG)
        row = lax.broadcasted_iota(jnp.int32, (16, 2 * BLK), 0)
        high = log.astype(BF16).astype(F32)
        middle = (log - high).astype(BF16).astype(F32)
        low = log - high - middle
        terms = jnp.where(row == 0, high, jnp.where(row == 1, middle, jnp.where(row == 2, low, 0.0)))
        out[HEAD:, :] = terms.astype(BF16)


def last(state, kv):
    return pl.pallas_call(
        last_kernel,
        out_shape=(jax.ShapeDtypeStruct((HEAD + 16, 2 * BLK), BF16),) * 2,
        in_specs=[VMEM] * 6,
        out_specs=(VMEM,) * 2,
        scratch_shapes=[pltpu.VMEM(s.shape, s.dtype) for s in STATE[2:]],
        cost_estimate=visit_cost(2),
        compiler_params=vmem(24),
        name="last",
    )(*state, kv)


def merge_kernel(a, b, mine, other):
    la = jnp.sum(a[HEAD:, :].astype(F32), axis=0, keepdims=True)
    lb = jnp.sum(b[HEAD:, :].astype(F32), axis=0, keepdims=True)
    top = jnp.maximum(la, lb)
    wa, wb = jnp.exp(la - top), jnp.exp(lb - top)
    inv = 1.0 / (wa + wb)
    total = (a[:HEAD, :].astype(F32) * (wa * inv) + b[:HEAD, :].astype(F32) * (wb * inv)).astype(BF16)
    mine[...] = total[:, :BLK]
    other[...] = total[:, BLK:]


def merge(a, b):
    half = jax.ShapeDtypeStruct((HEAD, BLK), BF16)
    return pl.pallas_call(
        merge_kernel,
        out_shape=(half, half),
        in_specs=[VMEM] * 2,
        out_specs=(VMEM,) * 2,
        cost_estimate=pl.CostEstimate(flops=1 << 18, bytes_accessed=1 << 19, transcendentals=1024),
        compiler_params=vmem(8),
        name="merge",
    )(a, b)


def output_kernel(mine, other, w, *outs):
    first = lax.axis_index("c") == 0
    a, b = (jnp.transpose(ref[...].astype(F32)) for ref in (mine, other))
    rows = jnp.concatenate([jnp.where(first, a, b), jnp.where(first, b, a)], axis=1).astype(BF16)
    for out, shift in zip(outs, NEAR + FAR):
        out[...] = jnp.dot(rows, w[:, target_cols(*shift)], preferred_element_type=F32).astype(BF16)


def target_cols(dx, dy):
    x, yl = lax.axis_index("x"), lax.axis_index("yl")
    target = ((x + dx) % 4) * 2 + (yl + dy) % 2
    return pl.ds(pl.multiple_of(target * BLK, BLK), BLK)


def output(mine, other, w):
    return pl.pallas_call(
        output_kernel,
        out_shape=(jax.ShapeDtypeStruct((BLK, BLK), BF16),) * 8,
        in_specs=[VMEM] * 3,
        out_specs=(VMEM,) * 8,
        cost_estimate=pl.CostEstimate(
            flops=2 * BLK * BLK * 2048, bytes_accessed=3 << 20, transcendentals=0
        ),
        compiler_params=vmem(16),
        name="output",
    )(mine, other, w)


def add_kernel(a0, b0, a1, b1, out0, out1):
    out0[...] = (a0[...].astype(F32) + b0[...].astype(F32)).astype(BF16)
    out1[...] = (a1[...].astype(F32) + b1[...].astype(F32)).astype(BF16)


def add_pairs(a0, b0, a1, b1):
    return pl.pallas_call(
        add_kernel,
        out_shape=(jax.ShapeDtypeStruct(a0.shape, BF16),) * 2,
        in_specs=[VMEM] * 4,
        out_specs=(VMEM,) * 2,
        cost_estimate=pl.CostEstimate(flops=a0.size, bytes_accessed=12 * a0.size, transcendentals=0),
        compiler_params=vmem(8),
        name="add_pairs",
    )(a0, b0, a1, b1)


def sum_kernel(*refs):
    total = refs[0][...].astype(F32)
    for ref in refs[1:-1]:
        total = total + ref[...].astype(F32)
    refs[-1][...] = total.astype(BF16)


def sum_all(terms):
    return pl.pallas_call(
        sum_kernel,
        out_shape=jax.ShapeDtypeStruct(terms[0].shape, BF16),
        in_specs=[VMEM] * len(terms),
        out_specs=VMEM,
        cost_estimate=pl.CostEstimate(
            flops=6 * terms[0].size, bytes_accessed=14 * terms[0].size, transcendentals=0
        ),
        compiler_params=vmem(8),
        name="sum_all",
    )(*terms)


def slots_kernel(*refs):
    terms = refs[:6]
    stream, slot, mixed, rows = refs[6:]
    total = stream[...].astype(F32)
    for term in terms:
        total = total + term[...].astype(F32)
    kept = total.astype(BF16)
    mixed[...] = kept
    ids = lax.broadcasted_iota(jnp.int32, (EXPERTS * CAP, BLK), 0)
    pick = jnp.where(ids == slot[...], 1.0, 0.0).astype(BF16)
    rows[...] = jnp.dot(pick, kept, preferred_element_type=F32).astype(BF16)


def to_slots(terms, stream, slot):
    return pl.pallas_call(
        slots_kernel,
        out_shape=(
            jax.ShapeDtypeStruct((BLK, BLK), BF16),
            jax.ShapeDtypeStruct((EXPERTS * CAP, BLK), BF16),
        ),
        in_specs=[VMEM] * 8,
        out_specs=(VMEM, VMEM),
        cost_estimate=pl.CostEstimate(
            flops=2 * 512 * BLK * BLK, bytes_accessed=2 << 20, transcendentals=0
        ),
        compiler_params=vmem(16),
        name="slots",
    )(*terms, stream, slot)


UNITS = 704
WIDE = 768
SOME = 64


def prepare(blocks, shifts, places, gain, n_s, square):
    def some_rows(i, carry):
        at = pl.ds(pl.multiple_of(i * SOME, SOME), SOME)
        total = None
        for block, shift, cols in zip(blocks, shifts, places):
            v = block[at, :].astype(F32)
            n_s[at, cols] = (v * gain[:, source_rows(*shift)]).astype(BF16)
            total = v * v if total is None else total + v * v
        square[at, :] = jnp.sum(total, axis=1, keepdims=True)
        return carry

    lax.fori_loop(0, blocks[0].shape[0] // SOME, some_rows, 0)


def expert_near_kernel(*refs):
    blocks = refs[:6]
    gain, own, far = refs[6:9]
    acc, square, rest, w2 = refs[9:13]
    n_s, w1, sem = refs[13:]
    half = UNITS // 2
    places = [(w1, 0), (w1, WIDE), (w2, 0)]
    copies = [
        pltpu.make_async_copy(
            src.at[pl.ds(i * half, half), :], dst.at[pl.ds(at + j * half, half), :], sem.at[3 * j + i]
        )
        for i, (dst, at) in enumerate(places)
        for j, src in enumerate((own, far))
    ]
    for copy in copies:
        copy.start()
    pad = jnp.zeros((WIDE - UNITS, 2048), BF16)
    w1[UNITS:WIDE, :] = pad
    w1[WIDE + UNITS :, :] = pad
    w2[UNITS:, :] = pad
    for shift in FAR:
        n_s[:, source_rows(*shift)] = jnp.zeros((n_s.shape[0], BLK), BF16)
    prepare(blocks, NEAR, [source_rows(*shift) for shift in NEAR], gain, n_s, square)
    for copy in copies:
        copy.wait()
    for j, shift in enumerate(FAR):
        rest[:, j * BLK : (j + 1) * BLK] = w1[:, source_rows(*shift)]

    def tile(j, carry):
        cols = pl.ds(pl.multiple_of(j * BLK, BLK), BLK)
        acc[:, cols] = nt_dot(n_s[...], w1[cols, :])
        return carry

    lax.fori_loop(0, 2 * WIDE // BLK, tile, 0)


def expert_near(blocks, gain, own, far):
    rows = blocks[0].shape[0]
    return pl.pallas_call(
        expert_near_kernel,
        out_shape=(
            jax.ShapeDtypeStruct((rows, 2 * WIDE), F32),
            jax.ShapeDtypeStruct((rows, 1), F32),
            jax.ShapeDtypeStruct((2 * WIDE, 2 * BLK), BF16),
            jax.ShapeDtypeStruct((WIDE, 2048), BF16),
        ),
        in_specs=[VMEM] * 7 + [HBM] * 2,
        out_specs=(VMEM,) * 4,
        scratch_shapes=[
            pltpu.VMEM((rows, 2048), BF16),
            pltpu.VMEM((2 * WIDE, 2048), BF16),
            pltpu.SemaphoreType.DMA((6,)),
        ],
        cost_estimate=pl.CostEstimate(
            flops=4 * rows * 2048 * WIDE, bytes_accessed=13 << 20, transcendentals=0
        ),
        compiler_params=vmem(24),
        name="expert_near",
    )(*blocks, gain, own, far)


def expert_far_kernel(b0, b1, gain, acc, square, rest, w2, *refs):
    outs = refs[:8]
    n_s, h_s, r_s = refs[8:]
    rows = n_s.shape[0]
    prepare((b0, b1), FAR, (slice(0, BLK), slice(BLK, 2 * BLK)), gain, n_s, r_s)
    factor = lax.rsqrt((square[...] + r_s[...]) * (1.0 / 2048) + NORM_EPS)

    def hidden(j, carry):
        cols = pl.ds(pl.multiple_of(j * BLK, BLK), BLK)
        later = pl.ds(pl.multiple_of(WIDE + j * BLK, BLK), BLK)
        g = (acc[:, cols] + nt_dot(n_s[...], rest[cols, :])) * factor
        u = (acc[:, later] + nt_dot(n_s[...], rest[later, :])) * factor
        h_s[:, cols] = (g / (1.0 + jnp.exp(-g)) * u).astype(BF16)
        return carry

    lax.fori_loop(0, WIDE // BLK, hidden, 0)

    def lower(i, carry):
        at = pl.ds(pl.multiple_of(i * BLK, BLK), BLK)
        for out, shift in zip(outs, NEAR + FAR):
            out[at, :] = jnp.dot(
                h_s[at, :], w2[:, target_cols(*shift)], preferred_element_type=F32
            ).astype(BF16)
        return carry

    lax.fori_loop(0, rows // BLK, lower, 0)


def expert_far(b0, b1, gain, acc, square, rest, w2):
    rows = b0.shape[0]
    return pl.pallas_call(
        expert_far_kernel,
        out_shape=(jax.ShapeDtypeStruct(b0.shape, BF16),) * 8,
        in_specs=[VMEM] * 7,
        out_specs=(VMEM,) * 8,
        scratch_shapes=[
            pltpu.VMEM((rows, 2 * BLK), BF16),
            pltpu.VMEM((rows, WIDE), BF16),
            pltpu.VMEM((rows, 1), F32),
        ],
        cost_estimate=pl.CostEstimate(
            flops=4 * rows * 1024 * WIDE, bytes_accessed=10 << 20, transcendentals=rows * WIDE
        ),
        compiler_params=vmem(24),
        name="expert_far",
    )(b0, b1, gain, acc, square, rest, w2)


def finish_kernel(mixed, rows, slot, out):
    ids = lax.broadcasted_iota(jnp.int32, (EXPERTS * CAP, BLK), 0)
    pick = jnp.where(ids == slot[...], 1.0, 0.0).astype(BF16)
    out[...] = (mixed[...].astype(F32) + tn_dot(pick, rows[...])).astype(BF16)


def finish(mixed, rows, slot):
    return pl.pallas_call(
        finish_kernel,
        out_shape=jax.ShapeDtypeStruct((BLK, BLK), BF16),
        in_specs=[VMEM] * 3,
        out_specs=VMEM,
        cost_estimate=pl.CostEstimate(
            flops=2 * 512 * BLK * BLK, bytes_accessed=1 << 20, transcendentals=0
        ),
        compiler_params=vmem(8),
        name="finish",
    )(mixed, rows, slot)


def tp_shift(a, dx, dy):
    pairs = [(i * 2 + j, ((i + dx) % 4) * 2 + (j + dy) % 2) for i in range(4) for j in range(2)]
    return lax.ppermute(a, TP, pairs)


def tp_gather(a):
    near = [a] + [tp_shift(a, *s) for s in NEAR[1:]]
    return near + [tp_shift(near[1], 1, 0), tp_shift(near[2], 3, 0)]


def tp_scatter(pieces):
    got = tp_shift(pieces[6], 1, 0), tp_shift(pieces[7], 3, 0)
    straight = [tp_shift(p, *s) for p, s in zip(pieces[3:6], NEAR[3:6])]
    sums = add_pairs(pieces[1], got[0], pieces[2], got[1])
    return [pieces[0]] + straight + [tp_shift(p, *s) for p, s in zip(sums, NEAR[1:3])]


def swap(a, dy, dc):
    pairs = [(i * 2 + j, (i ^ dy) * 2 + (j ^ dc)) for i in range(2) for j in range(2)]
    return lax.ppermute(a, ("yh", "c"), pairs)


def ring(a, step):
    return lax.ppermute(a, "z", [(i, (i + step) % 8) for i in range(8)])


def attention(blocks, wq, wk, wv, frames, weights):
    acc, rest = project_near(blocks[:6], fetch(wk, wv, wq))
    own, other = project_far(acc, rest, *blocks[6:], frames)
    kv, q = join(own, swap(other, 0, 1))
    f, b = ring(kv, 1), ring(kv, -1)
    theirs = swap(q, 1, 0)
    f, b, theirs = lax.optimization_barrier((f, b, theirs))
    state = local(q, theirs, kv)
    for k in range(1, 4):
        if k == 2:
            f, b, *held = lax.optimization_barrier((f, b, *state, *weights))
            state, weights = held[:5], held[5:]
            weights = jnp.concatenate(weights, axis=0)
        if k == 3:
            f, b, weights, *state = lax.optimization_barrier((f, b, weights, *state))
        here = f, b
        if k < 3:
            f, b = ring(f, 1), ring(b, -1)
        else:
            way = jnp.where(lax.axis_index("c") == 0, f, b)
            hops = [(i * 2 + c, (i + (-1 if c else 1)) % 8 * 2 + c) for i in range(8) for c in range(2)]
            far = lax.ppermute(way, ("z", "c"), hops)
        state = step(k, state, *here)
    mine, theirs = last(state, far)
    mine, other = merge(mine, swap(theirs, 1, 0))
    return mine, swap(other, 0, 1), weights


def shards(stream, frames, fidelity, wq, wk, wv, wo, gain, gate, up, down):
    route = fidelity[:, 0]
    spot = lax.iota(jnp.int32, BLK)
    same = (route[:, None] == route[None, :]) & (spot[None, :] < spot[:, None])
    slot = (route * CAP + jnp.sum(same.astype(jnp.int32), axis=1))[None, :]
    gain = gain[None, :]

    expert_weights = (gate[0].T, up[0].T, down[0])
    mine, other, own = attention(tp_gather(stream), wq, wk, wv, frames[None, :], expert_weights)
    mixed, rows = to_slots(tp_scatter(output(mine, other, wo)), stream, slot)

    sending, rows = lax.optimization_barrier((own, rows))
    far = lax.ppermute(sending, "c", [(0, 1), (1, 0)])
    sent = lax.all_to_all(rows.reshape(EXPERTS, CAP, BLK), CHIPS, 0, 0, tiled=True)
    sent, far = lax.optimization_barrier((sent, far))
    blocks = tp_gather(sent.reshape(EXPERTS * CAP, BLK))
    lowered = expert_far(*blocks[6:], gain, *expert_near(blocks[:6], gain, own, far))
    summed = sum_all(tp_scatter(lowered))
    back = lax.all_to_all(summed.reshape(EXPERTS, CAP, BLK), CHIPS, 0, 0, tiled=True)
    return finish(mixed, back.reshape(EXPERTS * CAP, BLK), slot)


def solution(mesh):
    axes = ("z", "yh", "c", "x", "yl")
    fine = Mesh(np.asarray(mesh.devices).reshape(8, 2, 2, 4, 2), axes)
    return jax.shard_map(
        shards,
        mesh=fine,
        in_specs=(
            P(SEQ, TP),
            P(SEQ),
            P(SEQ, None),
            P(None, TP),
            P(None, TP),
            P(None, TP),
            P(TP, None),
            P(),
            P(SEQ, None, TP),
            P(SEQ, None, TP),
            P(SEQ, TP, None),
        ),
        out_specs=P(SEQ, TP),
        check_vma=False,
    )
```

profile of v0, /device:TPU:6, one launch (start us, length us, event | category | flops | bytes accessed | tf_op | source)
XLA Modules:
  0.0 182.0 jit_solution(4861873983262418029)
XLA Ops:
  3.9 2.5 %collective-permute-start.3 = (bf16[256,256]{1,0:T(8,128)(2,1)}, bf16[256,256]{1,0:T(8,128)(2,1)S(1)}, u32[]{:S(2)}, u32[]{:S(2)}) collective-permute-start(bf16[256,256]{1,0:T(8,128)(2,1)} %refs_6_.1), channel_id=1, source_target_pairs={{0,3},{1,2},{2,5},{3,4},{4,7},{5,6},{6,1},{7,0},{8,11},{9,10},{10,... | collective-permute-start | bytes 393224 | tf_op jit(solution)/shard_map/ppermute | solution.py:587
  20.2 4.0 %collective-permute-start.9 = (bf16[528,256]{1,0:T(8,128)(2,1)S(1)}, bf16[528,256]{1,0:T(8,128)(2,1)S(1)}, u32[]{:S(2)}, u32[]{:S(2)}) collective-permute-start(bf16[528,256]{1,0:T(8,128)(2,1)S(1)} %get-tuple-element.84.kv), channel_id=1, source_target_pairs={{0,224},{32,0},{64,32},{96,64},{128,96},{160,128},{192,160},{224,1... | collective-permute-start | bytes 811016 | tf_op jit(solution)/shard_map/ppermute | solution.py:608
  24.3 3.3 %collective-permute-start.10 = (bf16[528,128]{1,0:T(8,128)(2,1)S(1)}, bf16[528,128]{1,0:T(8,128)(2,1)S(1)}, u32[]{:S(2)}, u32[]{:S(2)}) collective-permute-start(bf16[528,128]{1,0:T(8,128)(2,1)S(1)} %get-tuple-element.85.mine), channel_id=1, source_target_pairs={{0,16},{8,24},{16,0},{24,8},{1,17},{9,25},{17,1},{25,9},{2,18},{10... | collective-permute-start | bytes 405512 | tf_op jit(solution)/shard_map/ppermute | solution.py:604
  27.6 3.6 %collective-permute-done.10.theirs = bf16[528,128]{1,0:T(8,128)(2,1)S(1)} collective-permute-done((bf16[528,128]{1,0:T(8,128)(2,1)S(1)}, bf16[528,128]{1,0:T(8,128)(2,1)S(1)}, u32[]{:S(2)}, u32[]{:S(2)}) %collective-permute-start.10) | collective-permute-done | bytes 135200 | tf_op jit(solution)/shard_map/ppermute | solution.py:604
  31.2 3.2 %collective-permute-start.12 = (bf16[528,256]{1,0:T(8,128)(2,1)S(1)}, bf16[528,256]{1,0:T(8,128)(2,1)S(1)}, u32[]{:S(2)}, u32[]{:S(2)}) collective-permute-start(bf16[528,256]{1,0:T(8,128)(2,1)S(1)} %collective-permute-done.9.b), channel_id=1, source_target_pairs={{0,224},{32,0},{64,32},{96,64},{128,96},{160,128},{192,160},{224,1... | collective-permute-start | bytes 811016 | tf_op jit(solution)/shard_map/ppermute | solution.py:608
  44.1 4.6 %collective-permute-done.13.f = bf16[528,256]{1,0:T(8,128)(2,1)S(1)} collective-permute-done((bf16[528,256]{1,0:T(8,128)(2,1)S(1)}, bf16[528,256]{1,0:T(8,128)(2,1)S(1)}, u32[]{:S(2)}, u32[]{:S(2)}) %collective-permute-start.13) | collective-permute-done | bytes 270368 | tf_op jit(solution)/shard_map/ppermute | solution.py:608
  50.9 5.8 %collective-permute-done.15.kv = bf16[528,256]{1,0:T(8,128)(2,1)S(1)} collective-permute-done((bf16[528,256]{1,0:T(8,128)(2,1)S(1)}, bf16[528,256]{1,0:T(8,128)(2,1)S(1)}, u32[]{:S(2)}, u32[]{:S(2)}) %collective-permute-start.15) | collective-permute-done | bytes 270368 | tf_op jit(solution)/shard_map/ppermute | solution.py:632
  56.9 3.1 %collective-permute-start.16 = (bf16[144,512]{1,0:T(8,128)(2,1)S(1)}, bf16[144,512]{1,0:T(8,128)(2,1)S(1)}, u32[]{:S(2)}, u32[]{:S(2)}) collective-permute-start(bf16[144,512]{1,0:T(8,128)(2,1)S(1)} %get-tuple-element.121), channel_id=1, source_target_pairs={{0,16},{8,24},{16,0},{24,8},{1,17},{9,25},{17,1},{25,9},{2,18},{10... | collective-permute-start | bytes 442376 | tf_op jit(solution)/shard_map/ppermute | solution.py:604
  59.9 3.6 %collective-permute-done.16.b = bf16[144,512]{1,0:T(8,128)(2,1)S(1)} collective-permute-done((bf16[144,512]{1,0:T(8,128)(2,1)S(1)}, bf16[144,512]{1,0:T(8,128)(2,1)S(1)}, u32[]{:S(2)}, u32[]{:S(2)}) %collective-permute-start.16) | collective-permute-done | bytes 147488 | tf_op jit(solution)/shard_map/ppermute | solution.py:604
  65.5 2.9 %collective-permute-start.21 = (bf16[256,256]{1,0:T(8,128)(2,1)S(1)}, bf16[256,256]{1,0:T(8,128)(2,1)S(1)}, u32[]{:S(2)}, u32[]{:S(2)}) collective-permute-start(bf16[256,256]{1,0:T(8,128)(2,1)S(1)} %get-tuple-element.129), channel_id=1, source_target_pairs={{0,2},{1,3},{2,4},{3,5},{4,6},{5,7},{6,0},{7,1},{8,10},{9,11},{10,... | collective-permute-start | bytes 393224 | tf_op jit(solution)/shard_map/ppermute | solution.py:587
  68.7 4.8 %collective-permute-start.19 = (bf16[256,256]{1,0:T(8,128)(2,1)S(1)}, bf16[256,256]{1,0:T(8,128)(2,1)S(1)}, u32[]{:S(2)}, u32[]{:S(2)}) collective-permute-start(bf16[256,256]{1,0:T(8,128)(2,1)S(1)} %get-tuple-element.126), channel_id=1, source_target_pairs={{0,3},{1,2},{2,5},{3,4},{4,7},{5,6},{6,1},{7,0},{8,11},{9,10},{10,... | collective-permute-start | bytes 393224 | tf_op jit(solution)/shard_map/ppermute | solution.py:587
  73.5 2.5 %collective-permute-done.22.b1 = bf16[256,256]{1,0:T(8,128)(2,1)S(1)} collective-permute-done((bf16[256,256]{1,0:T(8,128)(2,1)S(1)}, bf16[256,256]{1,0:T(8,128)(2,1)S(1)}, u32[]{:S(2)}, u32[]{:S(2)}) %collective-permute-start.22) | collective-permute-done | bytes 131104 | tf_op jit(solution)/shard_map/ppermute | solution.py:587
  76.2 3.5 %collective-permute-start.24 = (bf16[256,256]{1,0:T(8,128)(2,1)S(1)}, bf16[256,256]{1,0:T(8,128)(2,1)S(1)}, u32[]{:S(2)}, u32[]{:S(2)}) collective-permute-start(bf16[256,256]{1,0:T(8,128)(2,1)S(1)} %get-tuple-element.133), channel_id=1, source_target_pairs={{0,7},{1,6},{2,1},{3,0},{4,3},{5,2},{6,5},{7,4},{8,15},{9,14},{10,... | collective-permute-start | bytes 393224 | tf_op jit(solution)/shard_map/ppermute | solution.py:587
  83.8 23.4 %all_to_all.10 = bf16[16,32,256]{2,1,0:T(8,128)(2,1)S(1)} all-to-all(bf16[16,32,256]{2,1,0:T(8,128)(2,1)S(1)} %bitcast.25), channel_id=1, replica_groups=mesh['z'=8,'yh'=2,'c'=2,'x'=4,'yl'=2] {'z','yh'}, dimensions={0} | all-to-all | bytes 524288 | tf_op jit(solution)/shard_map/all_to_all | solution.py:652
  110.7 2.7 %collective-permute-start.31 = (bf16[512,256]{1,0:T(8,128)(2,1)S(1)}, bf16[512,256]{1,0:T(8,128)(2,1)S(1)}, u32[]{:S(2)}, u32[]{:S(2)}) collective-permute-start(bf16[512,256]{1,0:T(8,128)(2,1)S(1)} %bitcast.22), channel_id=1, source_target_pairs={{0,3},{1,2},{2,5},{3,4},{4,7},{5,6},{6,1},{7,0},{8,11},{9,10},{10,... | collective-permute-start | bytes 786440 | tf_op jit(solution)/shard_map/ppermute | solution.py:587
  118.6 2.5 %collective-permute-done.28.refs_2_ = bf16[512,256]{1,0:T(8,128)(2,1)S(1)} collective-permute-done((bf16[512,256]{1,0:T(8,128)(2,1)S(1)}, bf16[512,256]{1,0:T(8,128)(2,1)S(1)}, u32[]{:S(2)}, u32[]{:S(2)}) %collective-permute-start.28) | collective-permute-done | bytes 262176 | tf_op jit(solution)/shard_map/ppermute | solution.py:587
  121.1 2.9 %collective-permute-done.30.refs_3_ = bf16[512,256]{1,0:T(8,128)(2,1)S(1)} collective-permute-done((bf16[512,256]{1,0:T(8,128)(2,1)S(1)}, bf16[512,256]{1,0:T(8,128)(2,1)S(1)}, u32[]{:S(2)}, u32[]{:S(2)}) %collective-permute-start.30) | collective-permute-done | bytes 262176 | tf_op jit(solution)/shard_map/ppermute | solution.py:587
  124.5 4.3 %collective-permute-done.32.refs_5_ = bf16[512,256]{1,0:T(8,128)(2,1)S(1)} collective-permute-done((bf16[512,256]{1,0:T(8,128)(2,1)S(1)}, bf16[512,256]{1,0:T(8,128)(2,1)S(1)}, u32[]{:S(2)}, u32[]{:S(2)}) %collective-permute-start.32) | collective-permute-done | bytes 262176 | tf_op jit(solution)/shard_map/ppermute | solution.py:587
  128.8 7.6 %expert_near.1 = (f32[512,1536]{1,0:T(8,128)S(1)}, f32[512,1]{1,0:T(8,128)S(1)}, bf16[1536,512]{1,0:T(8,128)(2,1)S(1)}, bf16[768,2048]{1,0:T(8,128)(2,1)S(1)}) custom-call(bf16[512,256]{1,0:T(8,128)(2,1)S(1)} %bitcast.24, bf16[512,256]{1,0:T(8,128)(2,1)S(1)} %collective-permute-done.26.refs_1_, bf16[512,256]{1,0:T(8,128)(2,1)S(1)} %collective-permute-done.28.refs_2_, ...), custom_call_target="tpu_custom_call" | custom-call | flops 3221225472 | bytes 13631488 | tf_op jit(solution)/shard_map/expert_near/pallas_call | solution.py:494
  136.4 4.5 %expert_far.1 = (bf16[512,256]{1,0:T(8,128)(2,1)S(1)}, bf16[512,256]{1,0:T(8,128)(2,1)S(1)}, bf16[512,256]{1,0:T(8,128)(2,1)S(1)}, bf16[512,256]{1,0:T(8,128)(2,...) custom-call(bf16[512,256]{1,0:T(8,128)(2,1)S(1)} %collective-permute, ...), custom_call_target="tpu_custom_call" | custom-call | flops 1610612736 | bytes 10485760 | tf_op jit(solution)/shard_map/expert_far/pallas_call | solution.py:547
  143.0 2.8 %collective-permute-start.34 = (bf16[512,256]{1,0:T(8,128)(2,1)S(1)}, bf16[512,256]{1,0:T(8,128)(2,1)S(1)}, u32[]{:S(2)}, u32[]{:S(2)}) collective-permute-start(bf16[512,256]{1,0:T(8,128)(2,1)S(1)} %get-tuple-element.147), channel_id=1, source_target_pairs={{0,3},{1,2},{2,5},{3,4},{4,7},{5,6},{6,1},{7,0},{8,11},{9,10},{10,... | collective-permute-start | bytes 786440 | tf_op jit(solution)/shard_map/ppermute | solution.py:587
  153.3 3.7 %collective-permute-done.33.refs_1_ = bf16[512,256]{1,0:T(8,128)(2,1)S(1)} collective-permute-done((bf16[512,256]{1,0:T(8,128)(2,1)S(1)}, bf16[512,256]{1,0:T(8,128)(2,1)S(1)}, u32[]{:S(2)}, u32[]{:S(2)}) %collective-permute-start.33) | collective-permute-done | bytes 262176 | tf_op jit(solution)/shard_map/ppermute | solution.py:587
  157.1 7.2 %collective-permute-done.35.refs_3_ = bf16[512,256]{1,0:T(8,128)(2,1)S(1)} collective-permute-done((bf16[512,256]{1,0:T(8,128)(2,1)S(1)}, bf16[512,256]{1,0:T(8,128)(2,1)S(1)}, u32[]{:S(2)}, u32[]{:S(2)}) %collective-permute-start.35) | collective-permute-done | bytes 262176 | tf_op jit(solution)/shard_map/ppermute | solution.py:587
  164.5 16.5 %all_to_all.11 = bf16[16,32,256]{2,1,0:T(8,128)(2,1)S(1)} all-to-all(bf16[16,32,256]{2,1,0:T(8,128)(2,1)S(1)} %bitcast.17), channel_id=1, replica_groups=mesh['z'=8,'yh'=2,'c'=2,'x'=4,'yl'=2] {'z','yh'}, dimensions={0} | all-to-all | bytes 524288 | tf_op jit(solution)/shard_map/all_to_all | solution.py:657
  (102 shorter events, 55.9 us)
Async XLA Ops:
  3.0 11.0 %collective-permute-start.2 = (bf16[256,256]{1,0:T(8,128)(2,1)}, bf16[256,256]{1,0:T(8,128)(2,1)S(1)}, u32[]{:S(2)}, u32[]{:S(2)}) collective-permute-start(bf16[256,256]{1,0:T(8,128)(2,1)} %refs_6_.1), channel_id=1, source_target_pairs={{0,6},{1,7},{2,0},{3,1},{4,2},{5,3},{6,4},{7,5},{8,14},{9,15},{10,... | collective-permute-start | bytes 393224 | tf_op jit(solution)/shard_map/ppermute | solution.py:587
  3.9 10.2 %collective-permute-start.3 = (bf16[256,256]{1,0:T(8,128)(2,1)}, bf16[256,256]{1,0:T(8,128)(2,1)S(1)}, u32[]{:S(2)}, u32[]{:S(2)}) collective-permute-start(bf16[256,256]{1,0:T(8,128)(2,1)} %refs_6_.1), channel_id=1, source_target_pairs={{0,3},{1,2},{2,5},{3,4},{4,7},{5,6},{6,1},{7,0},{8,11},{9,10},{10,... | collective-permute-start | bytes 393224 | tf_op jit(solution)/shard_map/ppermute | solution.py:587
  18.6 12.6 %collective-permute-start.8 = (bf16[528,256]{1,0:T(8,128)(2,1)S(1)}, bf16[528,256]{1,0:T(8,128)(2,1)S(1)}, u32[]{:S(2)}, u32[]{:S(2)}) collective-permute-start(bf16[528,256]{1,0:T(8,128)(2,1)S(1)} %get-tuple-element.84.kv), channel_id=1, source_target_pairs={{0,32},{32,64},{64,96},{96,128},{128,160},{160,192},{192,224},{224... | collective-permute-start | bytes 811016 | tf_op jit(solution)/shard_map/ppermute | solution.py:608
  20.2 11.0 %collective-permute-start.9 = (bf16[528,256]{1,0:T(8,128)(2,1)S(1)}, bf16[528,256]{1,0:T(8,128)(2,1)S(1)}, u32[]{:S(2)}, u32[]{:S(2)}) collective-permute-start(bf16[528,256]{1,0:T(8,128)(2,1)S(1)} %get-tuple-element.84.kv), channel_id=1, source_target_pairs={{0,224},{32,0},{64,32},{96,64},{128,96},{160,128},{192,160},{224,1... | collective-permute-start | bytes 811016 | tf_op jit(solution)/shard_map/ppermute | solution.py:608
  31.2 9.0 %collective-permute-start.11 = (bf16[528,256]{1,0:T(8,128)(2,1)S(1)}, bf16[528,256]{1,0:T(8,128)(2,1)S(1)}, u32[]{:S(2)}, u32[]{:S(2)}) collective-permute-start(bf16[528,256]{1,0:T(8,128)(2,1)S(1)} %collective-permute-done.8.f), channel_id=1, source_target_pairs={{0,32},{32,64},{64,96},{96,128},{128,160},{160,192},{192,224},{224... | collective-permute-start | bytes 811016 | tf_op jit(solution)/shard_map/ppermute | solution.py:608
  31.2 9.0 %collective-permute-start.12 = (bf16[528,256]{1,0:T(8,128)(2,1)S(1)}, bf16[528,256]{1,0:T(8,128)(2,1)S(1)}, u32[]{:S(2)}, u32[]{:S(2)}) collective-permute-start(bf16[528,256]{1,0:T(8,128)(2,1)S(1)} %collective-permute-done.9.b), channel_id=1, source_target_pairs={{0,224},{32,0},{64,32},{96,64},{128,96},{160,128},{192,160},{224,1... | collective-permute-start | bytes 811016 | tf_op jit(solution)/shard_map/ppermute | solution.py:608
  40.2 8.5 %collective-permute-start.13 = (bf16[528,256]{1,0:T(8,128)(2,1)S(1)}, bf16[528,256]{1,0:T(8,128)(2,1)S(1)}, u32[]{:S(2)}, u32[]{:S(2)}) collective-permute-start(bf16[528,256]{1,0:T(8,128)(2,1)S(1)} %collective-permute-done.11.f), channel_id=1, source_target_pairs={{0,32},{32,64},{64,96},{96,128},{128,160},{160,192},{192,224},{224... | collective-permute-start | bytes 811016 | tf_op jit(solution)/shard_map/ppermute | solution.py:608
  68.6 11.1 %collective-permute-start.18 = (bf16[256,256]{1,0:T(8,128)(2,1)S(1)}, bf16[256,256]{1,0:T(8,128)(2,1)S(1)}, u32[]{:S(2)}, u32[]{:S(2)}) collective-permute-start(bf16[256,256]{1,0:T(8,128)(2,1)S(1)} %get-tuple-element.125), channel_id=1, source_target_pairs={{0,6},{1,7},{2,0},{3,1},{4,2},{5,3},{6,4},{7,5},{8,14},{9,15},{10,... | collective-permute-start | bytes 393224 | tf_op jit(solution)/shard_map/ppermute | solution.py:587
  68.7 11.0 %collective-permute-start.19 = (bf16[256,256]{1,0:T(8,128)(2,1)S(1)}, bf16[256,256]{1,0:T(8,128)(2,1)S(1)}, u32[]{:S(2)}, u32[]{:S(2)}) collective-permute-start(bf16[256,256]{1,0:T(8,128)(2,1)S(1)} %get-tuple-element.126), channel_id=1, source_target_pairs={{0,3},{1,2},{2,5},{3,4},{4,7},{5,6},{6,1},{7,0},{8,11},{9,10},{10,... | collective-permute-start | bytes 393224 | tf_op jit(solution)/shard_map/ppermute | solution.py:587
  83.7 23.5 %collective-permute-start.25 = (bf16[1056,2048]{1,0:T(8,128)(2,1)S(1)}, bf16[1056,2048]{1,0:T(8,128)(2,1)S(1)}, u32[]{:S(2)}, u32[]{:S(2)}) collective-permute-start(bf16[1056,2048]{1,0:T(8,128)(2,1)S(1)} %pad_maximum_fusion.refs_7_), channel_id=1, source_target_pairs={{0,8},{8,0},{1,9},{9,1},{2,10},{10,2},{3,11},{11,3},{4,12},{12,4},... | collective-permute-start | bytes 12976136 | tf_op jit(solution)/shard_map/ppermute | solution.py:651
  107.3 9.2 %collective-permute-start.26 = (bf16[512,256]{1,0:T(8,128)(2,1)S(1)}, bf16[512,256]{1,0:T(8,128)(2,1)S(1)}, u32[]{:S(2)}, u32[]{:S(2)}) collective-permute-start(bf16[512,256]{1,0:T(8,128)(2,1)S(1)} %bitcast.19), channel_id=1, source_target_pairs={{0,2},{1,3},{2,4},{3,5},{4,6},{5,7},{6,0},{7,1},{8,10},{9,11},{10,... | collective-permute-start | bytes 786440 | tf_op jit(solution)/shard_map/ppermute | solution.py:587
  108.7 12.4 %collective-permute-start.28 = (bf16[512,256]{1,0:T(8,128)(2,1)S(1)}, bf16[512,256]{1,0:T(8,128)(2,1)S(1)}, u32[]{:S(2)}, u32[]{:S(2)}) collective-permute-start(bf16[512,256]{1,0:T(8,128)(2,1)S(1)} %bitcast.20), channel_id=1, source_target_pairs={{0,7},{1,6},{2,1},{3,0},{4,3},{5,2},{6,5},{7,4},{8,15},{9,14},{10,... | collective-permute-start | bytes 786440 | tf_op jit(solution)/shard_map/ppermute | solution.py:587
  110.0 14.0 %collective-permute-start.30 = (bf16[512,256]{1,0:T(8,128)(2,1)S(1)}, bf16[512,256]{1,0:T(8,128)(2,1)S(1)}, u32[]{:S(2)}, u32[]{:S(2)}) collective-permute-start(bf16[512,256]{1,0:T(8,128)(2,1)S(1)} %bitcast.21), channel_id=1, source_target_pairs={{0,6},{1,7},{2,0},{3,1},{4,2},{5,3},{6,4},{7,5},{8,14},{9,15},{10,... | collective-permute-start | bytes 786440 | tf_op jit(solution)/shard_map/ppermute | solution.py:587
  110.7 13.7 %collective-permute-start.31 = (bf16[512,256]{1,0:T(8,128)(2,1)S(1)}, bf16[512,256]{1,0:T(8,128)(2,1)S(1)}, u32[]{:S(2)}, u32[]{:S(2)}) collective-permute-start(bf16[512,256]{1,0:T(8,128)(2,1)S(1)} %bitcast.22), channel_id=1, source_target_pairs={{0,3},{1,2},{2,5},{3,4},{4,7},{5,6},{6,1},{7,0},{8,11},{9,10},{10,... | collective-permute-start | bytes 786440 | tf_op jit(solution)/shard_map/ppermute | solution.py:587
  113.4 15.4 %collective-permute-start.32 = (bf16[512,256]{1,0:T(8,128)(2,1)S(1)}, bf16[512,256]{1,0:T(8,128)(2,1)S(1)}, u32[]{:S(2)}, u32[]{:S(2)}) collective-permute-start(bf16[512,256]{1,0:T(8,128)(2,1)S(1)} %bitcast.23), channel_id=1, source_target_pairs={{0,1},{1,0},{2,3},{3,2},{4,5},{5,4},{6,7},{7,6},{8,9},{9,8},{10,11... | collective-permute-start | bytes 786440 | tf_op jit(solution)/shard_map/ppermute | solution.py:587
  116.5 19.9 %collective-permute-start.27 = (bf16[512,256]{1,0:T(8,128)(2,1)S(1)}, bf16[512,256]{1,0:T(8,128)(2,1)S(1)}, u32[]{:S(2)}, u32[]{:S(2)}) collective-permute-start(bf16[512,256]{1,0:T(8,128)(2,1)S(1)} %collective-permute-done.26.refs_1_), channel_id=1, source_target_pairs={{0,2},{1,3},{2,4},{3,5},{4,6},{5,7},{6,0},{7,1},{8,10},{9,11},{10,... | collective-permute-start | bytes 786440 | tf_op jit(solution)/shard_map/ppermute | solution.py:587
  121.1 15.3 %collective-permute-start.29 = (bf16[512,256]{1,0:T(8,128)(2,1)S(1)}, bf16[512,256]{1,0:T(8,128)(2,1)S(1)}, u32[]{:S(2)}, u32[]{:S(2)}) collective-permute-start(bf16[512,256]{1,0:T(8,128)(2,1)S(1)} %collective-permute-done.28.refs_2_), channel_id=1, source_target_pairs={{0,6},{1,7},{2,0},{3,1},{4,2},{5,3},{6,4},{7,5},{8,14},{9,15},{10,... | collective-permute-start | bytes 786440 | tf_op jit(solution)/shard_map/ppermute | solution.py:587
  140.9 9.2 %collective-permute-start.36 = (bf16[512,256]{1,0:T(8,128)(2,1)S(1)}, bf16[512,256]{1,0:T(8,128)(2,1)S(1)}, u32[]{:S(2)}, u32[]{:S(2)}) collective-permute-start(bf16[512,256]{1,0:T(8,128)(2,1)S(1)} %get-tuple-element.150), channel_id=1, source_target_pairs={{0,2},{1,3},{2,4},{3,5},{4,6},{5,7},{6,0},{7,1},{8,10},{9,11},{10,... | collective-permute-start | bytes 786440 | tf_op jit(solution)/shard_map/ppermute | solution.py:587
  141.0 10.5 %collective-permute-start.37 = (bf16[512,256]{1,0:T(8,128)(2,1)S(1)}, bf16[512,256]{1,0:T(8,128)(2,1)S(1)}, u32[]{:S(2)}, u32[]{:S(2)}) collective-permute-start(bf16[512,256]{1,0:T(8,128)(2,1)S(1)} %get-tuple-element.152), channel_id=1, source_target_pairs={{0,6},{1,7},{2,0},{3,1},{4,2},{5,3},{6,4},{7,5},{8,14},{9,15},{10,... | collective-permute-start | bytes 786440 | tf_op jit(solution)/shard_map/ppermute | solution.py:587
  143.0 14.1 %collective-permute-start.33 = (bf16[512,256]{1,0:T(8,128)(2,1)S(1)}, bf16[512,256]{1,0:T(8,128)(2,1)S(1)}, u32[]{:S(2)}, u32[]{:S(2)}) collective-permute-start(bf16[512,256]{1,0:T(8,128)(2,1)S(1)} %get-tuple-element.146), channel_id=1, source_target_pairs={{0,6},{1,7},{2,0},{3,1},{4,2},{5,3},{6,4},{7,5},{8,14},{9,15},{10,... | collective-permute-start | bytes 786440 | tf_op jit(solution)/shard_map/ppermute | solution.py:587
  143.0 14.0 %collective-permute-start.34 = (bf16[512,256]{1,0:T(8,128)(2,1)S(1)}, bf16[512,256]{1,0:T(8,128)(2,1)S(1)}, u32[]{:S(2)}, u32[]{:S(2)}) collective-permute-start(bf16[512,256]{1,0:T(8,128)(2,1)S(1)} %get-tuple-element.147), channel_id=1, source_target_pairs={{0,3},{1,2},{2,5},{3,4},{4,7},{5,6},{6,1},{7,0},{8,11},{9,10},{10,... | collective-permute-start | bytes 786440 | tf_op jit(solution)/shard_map/ppermute | solution.py:587
  145.9 18.4 %collective-permute-start.35 = (bf16[512,256]{1,0:T(8,128)(2,1)S(1)}, bf16[512,256]{1,0:T(8,128)(2,1)S(1)}, u32[]{:S(2)}, u32[]{:S(2)}) collective-permute-start(bf16[512,256]{1,0:T(8,128)(2,1)S(1)} %get-tuple-element.148), channel_id=1, source_target_pairs={{0,1},{1,0},{2,3},{3,2},{4,5},{5,4},{6,7},{7,6},{8,9},{9,8},{10,11... | collective-permute-start | bytes 786440 | tf_op jit(solution)/shard_map/ppermute | solution.py:587
  151.6 12.7 %collective-permute-start.38 = (bf16[512,256]{1,0:T(8,128)(2,1)S(1)}, bf16[512,256]{1,0:T(8,128)(2,1)S(1)}, u32[]{:S(2)}, u32[]{:S(2)}) collective-permute-start(bf16[512,256]{1,0:T(8,128)(2,1)S(1)} %get-tuple-element.153), channel_id=1, source_target_pairs={{0,2},{1,3},{2,4},{3,5},{4,6},{5,7},{6,0},{7,1},{8,10},{9,11},{10,... | collective-permute-start | bytes 786440 | tf_op jit(solution)/shard_map/ppermute | solution.py:587
  151.6 12.7 %collective-permute-start.39 = (bf16[512,256]{1,0:T(8,128)(2,1)S(1)}, bf16[512,256]{1,0:T(8,128)(2,1)S(1)}, u32[]{:S(2)}, u32[]{:S(2)}) collective-permute-start(bf16[512,256]{1,0:T(8,128)(2,1)S(1)} %get-tuple-element.154), channel_id=1, source_target_pairs={{0,7},{1,6},{2,1},{3,0},{4,3},{5,2},{6,5},{7,4},{8,15},{9,14},{10,... | collective-permute-start | bytes 786440 | tf_op jit(solution)/shard_map/ppermute | solution.py:587
  (27 other events, 288.1 us)
where the time goes:
time: 182 us
  starting transfers between devices  58.8 us (32%)
  waiting for transfers between devices  56.5 us (31%)
  blocking collectives  40 us (22%)
  Pallas kernels  21.4 us (12%)
  local copies, waits for them, and re-layouts  4.32 us (2%)
    ppermute x28, starting transfers between devices, tp_shift(): return lax.ppermute(a, TP, pairs)  38 us
    ppermute x28, waiting for transfers between devices, tp_shift(): return lax.ppermute(a, TP, pairs)  34.9 us
    all_to_all x1, blocking collectives, shards(): lax.all_to_all(rows.reshape(EXPERTS, CAP, BLK), CHIPS, 0, 0, tiled=True)  23.4 us
    all_to_all x1, blocking collectives, shards(): lax.all_to_all(summed.reshape(EXPERTS, CAP, BLK), CHIPS, 0, 0, tiled=True)  16.5 us
    ppermute x6, starting transfers between devices, ring(): return lax.ppermute(a, 'z', [(i, (i + step) % 8) for i in range(8)])  12.3 us
    ppermute x4, waiting for transfers between devices, swap(): return lax.ppermute(a, ('yh', 'c'), pairs)  9.94 us
    pallas_call x1, Pallas kernels, expert_near(): pl.pallas_call(expert_near_kernel, out_shape=(jax.ShapeDtypeStruct((rows,...  7.55 us
    ppermute x4, starting transfers between devices, swap(): return lax.ppermute(a, ('yh', 'c'), pairs)  6.58 us
  transfers between devices with their start and end apart: 40, of which 22 were waited for; matrix products, arithmetic and copies ran while one was open for 0% of the time, Pallas kernels for 8%

commit v1 on v0

--- a/solution.py
+++ b/solution.py
@@ -453,18 +453,16 @@
     lax.fori_loop(0, blocks[0].shape[0] // SOME, some_rows, 0)
 
 
-def expert_near_kernel(*refs):
-    blocks = refs[:6]
-    gain, own, far = refs[6:9]
-    acc, square, rest, w2 = refs[9:13]
-    n_s, w1, sem = refs[13:]
+EARLY = 3
+
+
+def ready_kernel(b0, b1, b2, gain, own, far, w1, w2, n_s, square, sem):
     half = UNITS // 2
-    places = [(w1, 0), (w1, WIDE), (w2, 0)]
     copies = [
         pltpu.make_async_copy(
             src.at[pl.ds(i * half, half), :], dst.at[pl.ds(at + j * half, half), :], sem.at[3 * j + i]
         )
-        for i, (dst, at) in enumerate(places)
+        for i, (dst, at) in enumerate([(w1, 0), (w1, WIDE), (w2, 0)])
         for j, src in enumerate((own, far))
     ]
     for copy in copies:
@@ -473,93 +471,98 @@
     w1[UNITS:WIDE, :] = pad
     w1[WIDE + UNITS :, :] = pad
     w2[UNITS:, :] = pad
-    for shift in FAR:
-        n_s[:, source_rows(*shift)] = jnp.zeros((n_s.shape[0], BLK), BF16)
-    prepare(blocks, NEAR, [source_rows(*shift) for shift in NEAR], gain, n_s, square)
+    places = [slice(j * BLK, (j + 1) * BLK) for j in range(EARLY)]
+    prepare((b0, b1, b2), NEAR[:EARLY], places, gain, n_s, square)
     for copy in copies:
         copy.wait()
-    for j, shift in enumerate(FAR):
-        rest[:, j * BLK : (j + 1) * BLK] = w1[:, source_rows(*shift)]
-
-    def tile(j, carry):
-        cols = pl.ds(pl.multiple_of(j * BLK, BLK), BLK)
-        acc[:, cols] = nt_dot(n_s[...], w1[cols, :])
-        return carry
-
-    lax.fori_loop(0, 2 * WIDE // BLK, tile, 0)
-
-
-def expert_near(blocks, gain, own, far):
+
+
+def expert_ready(blocks, gain, own, far):
     rows = blocks[0].shape[0]
     return pl.pallas_call(
-        expert_near_kernel,
+        ready_kernel,
         out_shape=(
-            jax.ShapeDtypeStruct((rows, 2 * WIDE), F32),
+            jax.ShapeDtypeStruct((2 * WIDE, 2048), BF16),
+            jax.ShapeDtypeStruct((WIDE, 2048), BF16),
+            jax.ShapeDtypeStruct((rows, EARLY * BLK), BF16),
             jax.ShapeDtypeStruct((rows, 1), F32),
-            jax.ShapeDtypeStruct((2 * WIDE, 2 * BLK), BF16),
-            jax.ShapeDtypeStruct((WIDE, 2048), BF16),
-        ),
-        in_specs=[VMEM] * 7 + [HBM] * 2,
+        ),
+        in_specs=[VMEM] * 4 + [HBM] * 2,
         out_specs=(VMEM,) * 4,
-        scratch_shapes=[
-            pltpu.VMEM((rows, 2048), BF16),
-            pltpu.VMEM((2 * WIDE, 2048), BF16),
-            pltpu.SemaphoreType.DMA((6,)),
-        ],
-        cost_estimate=pl.CostEstimate(
-            flops=4 * rows * 2048 * WIDE, bytes_accessed=13 << 20, transcendentals=0
-        ),
-        compiler_params=vmem(24),
-        name="expert_near",
+        scratch_shapes=[pltpu.SemaphoreType.DMA((6,))],
+        cost_estimate=pl.CostEstimate(flops=1 << 20, bytes_accessed=18 << 20, transcendentals=0),
+        compiler_params=vmem(16),
+        name="expert_ready",
     )(*blocks, gain, own, far)
 
 
-def expert_far_kernel(b0, b1, gain, acc, square, rest, w2, *refs):
-    outs = refs[:8]
-    n_s, h_s, r_s = refs[8:]
-    rows = n_s.shape[0]
-    prepare((b0, b1), FAR, (slice(0, BLK), slice(BLK, 2 * BLK)), gain, n_s, r_s)
-    factor = lax.rsqrt((square[...] + r_s[...]) * (1.0 / 2048) + NORM_EPS)
-
-    def hidden(j, carry):
-        cols = pl.ds(pl.multiple_of(j * BLK, BLK), BLK)
-        later = pl.ds(pl.multiple_of(WIDE + j * BLK, BLK), BLK)
-        g = (acc[:, cols] + nt_dot(n_s[...], rest[cols, :])) * factor
-        u = (acc[:, later] + nt_dot(n_s[...], rest[later, :])) * factor
-        h_s[:, cols] = (g / (1.0 + jnp.exp(-g)) * u).astype(BF16)
-        return carry
-
-    lax.fori_loop(0, WIDE // BLK, hidden, 0)
-
-    def lower(i, carry):
+def lower(h_s, w2, outs, shifts):
+    def some_rows(i, carry):
         at = pl.ds(pl.multiple_of(i * BLK, BLK), BLK)
-        for out, shift in zip(outs, NEAR + FAR):
+        for out, shift in zip(outs, shifts):
             out[at, :] = jnp.dot(
                 h_s[at, :], w2[:, target_cols(*shift)], preferred_element_type=F32
             ).astype(BF16)
         return carry
 
-    lax.fori_loop(0, rows // BLK, lower, 0)
-
-
-def expert_far(b0, b1, gain, acc, square, rest, w2):
-    rows = b0.shape[0]
-    return pl.pallas_call(
-        expert_far_kernel,
-        out_shape=(jax.ShapeDtypeStruct(b0.shape, BF16),) * 8,
-        in_specs=[VMEM] * 7,
-        out_specs=(VMEM,) * 8,
-        scratch_shapes=[
-            pltpu.VMEM((rows, 2 * BLK), BF16),
-            pltpu.VMEM((rows, WIDE), BF16),
-            pltpu.VMEM((rows, 1), F32),
-        ],
-        cost_estimate=pl.CostEstimate(
-            flops=4 * rows * 1024 * WIDE, bytes_accessed=10 << 20, transcendentals=rows * WIDE
-        ),
-        compiler_params=vmem(24),
-        name="expert_far",
-    )(b0, b1, gain, acc, square, rest, w2)
+    lax.fori_loop(0, h_s.shape[0] // BLK, some_rows, 0)
+
+
+def hidden_kernel(*refs):
+    blocks = refs[:5]
+    gain, w1, w2, early, square, h_s, o0, o1, n_s, r_s = refs[5:]
+    for j, shift in enumerate(NEAR[:EARLY]):
+        n_s[:, source_rows(*shift)] = early[:, j * BLK : (j + 1) * BLK]
+    shifts = NEAR[EARLY:] + FAR
+    prepare(blocks, shifts, [source_rows(*shift) for shift in shifts], gain, n_s, r_s)
+    factor = lax.rsqrt((square[...] + r_s[...]) * (1.0 / 2048) + NORM_EPS)
+
+    def tile(j, carry):
+        cols = pl.ds(pl.multiple_of(j * BLK, BLK), BLK)
+        later = pl.ds(pl.multiple_of(WIDE + j * BLK, BLK), BLK)
+        g = nt_dot(n_s[...], w1[cols, :]) * factor
+        u = nt_dot(n_s[...], w1[later, :]) * factor
+        h_s[:, cols] = (g / (1.0 + jnp.exp(-g)) * u).astype(BF16)
+        return carry
+
+    lax.fori_loop(0, WIDE // BLK, tile, 0)
+    lower(h_s, w2, (o0, o1), FAR)
+
+
+def expert_hidden(blocks, gain, w1, w2, early, square):
+    rows = blocks[0].shape[0]
+    piece = jax.ShapeDtypeStruct((rows, BLK), BF16)
+    return pl.pallas_call(
+        hidden_kernel,
+        out_shape=(jax.ShapeDtypeStruct((rows, WIDE), BF16), piece, piece),
+        in_specs=[VMEM] * 10,
+        out_specs=(VMEM,) * 3,
+        scratch_shapes=[pltpu.VMEM((rows, 2048), BF16), pltpu.VMEM((rows, 1), F32)],
+        cost_estimate=pl.CostEstimate(
+            flops=5 * rows * 2048 * WIDE, bytes_accessed=13 << 20, transcendentals=rows * WIDE
+        ),
+        compiler_params=vmem(16),
+        name="expert_hidden",
+    )(*blocks, gain, w1, w2, early, square)
+
+
+def lower_kernel(h_s, w2, *outs):
+    lower(h_s, w2, outs, NEAR)
+
+
+def expert_lower(h, w2):
+    rows = h.shape[0]
+    return pl.pallas_call(
+        lower_kernel,
+        out_shape=(jax.ShapeDtypeStruct((rows, BLK), BF16),) * 6,
+        in_specs=[VMEM] * 2,
+        out_specs=(VMEM,) * 6,
+        cost_estimate=pl.CostEstimate(
+            flops=2 * rows * 1536 * WIDE, bytes_accessed=6 << 20, transcendentals=0
+        ),
+        compiler_params=vmem(16),
+        name="expert_lower",
+    )(h, w2)
 
 
 def finish_kernel(mixed, rows, slot, out):
@@ -652,8 +655,9 @@
     sent = lax.all_to_all(rows.reshape(EXPERTS, CAP, BLK), CHIPS, 0, 0, tiled=True)
     sent, far = lax.optimization_barrier((sent, far))
     blocks = tp_gather(sent.reshape(EXPERTS * CAP, BLK))
-    lowered = expert_far(*blocks[6:], gain, *expert_near(blocks[:6], gain, own, far))
-    summed = sum_all(tp_scatter(lowered))
+    w1, w2, *early = expert_ready(blocks[:EARLY], gain, own, far)
+    h, *far_pieces = expert_hidden(blocks[EARLY:], gain, w1, w2, *early)
+    summed = sum_all(tp_scatter([*expert_lower(h, w2), *far_pieces]))
     back = lax.all_to_all(summed.reshape(EXPERTS, CAP, BLK), CHIPS, 0, 0, tiled=True)
     return finish(mixed, back.reshape(EXPERTS * CAP, BLK), slot)
 

time: 182 us -> 178 us (0.978)
  waiting for transfers between devices: 56.5 us -> 53 us
  Pallas kernels: 21.4 us -> 19.5 us
    ppermute x28, waiting for transfers between devices: 34.9 us -> 31.3 us  [tp_shift(): return lax.ppermute(a, TP, pairs)]
    pallas_call x2 -> x3, Pallas kernels: 12 us -> 10.1 us  [the longest x1 6.03 us: expert_hidden(): pl.pallas_call(hidden_kernel, out_shape=(jax.ShapeDtypeStruct((rows, WIDE...]
  transfers between devices with their start and end apart: 40 -> 40, of which waited for: 22 -> 22; matrix products, arithmetic and copies ran while one was open for 0% -> 0% of each run, Pallas kernels for 8% -> 6%
where the time goes in v1:
time: 178 us
  starting transfers between devices  59.2 us (33%)
  waiting for transfers between devices  53 us (30%)
  blocking collectives  41 us (23%)
  Pallas kernels  19.5 us (11%)
  local copies, waits for them, and re-layouts  4.32 us (2%)
    ppermute x28, starting transfers between devices, tp_shift(): return lax.ppermute(a, TP, pairs)  38.5 us
    ppermute x28, waiting for transfers between devices, tp_shift(): return lax.ppermute(a, TP, pairs)  31.3 us
    all_to_all x1, blocking collectives, shards(): lax.all_to_all(rows.reshape(EXPERTS, CAP, BLK), CHIPS, 0, 0, tiled=True)  23.4 us
    all_to_all x1, blocking collectives, shards(): lax.all_to_all(summed.reshape(EXPERTS, CAP, BLK), CHIPS, 0, 0, tiled=True)  17.6 us
    ppermute x6, starting transfers between devices, ring(): return lax.ppermute(a, 'z', [(i, (i + step) % 8) for i in range(8)])  12.3 us
    ppermute x4, waiting for transfers between devices, swap(): return lax.ppermute(a, ('yh', 'c'), pairs)  9.94 us
    ppermute x4, starting transfers between devices, swap(): return lax.ppermute(a, ('yh', 'c'), pairs)  6.58 us
    pallas_call x1, Pallas kernels, expert_hidden(): pl.pallas_call(hidden_kernel, out_shape=(jax.ShapeDtypeStruct((rows, WIDE...  6.03 us
  transfers between devices with their start and end apart: 40, of which 22 were waited for; matrix products, arithmetic and copies ran while one was open for 0% of the time, Pallas kernels for 6%

profile of v1, /device:TPU:6, one launch (start us, length us, event | category | flops | bytes accessed | tf_op | source)
XLA Modules:
  0.0 178.0 jit_solution(4449638885684924124)
XLA Ops:
  3.9 2.5 %collective-permute-start.3 = (bf16[256,256]{1,0:T(8,128)(2,1)}, bf16[256,256]{1,0:T(8,128)(2,1)S(1)}, u32[]{:S(2)}, u32[]{:S(2)}) collective-permute-start(bf16[256,256]{1,0:T(8,128)(2,1)} %refs_6_.1), channel_id=1, source_target_pairs={{0,3},{1,2},{2,5},{3,4},{4,7},{5,6},{6,1},{7,0},{8,11},{9,10},{10,... | collective-permute-start | bytes 393224 | tf_op jit(solution)/shard_map/ppermute | solution.py:590
  20.2 4.0 %collective-permute-start.9 = (bf16[528,256]{1,0:T(8,128)(2,1)S(1)}, bf16[528,256]{1,0:T(8,128)(2,1)S(1)}, u32[]{:S(2)}, u32[]{:S(2)}) collective-permute-start(bf16[528,256]{1,0:T(8,128)(2,1)S(1)} %get-tuple-element.85.kv), channel_id=1, source_target_pairs={{0,224},{32,0},{64,32},{96,64},{128,96},{160,128},{192,160},{224,1... | collective-permute-start | bytes 811016 | tf_op jit(solution)/shard_map/ppermute | solution.py:611
  24.3 3.3 %collective-permute-start.10 = (bf16[528,128]{1,0:T(8,128)(2,1)S(1)}, bf16[528,128]{1,0:T(8,128)(2,1)S(1)}, u32[]{:S(2)}, u32[]{:S(2)}) collective-permute-start(bf16[528,128]{1,0:T(8,128)(2,1)S(1)} %get-tuple-element.86.mine), channel_id=1, source_target_pairs={{0,16},{8,24},{16,0},{24,8},{1,17},{9,25},{17,1},{25,9},{2,18},{10... | collective-permute-start | bytes 405512 | tf_op jit(solution)/shard_map/ppermute | solution.py:607
  27.6 3.6 %collective-permute-done.10.theirs = bf16[528,128]{1,0:T(8,128)(2,1)S(1)} collective-permute-done((bf16[528,128]{1,0:T(8,128)(2,1)S(1)}, bf16[528,128]{1,0:T(8,128)(2,1)S(1)}, u32[]{:S(2)}, u32[]{:S(2)}) %collective-permute-start.10) | collective-permute-done | bytes 135200 | tf_op jit(solution)/shard_map/ppermute | solution.py:607
  31.2 3.2 %collective-permute-start.12 = (bf16[528,256]{1,0:T(8,128)(2,1)S(1)}, bf16[528,256]{1,0:T(8,128)(2,1)S(1)}, u32[]{:S(2)}, u32[]{:S(2)}) collective-permute-start(bf16[528,256]{1,0:T(8,128)(2,1)S(1)} %collective-permute-done.9.b), channel_id=1, source_target_pairs={{0,224},{32,0},{64,32},{96,64},{128,96},{160,128},{192,160},{224,1... | collective-permute-start | bytes 811016 | tf_op jit(solution)/shard_map/ppermute | solution.py:611
  36.8 2.4 %step.3 = (f32[1,1024]{1,0:T(1,128)S(1)}, f32[1,1024]{1,0:T(1,128)S(1)}, f32[128,1024]{1,0:T(8,128)S(1)}) custom-call(bf16[1024,128]{1,0:T(8,128)(2,1)S(1)} %get-tuple-element.111.q_s, f32[1,1024]{1,0:T(1,128)S(1)} %get-tuple-element.112.f_s, f32[1,1024]{1,0:T(1,128)S(1)} %get-tuple-element.92.m_i, f32[1,1024]{1,0:T(1,128)S(1)} %get-tuple-element.93.l_i, ...), custom_call_target="tpu_custom_call" | custom-call | flops 536870912 | bytes 2097152 | tf_op jit(solution)/shard_map/step/pallas_call | solution.py:267
  44.1 4.6 %collective-permute-done.13.f = bf16[528,256]{1,0:T(8,128)(2,1)S(1)} collective-permute-done((bf16[528,256]{1,0:T(8,128)(2,1)S(1)}, bf16[528,256]{1,0:T(8,128)(2,1)S(1)}, u32[]{:S(2)}, u32[]{:S(2)}) %collective-permute-start.13) | collective-permute-done | bytes 270368 | tf_op jit(solution)/shard_map/ppermute | solution.py:611
  50.9 5.8 %collective-permute-done.15.kv = bf16[528,256]{1,0:T(8,128)(2,1)S(1)} collective-permute-done((bf16[528,256]{1,0:T(8,128)(2,1)S(1)}, bf16[528,256]{1,0:T(8,128)(2,1)S(1)}, u32[]{:S(2)}, u32[]{:S(2)}) %collective-permute-start.15) | collective-permute-done | bytes 270368 | tf_op jit(solution)/shard_map/ppermute | solution.py:635
  56.9 3.1 %collective-permute-start.16 = (bf16[144,512]{1,0:T(8,128)(2,1)S(1)}, bf16[144,512]{1,0:T(8,128)(2,1)S(1)}, u32[]{:S(2)}, u32[]{:S(2)}) collective-permute-start(bf16[144,512]{1,0:T(8,128)(2,1)S(1)} %get-tuple-element.122), channel_id=1, source_target_pairs={{0,16},{8,24},{16,0},{24,8},{1,17},{9,25},{17,1},{25,9},{2,18},{10... | collective-permute-start | bytes 442376 | tf_op jit(solution)/shard_map/ppermute | solution.py:607
  59.9 3.6 %collective-permute-done.16.b = bf16[144,512]{1,0:T(8,128)(2,1)S(1)} collective-permute-done((bf16[144,512]{1,0:T(8,128)(2,1)S(1)}, bf16[144,512]{1,0:T(8,128)(2,1)S(1)}, u32[]{:S(2)}, u32[]{:S(2)}) %collective-permute-start.16) | collective-permute-done | bytes 147488 | tf_op jit(solution)/shard_map/ppermute | solution.py:607
  65.5 2.9 %collective-permute-start.21 = (bf16[256,256]{1,0:T(8,128)(2,1)S(1)}, bf16[256,256]{1,0:T(8,128)(2,1)S(1)}, u32[]{:S(2)}, u32[]{:S(2)}) collective-permute-start(bf16[256,256]{1,0:T(8,128)(2,1)S(1)} %get-tuple-element.130), channel_id=1, source_target_pairs={{0,2},{1,3},{2,4},{3,5},{4,6},{5,7},{6,0},{7,1},{8,10},{9,11},{10,... | collective-permute-start | bytes 393224 | tf_op jit(solution)/shard_map/ppermute | solution.py:590
  68.7 4.8 %collective-permute-start.19 = (bf16[256,256]{1,0:T(8,128)(2,1)S(1)}, bf16[256,256]{1,0:T(8,128)(2,1)S(1)}, u32[]{:S(2)}, u32[]{:S(2)}) collective-permute-start(bf16[256,256]{1,0:T(8,128)(2,1)S(1)} %get-tuple-element.127), channel_id=1, source_target_pairs={{0,3},{1,2},{2,5},{3,4},{4,7},{5,6},{6,1},{7,0},{8,11},{9,10},{10,... | collective-permute-start | bytes 393224 | tf_op jit(solution)/shard_map/ppermute | solution.py:590
  73.5 2.5 %collective-permute-done.22.b1 = bf16[256,256]{1,0:T(8,128)(2,1)S(1)} collective-permute-done((bf16[256,256]{1,0:T(8,128)(2,1)S(1)}, bf16[256,256]{1,0:T(8,128)(2,1)S(1)}, u32[]{:S(2)}, u32[]{:S(2)}) %collective-permute-start.22) | collective-permute-done | bytes 131104 | tf_op jit(solution)/shard_map/ppermute | solution.py:590
  76.2 3.5 %collective-permute-start.24 = (bf16[256,256]{1,0:T(8,128)(2,1)S(1)}, bf16[256,256]{1,0:T(8,128)(2,1)S(1)}, u32[]{:S(2)}, u32[]{:S(2)}) collective-permute-start(bf16[256,256]{1,0:T(8,128)(2,1)S(1)} %get-tuple-element.134), channel_id=1, source_target_pairs={{0,7},{1,6},{2,1},{3,0},{4,3},{5,2},{6,5},{7,4},{8,15},{9,14},{10,... | collective-permute-start | bytes 393224 | tf_op jit(solution)/shard_map/ppermute | solution.py:590
  83.8 23.4 %all_to_all.10 = bf16[16,32,256]{2,1,0:T(8,128)(2,1)S(1)} all-to-all(bf16[16,32,256]{2,1,0:T(8,128)(2,1)S(1)} %bitcast.25), channel_id=1, replica_groups=mesh['z'=8,'yh'=2,'c'=2,'x'=4,'yl'=2] {'z','yh'}, dimensions={0} | all-to-all | bytes 524288 | tf_op jit(solution)/shard_map/all_to_all | solution.py:655
  110.7 2.7 %collective-permute-start.27 = (bf16[512,256]{1,0:T(8,128)(2,1)S(1)}, bf16[512,256]{1,0:T(8,128)(2,1)S(1)}, u32[]{:S(2)}, u32[]{:S(2)}) collective-permute-start(bf16[512,256]{1,0:T(8,128)(2,1)S(1)} %bitcast.20), channel_id=1, source_target_pairs={{0,3},{1,2},{2,5},{3,4},{4,7},{5,6},{6,1},{7,0},{8,11},{9,10},{10,... | collective-permute-start | bytes 786440 | tf_op jit(solution)/shard_map/ppermute | solution.py:590
  118.6 2.5 %collective-permute-done.31.b2 = bf16[512,256]{1,0:T(8,128)(2,1)S(1)} collective-permute-done((bf16[512,256]{1,0:T(8,128)(2,1)S(1)}, bf16[512,256]{1,0:T(8,128)(2,1)S(1)}, u32[]{:S(2)}, u32[]{:S(2)}) %collective-permute-start.31) | collective-permute-done | bytes 262176 | tf_op jit(solution)/shard_map/ppermute | solution.py:590
  121.1 2.5 %expert_ready.1 = (bf16[1536,2048]{1,0:T(8,128)(2,1)S(1)}, bf16[768,2048]{1,0:T(8,128)(2,1)S(1)}, bf16[512,768]{1,0:T(8,128)(2,1)S(1)}, f32[512,1]{1,0:T(8,128)S(1)}) custom-call(bf16[512,256]{1,0:T(8,128)(2,1)S(1)} %bitcast.22, bf16[512,256]{1,0:T(8,128)(2,1)S(1)} %collective-permute-done.29.b1, bf16[512,256]{1,0:T(8,128)(2,1)S(1)} %collective-permute-done.31.b2, ...), custom_call_target="tpu_custom_call" | custom-call | flops 1048576 | bytes 18874368 | tf_op jit(solution)/shard_map/expert_ready/pallas_call | solution.py:482
  124.5 4.3 %collective-permute-done.28.refs_2_ = bf16[512,256]{1,0:T(8,128)(2,1)S(1)} collective-permute-done((bf16[512,256]{1,0:T(8,128)(2,1)S(1)}, bf16[512,256]{1,0:T(8,128)(2,1)S(1)}, u32[]{:S(2)}, u32[]{:S(2)}) %collective-permute-start.28) | collective-permute-done | bytes 262176 | tf_op jit(solution)/shard_map/ppermute | solution.py:590
  128.8 6.0 %expert_hidden.1 = (bf16[512,768]{1,0:T(8,128)(2,1)S(1)}, bf16[512,256]{1,0:T(8,128)(2,1)S(1)}, bf16[512,256]{1,0:T(8,128)(2,1)S(1)}) custom-call(bf16[512,256]{1,0:T(8,128)(2,1)S(1)} %collective-permute-done.26.refs_0_, bf16[512,256]{1,0:T(8,128)(2,1)S(1)} %collective-permute-done.27.refs_1_, bf16[512,256]{1,0:T(8,128)(2,1)S(1)} %collective-permute-done.28.refs_2_, ...), custom_call_target="tpu_custom_call" | custom-call | flops 4026531840 | bytes 13631488 | tf_op jit(solution)/shard_map/expert_hidden/pallas_call | solution.py:535
  138.7 3.2 %collective-permute-start.34 = (bf16[512,256]{1,0:T(8,128)(2,1)S(1)}, bf16[512,256]{1,0:T(8,128)(2,1)S(1)}, u32[]{:S(2)}, u32[]{:S(2)}) collective-permute-start(bf16[512,256]{1,0:T(8,128)(2,1)S(1)} %get-tuple-element.149), channel_id=1, source_target_pairs={{0,3},{1,2},{2,5},{3,4},{4,7},{5,6},{6,1},{7,0},{8,11},{9,10},{10,... | collective-permute-start | bytes 786440 | tf_op jit(solution)/shard_map/ppermute | solution.py:590
  147.7 3.4 %collective-permute-done.33.refs_1_ = bf16[512,256]{1,0:T(8,128)(2,1)S(1)} collective-permute-done((bf16[512,256]{1,0:T(8,128)(2,1)S(1)}, bf16[512,256]{1,0:T(8,128)(2,1)S(1)}, u32[]{:S(2)}, u32[]{:S(2)}) %collective-permute-start.33) | collective-permute-done | bytes 262176 | tf_op jit(solution)/shard_map/ppermute | solution.py:590
  151.0 8.2 %collective-permute-done.35.refs_3_ = bf16[512,256]{1,0:T(8,128)(2,1)S(1)} collective-permute-done((bf16[512,256]{1,0:T(8,128)(2,1)S(1)}, bf16[512,256]{1,0:T(8,128)(2,1)S(1)}, u32[]{:S(2)}, u32[]{:S(2)}) %collective-permute-start.35) | collective-permute-done | bytes 262176 | tf_op jit(solution)/shard_map/ppermute | solution.py:590
  159.5 17.6 %all_to_all.11 = bf16[16,32,256]{2,1,0:T(8,128)(2,1)S(1)} all-to-all(bf16[16,32,256]{2,1,0:T(8,128)(2,1)S(1)} %bitcast.23), channel_id=1, replica_groups=mesh['z'=8,'yh'=2,'c'=2,'x'=4,'yl'=2] {'z','yh'}, dimensions={0} | all-to-all | bytes 524288 | tf_op jit(solution)/shard_map/all_to_all | solution.py:661
  (103 shorter events, 53.9 us)
Async XLA Ops:
  3.0 11.0 %collective-permute-start.2 = (bf16[256,256]{1,0:T(8,128)(2,1)}, bf16[256,256]{1,0:T(8,128)(2,1)S(1)}, u32[]{:S(2)}, u32[]{:S(2)}) collective-permute-start(bf16[256,256]{1,0:T(8,128)(2,1)} %refs_6_.1), channel_id=1, source_target_pairs={{0,6},{1,7},{2,0},{3,1},{4,2},{5,3},{6,4},{7,5},{8,14},{9,15},{10,... | collective-permute-start | bytes 393224 | tf_op jit(solution)/shard_map/ppermute | solution.py:590
  3.9 10.2 %collective-permute-start.3 = (bf16[256,256]{1,0:T(8,128)(2,1)}, bf16[256,256]{1,0:T(8,128)(2,1)S(1)}, u32[]{:S(2)}, u32[]{:S(2)}) collective-permute-start(bf16[256,256]{1,0:T(8,128)(2,1)} %refs_6_.1), channel_id=1, source_target_pairs={{0,3},{1,2},{2,5},{3,4},{4,7},{5,6},{6,1},{7,0},{8,11},{9,10},{10,... | collective-permute-start | bytes 393224 | tf_op jit(solution)/shard_map/ppermute | solution.py:590
  7.7 8.1 %collective-permute-start.5 = (bf16[256,256]{1,0:T(8,128)(2,1)S(1)}, bf16[256,256]{1,0:T(8,128)(2,1)S(1)}, u32[]{:S(2)}, u32[]{:S(2)}) collective-permute-start(bf16[256,256]{1,0:T(8,128)(2,1)S(1)} %collective-permute-done.refs_1_), channel_id=1, source_target_pairs={{0,2},{1,3},{2,4},{3,5},{4,6},{5,7},{6,0},{7,1},{8,10},{9,11},{10,... | collective-permute-start | bytes 393224 | tf_op jit(solution)/shard_map/ppermute | solution.py:590
  18.6 12.6 %collective-permute-start.8 = (bf16[528,256]{1,0:T(8,128)(2,1)S(1)}, bf16[528,256]{1,0:T(8,128)(2,1)S(1)}, u32[]{:S(2)}, u32[]{:S(2)}) collective-permute-start(bf16[528,256]{1,0:T(8,128)(2,1)S(1)} %get-tuple-element.85.kv), channel_id=1, source_target_pairs={{0,32},{32,64},{64,96},{96,128},{128,160},{160,192},{192,224},{224... | collective-permute-start | bytes 811016 | tf_op jit(solution)/shard_map/ppermute | solution.py:611
  20.2 11.0 %collective-permute-start.9 = (bf16[528,256]{1,0:T(8,128)(2,1)S(1)}, bf16[528,256]{1,0:T(8,128)(2,1)S(1)}, u32[]{:S(2)}, u32[]{:S(2)}) collective-permute-start(bf16[528,256]{1,0:T(8,128)(2,1)S(1)} %get-tuple-element.85.kv), channel_id=1, source_target_pairs={{0,224},{32,0},{64,32},{96,64},{128,96},{160,128},{192,160},{224,1... | collective-permute-start | bytes 811016 | tf_op jit(solution)/shard_map/ppermute | solution.py:611
  31.2 9.0 %collective-permute-start.11 = (bf16[528,256]{1,0:T(8,128)(2,1)S(1)}, bf16[528,256]{1,0:T(8,128)(2,1)S(1)}, u32[]{:S(2)}, u32[]{:S(2)}) collective-permute-start(bf16[528,256]{1,0:T(8,128)(2,1)S(1)} %collective-permute-done.8.f), channel_id=1, source_target_pairs={{0,32},{32,64},{64,96},{96,128},{128,160},{160,192},{192,224},{224... | collective-permute-start | bytes 811016 | tf_op jit(solution)/shard_map/ppermute | solution.py:611
  31.2 9.0 %collective-permute-start.12 = (bf16[528,256]{1,0:T(8,128)(2,1)S(1)}, bf16[528,256]{1,0:T(8,128)(2,1)S(1)}, u32[]{:S(2)}, u32[]{:S(2)}) collective-permute-start(bf16[528,256]{1,0:T(8,128)(2,1)S(1)} %collective-permute-done.9.b), channel_id=1, source_target_pairs={{0,224},{32,0},{64,32},{96,64},{128,96},{160,128},{192,160},{224,1... | collective-permute-start | bytes 811016 | tf_op jit(solution)/shard_map/ppermute | solution.py:611
  40.2 8.5 %collective-permute-start.13 = (bf16[528,256]{1,0:T(8,128)(2,1)S(1)}, bf16[528,256]{1,0:T(8,128)(2,1)S(1)}, u32[]{:S(2)}, u32[]{:S(2)}) collective-permute-start(bf16[528,256]{1,0:T(8,128)(2,1)S(1)} %collective-permute-done.11.f), channel_id=1, source_target_pairs={{0,32},{32,64},{64,96},{96,128},{128,160},{160,192},{192,224},{224... | collective-permute-start | bytes 811016 | tf_op jit(solution)/shard_map/ppermute | solution.py:611
  68.6 11.1 %collective-permute-start.18 = (bf16[256,256]{1,0:T(8,128)(2,1)S(1)}, bf16[256,256]{1,0:T(8,128)(2,1)S(1)}, u32[]{:S(2)}, u32[]{:S(2)}) collective-permute-start(bf16[256,256]{1,0:T(8,128)(2,1)S(1)} %get-tuple-element.126), channel_id=1, source_target_pairs={{0,6},{1,7},{2,0},{3,1},{4,2},{5,3},{6,4},{7,5},{8,14},{9,15},{10,... | collective-permute-start | bytes 393224 | tf_op jit(solution)/shard_map/ppermute | solution.py:590
  68.7 11.0 %collective-permute-start.19 = (bf16[256,256]{1,0:T(8,128)(2,1)S(1)}, bf16[256,256]{1,0:T(8,128)(2,1)S(1)}, u32[]{:S(2)}, u32[]{:S(2)}) collective-permute-start(bf16[256,256]{1,0:T(8,128)(2,1)S(1)} %get-tuple-element.127), channel_id=1, source_target_pairs={{0,3},{1,2},{2,5},{3,4},{4,7},{5,6},{6,1},{7,0},{8,11},{9,10},{10,... | collective-permute-start | bytes 393224 | tf_op jit(solution)/shard_map/ppermute | solution.py:590
  83.7 23.5 %collective-permute-start.25 = (bf16[1056,2048]{1,0:T(8,128)(2,1)S(1)}, bf16[1056,2048]{1,0:T(8,128)(2,1)S(1)}, u32[]{:S(2)}, u32[]{:S(2)}) collective-permute-start(bf16[1056,2048]{1,0:T(8,128)(2,1)S(1)} %pad_maximum_fusion.own), channel_id=1, source_target_pairs={{0,8},{8,0},{1,9},{9,1},{2,10},{10,2},{3,11},{11,3},{4,12},{12,4},... | collective-permute-start | bytes 12976136 | tf_op jit(solution)/shard_map/ppermute | solution.py:654
  107.3 9.2 %collective-permute-start.29 = (bf16[512,256]{1,0:T(8,128)(2,1)S(1)}, bf16[512,256]{1,0:T(8,128)(2,1)S(1)}, u32[]{:S(2)}, u32[]{:S(2)}) collective-permute-start(bf16[512,256]{1,0:T(8,128)(2,1)S(1)} %bitcast.17), channel_id=1, source_target_pairs={{0,2},{1,3},{2,4},{3,5},{4,6},{5,7},{6,0},{7,1},{8,10},{9,11},{10,... | collective-permute-start | bytes 786440 | tf_op jit(solution)/shard_map/ppermute | solution.py:590
  108.7 12.4 %collective-permute-start.31 = (bf16[512,256]{1,0:T(8,128)(2,1)S(1)}, bf16[512,256]{1,0:T(8,128)(2,1)S(1)}, u32[]{:S(2)}, u32[]{:S(2)}) collective-permute-start(bf16[512,256]{1,0:T(8,128)(2,1)S(1)} %bitcast.18), channel_id=1, source_target_pairs={{0,7},{1,6},{2,1},{3,0},{4,3},{5,2},{6,5},{7,4},{8,15},{9,14},{10,... | collective-permute-start | bytes 786440 | tf_op jit(solution)/shard_map/ppermute | solution.py:590
  110.0 14.0 %collective-permute-start.26 = (bf16[512,256]{1,0:T(8,128)(2,1)S(1)}, bf16[512,256]{1,0:T(8,128)(2,1)S(1)}, u32[]{:S(2)}, u32[]{:S(2)}) collective-permute-start(bf16[512,256]{1,0:T(8,128)(2,1)S(1)} %bitcast.19), channel_id=1, source_target_pairs={{0,6},{1,7},{2,0},{3,1},{4,2},{5,3},{6,4},{7,5},{8,14},{9,15},{10,... | collective-permute-start | bytes 786440 | tf_op jit(solution)/shard_map/ppermute | solution.py:590
  110.7 13.7 %collective-permute-start.27 = (bf16[512,256]{1,0:T(8,128)(2,1)S(1)}, bf16[512,256]{1,0:T(8,128)(2,1)S(1)}, u32[]{:S(2)}, u32[]{:S(2)}) collective-permute-start(bf16[512,256]{1,0:T(8,128)(2,1)S(1)} %bitcast.20), channel_id=1, source_target_pairs={{0,3},{1,2},{2,5},{3,4},{4,7},{5,6},{6,1},{7,0},{8,11},{9,10},{10,... | collective-permute-start | bytes 786440 | tf_op jit(solution)/shard_map/ppermute | solution.py:590
  113.4 15.4 %collective-permute-start.28 = (bf16[512,256]{1,0:T(8,128)(2,1)S(1)}, bf16[512,256]{1,0:T(8,128)(2,1)S(1)}, u32[]{:S(2)}, u32[]{:S(2)}) collective-permute-start(bf16[512,256]{1,0:T(8,128)(2,1)S(1)} %bitcast.21), channel_id=1, source_target_pairs={{0,1},{1,0},{2,3},{3,2},{4,5},{5,4},{6,7},{7,6},{8,9},{9,8},{10,11... | collective-permute-start | bytes 786440 | tf_op jit(solution)/shard_map/ppermute | solution.py:590
  116.5 12.3 %collective-permute-start.30 = (bf16[512,256]{1,0:T(8,128)(2,1)S(1)}, bf16[512,256]{1,0:T(8,128)(2,1)S(1)}, u32[]{:S(2)}, u32[]{:S(2)}) collective-permute-start(bf16[512,256]{1,0:T(8,128)(2,1)S(1)} %collective-permute-done.29.b1), channel_id=1, source_target_pairs={{0,2},{1,3},{2,4},{3,5},{4,6},{5,7},{6,0},{7,1},{8,10},{9,11},{10,... | collective-permute-start | bytes 786440 | tf_op jit(solution)/shard_map/ppermute | solution.py:590
  134.9 9.3 %collective-permute-start.36 = (bf16[512,256]{1,0:T(8,128)(2,1)S(1)}, bf16[512,256]{1,0:T(8,128)(2,1)S(1)}, u32[]{:S(2)}, u32[]{:S(2)}) collective-permute-start(bf16[512,256]{1,0:T(8,128)(2,1)S(1)} %get-tuple-element.152), channel_id=1, source_target_pairs={{0,2},{1,3},{2,4},{3,5},{4,6},{5,7},{6,0},{7,1},{8,10},{9,11},{10,... | collective-permute-start | bytes 786440 | tf_op jit(solution)/shard_map/ppermute | solution.py:590
  135.0 10.5 %collective-permute-start.37 = (bf16[512,256]{1,0:T(8,128)(2,1)S(1)}, bf16[512,256]{1,0:T(8,128)(2,1)S(1)}, u32[]{:S(2)}, u32[]{:S(2)}) collective-permute-start(bf16[512,256]{1,0:T(8,128)(2,1)S(1)} %get-tuple-element.154), channel_id=1, source_target_pairs={{0,6},{1,7},{2,0},{3,1},{4,2},{5,3},{6,4},{7,5},{8,14},{9,15},{10,... | collective-permute-start | bytes 786440 | tf_op jit(solution)/shard_map/ppermute | solution.py:590
  138.6 12.5 %collective-permute-start.33 = (bf16[512,256]{1,0:T(8,128)(2,1)S(1)}, bf16[512,256]{1,0:T(8,128)(2,1)S(1)}, u32[]{:S(2)}, u32[]{:S(2)}) collective-permute-start(bf16[512,256]{1,0:T(8,128)(2,1)S(1)} %get-tuple-element.148), channel_id=1, source_target_pairs={{0,6},{1,7},{2,0},{3,1},{4,2},{5,3},{6,4},{7,5},{8,14},{9,15},{10,... | collective-permute-start | bytes 786440 | tf_op jit(solution)/shard_map/ppermute | solution.py:590
  138.7 12.4 %collective-permute-start.34 = (bf16[512,256]{1,0:T(8,128)(2,1)S(1)}, bf16[512,256]{1,0:T(8,128)(2,1)S(1)}, u32[]{:S(2)}, u32[]{:S(2)}) collective-permute-start(bf16[512,256]{1,0:T(8,128)(2,1)S(1)} %get-tuple-element.149), channel_id=1, source_target_pairs={{0,3},{1,2},{2,5},{3,4},{4,7},{5,6},{6,1},{7,0},{8,11},{9,10},{10,... | collective-permute-start | bytes 786440 | tf_op jit(solution)/shard_map/ppermute | solution.py:590
  141.9 17.4 %collective-permute-start.35 = (bf16[512,256]{1,0:T(8,128)(2,1)S(1)}, bf16[512,256]{1,0:T(8,128)(2,1)S(1)}, u32[]{:S(2)}, u32[]{:S(2)}) collective-permute-start(bf16[512,256]{1,0:T(8,128)(2,1)S(1)} %get-tuple-element.150), channel_id=1, source_target_pairs={{0,1},{1,0},{2,3},{3,2},{4,5},{5,4},{6,7},{7,6},{8,9},{9,8},{10,11... | collective-permute-start | bytes 786440 | tf_op jit(solution)/shard_map/ppermute | solution.py:590
  145.5 13.7 %collective-permute-start.38 = (bf16[512,256]{1,0:T(8,128)(2,1)S(1)}, bf16[512,256]{1,0:T(8,128)(2,1)S(1)}, u32[]{:S(2)}, u32[]{:S(2)}) collective-permute-start(bf16[512,256]{1,0:T(8,128)(2,1)S(1)} %get-tuple-element.155), channel_id=1, source_target_pairs={{0,2},{1,3},{2,4},{3,5},{4,6},{5,7},{6,0},{7,1},{8,10},{9,11},{10,... | collective-permute-start | bytes 786440 | tf_op jit(solution)/shard_map/ppermute | solution.py:590
  145.6 13.7 %collective-permute-start.39 = (bf16[512,256]{1,0:T(8,128)(2,1)S(1)}, bf16[512,256]{1,0:T(8,128)(2,1)S(1)}, u32[]{:S(2)}, u32[]{:S(2)}) collective-permute-start(bf16[512,256]{1,0:T(8,128)(2,1)S(1)} %get-tuple-element.156), channel_id=1, source_target_pairs={{0,7},{1,6},{2,1},{3,0},{4,3},{5,2},{6,5},{7,4},{8,15},{9,14},{10,... | collective-permute-start | bytes 786440 | tf_op jit(solution)/shard_map/ppermute | solution.py:590
  (27 other events, 280.0 us)

commit v2 on v1

--- a/solution.py
+++ b/solution.py
@@ -18,7 +18,7 @@
 SEQ = ("z", "yh", "c")
 CHIPS = ("z", "yh")
 TP = ("x", "yl")
-NEAR = ((0, 0), (1, 0), (3, 1), (3, 0), (1, 1), (0, 1))
+NEAR = ((0, 0), (1, 0), (3, 1), (0, 1), (1, 1), (3, 0))
 FAR = ((2, 0), (2, 1))
 F32 = jnp.float32
 BF16 = jnp.bfloat16
@@ -43,30 +43,6 @@
     x, yl = lax.axis_index("x"), lax.axis_index("yl")
     source = ((x + 4 - dx) % 4) * 2 + (yl + dy) % 2
     return pl.ds(pl.multiple_of(source * BLK, BLK), BLK)
-
-
-def fetch_kernel(wk, wv, wq, out, sem):
-    copies = [
-        pltpu.make_async_copy(src, out.at[:, pl.ds(i * BLK, BLK)], sem.at[i])
-        for i, src in enumerate((wk, wv, wq))
-    ]
-    for copy in copies:
-        copy.start()
-    for copy in copies:
-        copy.wait()
-
-
-def fetch(*weights):
-    return pl.pallas_call(
-        fetch_kernel,
-        out_shape=jax.ShapeDtypeStruct((2048, 3 * BLK), BF16),
-        in_specs=[HBM] * 3,
-        out_specs=VMEM,
-        scratch_shapes=[pltpu.SemaphoreType.DMA((3,))],
-        cost_estimate=pl.CostEstimate(flops=0, bytes_accessed=6 << 20, transcendentals=0),
-        compiler_params=vmem(8),
-        name="fetch",
-    )(*weights)
 
 
 def near_kernel(*refs):
@@ -453,6 +429,8 @@
     lax.fori_loop(0, blocks[0].shape[0] // SOME, some_rows, 0)
 
 
+FIRST_OUT = FAR + ((0, 1),)
+NEXT_OUT = ((0, 0), (1, 0), (3, 1), (1, 1), (3, 0))
 EARLY = 3
 
 
@@ -510,7 +488,7 @@
 
 def hidden_kernel(*refs):
     blocks = refs[:5]
-    gain, w1, w2, early, square, h_s, o0, o1, n_s, r_s = refs[5:]
+    gain, w1, w2, early, square, h_s, o0, o1, o2, n_s, r_s = refs[5:]
     for j, shift in enumerate(NEAR[:EARLY]):
         n_s[:, source_rows(*shift)] = early[:, j * BLK : (j + 1) * BLK]
     shifts = NEAR[EARLY:] + FAR
@@ -526,7 +504,7 @@
         return carry
 
     lax.fori_loop(0, WIDE // BLK, tile, 0)
-    lower(h_s, w2, (o0, o1), FAR)
+    lower(h_s, w2, (o0, o1, o2), FIRST_OUT)
 
 
 def expert_hidden(blocks, gain, w1, w2, early, square):
@@ -534,9 +512,9 @@
     piece = jax.ShapeDtypeStruct((rows, BLK), BF16)
     return pl.pallas_call(
         hidden_kernel,
-        out_shape=(jax.ShapeDtypeStruct((rows, WIDE), BF16), piece, piece),
+        out_shape=(jax.ShapeDtypeStruct((rows, WIDE), BF16), piece, piece, piece),
         in_specs=[VMEM] * 10,
-        out_specs=(VMEM,) * 3,
+        out_specs=(VMEM,) * 4,
         scratch_shapes=[pltpu.VMEM((rows, 2048), BF16), pltpu.VMEM((rows, 1), F32)],
         cost_estimate=pl.CostEstimate(
             flops=5 * rows * 2048 * WIDE, bytes_accessed=13 << 20, transcendentals=rows * WIDE
@@ -547,16 +525,16 @@
 
 
 def lower_kernel(h_s, w2, *outs):
-    lower(h_s, w2, outs, NEAR)
+    lower(h_s, w2, outs, NEXT_OUT)
 
 
 def expert_lower(h, w2):
     rows = h.shape[0]
     return pl.pallas_call(
         lower_kernel,
-        out_shape=(jax.ShapeDtypeStruct((rows, BLK), BF16),) * 6,
+        out_shape=(jax.ShapeDtypeStruct((rows, BLK), BF16),) * 5,
         in_specs=[VMEM] * 2,
-        out_specs=(VMEM,) * 6,
+        out_specs=(VMEM,) * 5,
         cost_estimate=pl.CostEstimate(
             flops=2 * rows * 1536 * WIDE, bytes_accessed=6 << 20, transcendentals=0
         ),
@@ -595,11 +573,16 @@
     return near + [tp_shift(near[1], 1, 0), tp_shift(near[2], 3, 0)]
 
 
-def tp_scatter(pieces):
+def tp_scatter(pieces, waves):
     got = tp_shift(pieces[6], 1, 0), tp_shift(pieces[7], 3, 0)
-    straight = [tp_shift(p, *s) for p, s in zip(pieces[3:6], NEAR[3:6])]
+    beside = tp_shift(pieces[3], *NEAR[3])
+    later = pieces[4:6]
+    if waves:
+        *got, beside, a, b = lax.optimization_barrier((*got, beside, *later))
+        later = [a, b]
     sums = add_pairs(pieces[1], got[0], pieces[2], got[1])
-    return [pieces[0]] + straight + [tp_shift(p, *s) for p, s in zip(sums, NEAR[1:3])]
+    straight = [tp_shift(p, *s) for p, s in zip(later, NEAR[4:6])]
+    return [pieces[0], beside] + straight + [tp_shift(p, *s) for p, s in zip(sums, NEAR[1:3])]
 
 
 def swap(a, dy, dc):
@@ -612,7 +595,7 @@
 
 
 def attention(blocks, wq, wk, wv, frames, weights):
-    acc, rest = project_near(blocks[:6], fetch(wk, wv, wq))
+    acc, rest = project_near(blocks[:6], jnp.concatenate([wk, wv, wq], axis=1))
     own, other = project_far(acc, rest, *blocks[6:], frames)
     kv, q = join(own, swap(other, 0, 1))
     f, b = ring(kv, 1), ring(kv, -1)
@@ -648,7 +631,7 @@
 
     expert_weights = (gate[0].T, up[0].T, down[0])
     mine, other, own = attention(tp_gather(stream), wq, wk, wv, frames[None, :], expert_weights)
-    mixed, rows = to_slots(tp_scatter(output(mine, other, wo)), stream, slot)
+    mixed, rows = to_slots(tp_scatter(output(mine, other, wo), False), stream, slot)
 
     sending, rows = lax.optimization_barrier((own, rows))
     far = lax.ppermute(sending, "c", [(0, 1), (1, 0)])
@@ -656,8 +639,9 @@
     sent, far = lax.optimization_barrier((sent, far))
     blocks = tp_gather(sent.reshape(EXPERTS * CAP, BLK))
     w1, w2, *early = expert_ready(blocks[:EARLY], gain, own, far)
-    h, *far_pieces = expert_hidden(blocks[EARLY:], gain, w1, w2, *early)
-    summed = sum_all(tp_scatter([*expert_lower(h, w2), *far_pieces]))
+    h, *lowered = expert_hidden(blocks[EARLY:], gain, w1, w2, *early)
+    lowered = dict(zip(FIRST_OUT + NEXT_OUT, [*lowered, *expert_lower(h, w2)]))
+    summed = sum_all(tp_scatter([lowered[shift] for shift in NEAR + FAR], True))
     back = lax.all_to_all(summed.reshape(EXPERTS, CAP, BLK), CHIPS, 0, 0, tiled=True)
     return finish(mixed, back.reshape(EXPERTS * CAP, BLK), slot)
 

time: 178 us -> 174 us (0.978)
  waiting for transfers between devices: 53 us -> 58.1 us
  starting transfers between devices: 59.2 us -> 54.6 us
  local copies, waits for them, and re-layouts: 4.32 us -> 0.04 us
  blocking collectives: 41 us -> 38.7 us
  other arithmetic: 0.62 us -> 2.58 us
    ppermute x28, waiting for transfers between devices: 31.3 us -> 35.7 us  [tp_shift(): return lax.ppermute(a, TP, pairs)]
    unnamed x22 -> x16, local copies, waits for them, and re-layouts: 4.32 us -> 0.04 us
    ppermute x28, starting transfers between devices: 38.5 us -> 35.5 us  [tp_shift(): return lax.ppermute(a, TP, pairs)]
    concatenate x0 -> x1, other arithmetic: none -> 1.96 us  [attention(): acc, rest = project_near(blocks[:6], jnp.concatenate([wk, wv, wq], axis=1))]
    all_to_all x1, blocking collectives: 17.6 us -> 15.7 us  [shards(): lax.all_to_all(summed.reshape(EXPERTS, CAP, BLK), CHIPS, 0, 0, tiled=True)]
  transfers between devices with their start and end apart: 40 -> 40, of which waited for: 22 -> 27; matrix products, arithmetic and copies ran while one was open for 0% -> 1% of each run, Pallas kernels for 6% -> 6%
where the time goes in v2:
time: 174 us
  waiting for transfers between devices  58.1 us (33%)
  starting transfers between devices  54.6 us (31%)
  blocking collectives  38.7 us (22%)
  Pallas kernels  19.2 us (11%)
  other arithmetic  2.58 us (1%)
    ppermute x28, waiting for transfers between devices, tp_shift(): return lax.ppermute(a, TP, pairs)  35.7 us
    ppermute x28, starting transfers between devices, tp_shift(): return lax.ppermute(a, TP, pairs)  35.5 us
    all_to_all x1, blocking collectives, shards(): lax.all_to_all(rows.reshape(EXPERTS, CAP, BLK), CHIPS, 0, 0, tiled=True)  23 us
    all_to_all x1, blocking collectives, shards(): lax.all_to_all(summed.reshape(EXPERTS, CAP, BLK), CHIPS, 0, 0, tiled=True)  15.7 us
    ppermute x6, starting transfers between devices, ring(): return lax.ppermute(a, 'z', [(i, (i + step) % 8) for i in range(8)])  11.4 us
    ppermute x4, waiting for transfers between devices, swap(): return lax.ppermute(a, ('yh', 'c'), pairs)  10.7 us
    pallas_call x1, Pallas kernels, expert_hidden(): pl.pallas_call(hidden_kernel, out_shape=(jax.ShapeDtypeStruct((rows, WIDE...  6.21 us
    ppermute x6, waiting for transfers between devices, ring(): return lax.ppermute(a, 'z', [(i, (i + step) % 8) for i in range(8)])  5.93 us
  transfers between devices with their start and end apart: 40, of which 27 were waited for; matrix products, arithmetic and copies ran while one was open for 1% of the time, Pallas kernels for 6%

profile of v2, /device:TPU:6, one launch (start us, length us, event | category | flops | bytes accessed | tf_op | source)
XLA Modules:
  0.0 173.6 jit_solution(3682122153186108379)
XLA Ops:
  3.5 2.9 %collective-permute-start.3 = (bf16[256,256]{1,0:T(8,128)(2,1)}, bf16[256,256]{1,0:T(8,128)(2,1)S(1)}, u32[]{:S(2)}, u32[]{:S(2)}) collective-permute-start(bf16[256,256]{1,0:T(8,128)(2,1)} %refs_6_.1), channel_id=1, source_target_pairs={{0,3},{1,2},{2,5},{3,4},{4,7},{5,6},{6,1},{7,0},{8,11},{9,10},{10,... | collective-permute-start | bytes 393224 | tf_op jit(solution)/shard_map/ppermute | solution.py:568
  6.5 3.1 %collective-permute-start.5 = (bf16[256,256]{1,0:T(8,128)(2,1)S(1)}, bf16[256,256]{1,0:T(8,128)(2,1)S(1)}, u32[]{:S(2)}, u32[]{:S(2)}) collective-permute-start(bf16[256,256]{1,0:T(8,128)(2,1)S(1)} %collective-permute-done.refs_1_), channel_id=1, source_target_pairs={{0,2},{1,3},{2,4},{3,5},{4,6},{5,7},{6,0},{7,1},{8,10},{9,11},{10,... | collective-permute-start | bytes 393224 | tf_op jit(solution)/shard_map/ppermute | solution.py:568
  19.9 4.0 %collective-permute-start.9 = (bf16[528,256]{1,0:T(8,128)(2,1)S(1)}, bf16[528,256]{1,0:T(8,128)(2,1)S(1)}, u32[]{:S(2)}, u32[]{:S(2)}) collective-permute-start(bf16[528,256]{1,0:T(8,128)(2,1)S(1)} %get-tuple-element.90.kv), channel_id=1, source_target_pairs={{0,224},{32,0},{64,32},{96,64},{128,96},{160,128},{192,160},{224,1... | collective-permute-start | bytes 811016 | tf_op jit(solution)/shard_map/ppermute | solution.py:594
  24.0 2.9 %collective-permute-start.10 = (bf16[528,128]{1,0:T(8,128)(2,1)S(1)}, bf16[528,128]{1,0:T(8,128)(2,1)S(1)}, u32[]{:S(2)}, u32[]{:S(2)}) collective-permute-start(bf16[528,128]{1,0:T(8,128)(2,1)S(1)} %get-tuple-element.91.mine), channel_id=1, source_target_pairs={{0,16},{8,24},{16,0},{24,8},{1,17},{9,25},{17,1},{25,9},{2,18},{10... | collective-permute-start | bytes 405512 | tf_op jit(solution)/shard_map/ppermute | solution.py:590
  26.9 4.0 %collective-permute-done.10.theirs = bf16[528,128]{1,0:T(8,128)(2,1)S(1)} collective-permute-done((bf16[528,128]{1,0:T(8,128)(2,1)S(1)}, bf16[528,128]{1,0:T(8,128)(2,1)S(1)}, u32[]{:S(2)}, u32[]{:S(2)}) %collective-permute-start.10) | collective-permute-done | bytes 135200 | tf_op jit(solution)/shard_map/ppermute | solution.py:590
  30.8 3.2 %collective-permute-start.12 = (bf16[528,256]{1,0:T(8,128)(2,1)S(1)}, bf16[528,256]{1,0:T(8,128)(2,1)S(1)}, u32[]{:S(2)}, u32[]{:S(2)}) collective-permute-start(bf16[528,256]{1,0:T(8,128)(2,1)S(1)} %collective-permute-done.9.b), channel_id=1, source_target_pairs={{0,224},{32,0},{64,32},{96,64},{128,96},{160,128},{192,160},{224,1... | collective-permute-start | bytes 811016 | tf_op jit(solution)/shard_map/ppermute | solution.py:594
  36.4 2.4 %step.3 = (f32[1,1024]{1,0:T(1,128)S(1)}, f32[1,1024]{1,0:T(1,128)S(1)}, f32[128,1024]{1,0:T(8,128)S(1)}) custom-call(bf16[1024,128]{1,0:T(8,128)(2,1)S(1)} %get-tuple-element.116.q_s, f32[1,1024]{1,0:T(1,128)S(1)} %get-tuple-element.117.f_s, f32[1,1024]{1,0:T(1,128)S(1)} %get-tuple-element.97.m_i, f32[1,1024]{1,0:T(1,128)S(1)} %get-tuple-element.98.l_i, ...), custom_call_target="tpu_custom_call" | custom-call | flops 536870912 | bytes 2097152 | tf_op jit(solution)/shard_map/step/pallas_call | solution.py:243
  43.8 4.6 %collective-permute-done.13.f = bf16[528,256]{1,0:T(8,128)(2,1)S(1)} collective-permute-done((bf16[528,256]{1,0:T(8,128)(2,1)S(1)}, bf16[528,256]{1,0:T(8,128)(2,1)S(1)}, u32[]{:S(2)}, u32[]{:S(2)}) %collective-permute-start.13) | collective-permute-done | bytes 270368 | tf_op jit(solution)/shard_map/ppermute | solution.py:594
  50.6 5.8 %collective-permute-done.15.kv = bf16[528,256]{1,0:T(8,128)(2,1)S(1)} collective-permute-done((bf16[528,256]{1,0:T(8,128)(2,1)S(1)}, bf16[528,256]{1,0:T(8,128)(2,1)S(1)}, u32[]{:S(2)}, u32[]{:S(2)}) %collective-permute-start.15) | collective-permute-done | bytes 270368 | tf_op jit(solution)/shard_map/ppermute | solution.py:618
  56.5 2.7 %collective-permute-start.16 = (bf16[144,512]{1,0:T(8,128)(2,1)S(1)}, bf16[144,512]{1,0:T(8,128)(2,1)S(1)}, u32[]{:S(2)}, u32[]{:S(2)}) collective-permute-start(bf16[144,512]{1,0:T(8,128)(2,1)S(1)} %get-tuple-element.127), channel_id=1, source_target_pairs={{0,16},{8,24},{16,0},{24,8},{1,17},{9,25},{17,1},{25,9},{2,18},{10... | collective-permute-start | bytes 442376 | tf_op jit(solution)/shard_map/ppermute | solution.py:590
  59.2 4.1 %collective-permute-done.16.b = bf16[144,512]{1,0:T(8,128)(2,1)S(1)} collective-permute-done((bf16[144,512]{1,0:T(8,128)(2,1)S(1)}, bf16[144,512]{1,0:T(8,128)(2,1)S(1)}, u32[]{:S(2)}, u32[]{:S(2)}) %collective-permute-start.16) | collective-permute-done | bytes 147488 | tf_op jit(solution)/shard_map/ppermute | solution.py:590
  77.3 3.8 %collective-permute-done.24.refs_5_ = bf16[256,256]{1,0:T(8,128)(2,1)S(1)} collective-permute-done((bf16[256,256]{1,0:T(8,128)(2,1)S(1)}, bf16[256,256]{1,0:T(8,128)(2,1)S(1)}, u32[]{:S(2)}, u32[]{:S(2)}) %collective-permute-start.24) | collective-permute-done | bytes 131104 | tf_op jit(solution)/shard_map/ppermute | solution.py:568
  81.5 23.0 %all_to_all.10 = bf16[16,32,256]{2,1,0:T(8,128)(2,1)S(1)} all-to-all(bf16[16,32,256]{2,1,0:T(8,128)(2,1)S(1)} %bitcast.25), channel_id=1, replica_groups=mesh['z'=8,'yh'=2,'c'=2,'x'=4,'yl'=2] {'z','yh'}, dimensions={0} | all-to-all | bytes 524288 | tf_op jit(solution)/shard_map/all_to_all | solution.py:638
  104.5 2.4 %collective-permute-start.31 = (bf16[512,256]{1,0:T(8,128)(2,1)S(1)}, bf16[512,256]{1,0:T(8,128)(2,1)S(1)}, u32[]{:S(2)}, u32[]{:S(2)}) collective-permute-start(bf16[512,256]{1,0:T(8,128)(2,1)S(1)} %bitcast.18), channel_id=1, source_target_pairs={{0,7},{1,6},{2,1},{3,0},{4,3},{5,2},{6,5},{7,4},{8,15},{9,14},{10,... | collective-permute-start | bytes 786440 | tf_op jit(solution)/shard_map/ppermute | solution.py:568
  110.4 3.4 %collective-permute-done.29.b1 = bf16[512,256]{1,0:T(8,128)(2,1)S(1)} collective-permute-done((bf16[512,256]{1,0:T(8,128)(2,1)S(1)}, bf16[512,256]{1,0:T(8,128)(2,1)S(1)}, u32[]{:S(2)}, u32[]{:S(2)}) %collective-permute-start.29) | collective-permute-done | bytes 262176 | tf_op jit(solution)/shard_map/ppermute | solution.py:568
  118.6 2.5 %expert_ready.1 = (bf16[1536,2048]{1,0:T(8,128)(2,1)S(1)}, bf16[768,2048]{1,0:T(8,128)(2,1)S(1)}, bf16[512,768]{1,0:T(8,128)(2,1)S(1)}, f32[512,1]{1,0:T(8,128)S(1)}) custom-call(bf16[512,256]{1,0:T(8,128)(2,1)S(1)} %bitcast.22, bf16[512,256]{1,0:T(8,128)(2,1)S(1)} %collective-permute-done.29.b1, bf16[512,256]{1,0:T(8,128)(2,1)S(1)} %collective-permute-done.31.b2, ...), custom_call_target="tpu_custom_call" | custom-call | flops 1048576 | bytes 18874368 | tf_op jit(solution)/shard_map/expert_ready/pallas_call | solution.py:460
  121.1 3.6 %collective-permute-done.26.refs_0_ = bf16[512,256]{1,0:T(8,128)(2,1)S(1)} collective-permute-done((bf16[512,256]{1,0:T(8,128)(2,1)S(1)}, bf16[512,256]{1,0:T(8,128)(2,1)S(1)}, u32[]{:S(2)}, u32[]{:S(2)}) %collective-permute-start.26) | collective-permute-done | bytes 262176 | tf_op jit(solution)/shard_map/ppermute | solution.py:568
  124.7 6.2 %expert_hidden.1 = (bf16[512,768]{1,0:T(8,128)(2,1)S(1)}, bf16[512,256]{1,0:T(8,128)(2,1)S(1)}, bf16[512,256]{1,0:T(8,128)(2,1)S(1)}, bf16[512,256]{1,0:T(8,128)(2,1)S(1)}) custom-call(bf16[512,256]{1,0:T(8,128)(2,1)S(1)} %collective-permute-done.26.refs_0_, bf16[512,256]{1,0:T(8,128)(2,1)S(1)} %collective-permute-done.27.refs_1_, ...), custom_call_target="tpu_custom_call" | custom-call | flops 4026531840 | bytes 13631488 | tf_op jit(solution)/shard_map/expert_hidden/pallas_call | solution.py:513
  135.5 3.3 %collective-permute-done.33.b0 = bf16[512,256]{1,0:T(8,128)(2,1)S(1)} collective-permute-done((bf16[512,256]{1,0:T(8,128)(2,1)S(1)}, bf16[512,256]{1,0:T(8,128)(2,1)S(1)}, u32[]{:S(2)}, u32[]{:S(2)}) %collective-permute-start.33) | collective-permute-done | bytes 262176 | tf_op jit(solution)/shard_map/ppermute | solution.py:568
  143.3 2.9 %collective-permute-start.36 = (bf16[512,256]{1,0:T(8,128)(2,1)S(1)}, bf16[512,256]{1,0:T(8,128)(2,1)S(1)}, u32[]{:S(2)}, u32[]{:S(2)}) collective-permute-start(bf16[512,256]{1,0:T(8,128)(2,1)S(1)} %get-tuple-element.159), channel_id=1, source_target_pairs={{0,3},{1,2},{2,5},{3,4},{4,7},{5,6},{6,1},{7,0},{8,11},{9,10},{10,... | collective-permute-start | bytes 786440 | tf_op jit(solution)/shard_map/ppermute | solution.py:568
  146.2 3.7 %collective-permute-done.38.refs_4_ = bf16[512,256]{1,0:T(8,128)(2,1)S(1)} collective-permute-done((bf16[512,256]{1,0:T(8,128)(2,1)S(1)}, bf16[512,256]{1,0:T(8,128)(2,1)S(1)}, u32[]{:S(2)}, u32[]{:S(2)}) %collective-permute-start.38) | collective-permute-done | bytes 262176 | tf_op jit(solution)/shard_map/ppermute | solution.py:568
  150.0 3.7 %collective-permute-done.39.refs_5_ = bf16[512,256]{1,0:T(8,128)(2,1)S(1)} collective-permute-done((bf16[512,256]{1,0:T(8,128)(2,1)S(1)}, bf16[512,256]{1,0:T(8,128)(2,1)S(1)}, u32[]{:S(2)}, u32[]{:S(2)}) %collective-permute-start.39) | collective-permute-done | bytes 262176 | tf_op jit(solution)/shard_map/ppermute | solution.py:568
  153.7 2.5 %collective-permute-done.36.refs_2_ = bf16[512,256]{1,0:T(8,128)(2,1)S(1)} collective-permute-done((bf16[512,256]{1,0:T(8,128)(2,1)S(1)}, bf16[512,256]{1,0:T(8,128)(2,1)S(1)}, u32[]{:S(2)}, u32[]{:S(2)}) %collective-permute-start.36) | collective-permute-done | bytes 262176 | tf_op jit(solution)/shard_map/ppermute | solution.py:568
  156.9 15.7 %all_to_all.11 = bf16[16,32,256]{2,1,0:T(8,128)(2,1)S(1)} all-to-all(bf16[16,32,256]{2,1,0:T(8,128)(2,1)S(1)} %bitcast.23), channel_id=1, replica_groups=mesh['z'=8,'yh'=2,'c'=2,'x'=4,'yl'=2] {'z','yh'}, dimensions={0} | all-to-all | bytes 524288 | tf_op jit(solution)/shard_map/all_to_all | solution.py:645
  (97 shorter events, 56.9 us)
Async XLA Ops:
  2.2 8.4 %collective-permute-start.1 = (bf16[256,256]{1,0:T(8,128)(2,1)}, bf16[256,256]{1,0:T(8,128)(2,1)S(1)}, u32[]{:S(2)}, u32[]{:S(2)}) collective-permute-start(bf16[256,256]{1,0:T(8,128)(2,1)} %refs_6_.1), channel_id=1, source_target_pairs={{0,7},{1,6},{2,1},{3,0},{4,3},{5,2},{6,5},{7,4},{8,15},{9,14},{10,... | collective-permute-start | bytes 393224 | tf_op jit(solution)/shard_map/ppermute | solution.py:568
  3.0 10.2 %collective-permute-start.2 = (bf16[256,256]{1,0:T(8,128)(2,1)}, bf16[256,256]{1,0:T(8,128)(2,1)S(1)}, u32[]{:S(2)}, u32[]{:S(2)}) collective-permute-start(bf16[256,256]{1,0:T(8,128)(2,1)} %refs_6_.1), channel_id=1, source_target_pairs={{0,1},{1,0},{2,3},{3,2},{4,5},{5,4},{6,7},{7,6},{8,9},{9,8},{10,11... | collective-permute-start | bytes 393224 | tf_op jit(solution)/shard_map/ppermute | solution.py:568
  3.5 9.8 %collective-permute-start.3 = (bf16[256,256]{1,0:T(8,128)(2,1)}, bf16[256,256]{1,0:T(8,128)(2,1)S(1)}, u32[]{:S(2)}, u32[]{:S(2)}) collective-permute-start(bf16[256,256]{1,0:T(8,128)(2,1)} %refs_6_.1), channel_id=1, source_target_pairs={{0,3},{1,2},{2,5},{3,4},{4,7},{5,6},{6,1},{7,0},{8,11},{9,10},{10,... | collective-permute-start | bytes 393224 | tf_op jit(solution)/shard_map/ppermute | solution.py:568
  6.5 8.7 %collective-permute-start.5 = (bf16[256,256]{1,0:T(8,128)(2,1)S(1)}, bf16[256,256]{1,0:T(8,128)(2,1)S(1)}, u32[]{:S(2)}, u32[]{:S(2)}) collective-permute-start(bf16[256,256]{1,0:T(8,128)(2,1)S(1)} %collective-permute-done.refs_1_), channel_id=1, source_target_pairs={{0,2},{1,3},{2,4},{3,5},{4,6},{5,7},{6,0},{7,1},{8,10},{9,11},{10,... | collective-permute-start | bytes 393224 | tf_op jit(solution)/shard_map/ppermute | solution.py:568
  19.1 11.7 %collective-permute-start.8 = (bf16[528,256]{1,0:T(8,128)(2,1)S(1)}, bf16[528,256]{1,0:T(8,128)(2,1)S(1)}, u32[]{:S(2)}, u32[]{:S(2)}) collective-permute-start(bf16[528,256]{1,0:T(8,128)(2,1)S(1)} %get-tuple-element.90.kv), channel_id=1, source_target_pairs={{0,32},{32,64},{64,96},{96,128},{128,160},{160,192},{192,224},{224... | collective-permute-start | bytes 811016 | tf_op jit(solution)/shard_map/ppermute | solution.py:594
  19.9 10.9 %collective-permute-start.9 = (bf16[528,256]{1,0:T(8,128)(2,1)S(1)}, bf16[528,256]{1,0:T(8,128)(2,1)S(1)}, u32[]{:S(2)}, u32[]{:S(2)}) collective-permute-start(bf16[528,256]{1,0:T(8,128)(2,1)S(1)} %get-tuple-element.90.kv), channel_id=1, source_target_pairs={{0,224},{32,0},{64,32},{96,64},{128,96},{160,128},{192,160},{224,1... | collective-permute-start | bytes 811016 | tf_op jit(solution)/shard_map/ppermute | solution.py:594
  30.8 9.1 %collective-permute-start.11 = (bf16[528,256]{1,0:T(8,128)(2,1)S(1)}, bf16[528,256]{1,0:T(8,128)(2,1)S(1)}, u32[]{:S(2)}, u32[]{:S(2)}) collective-permute-start(bf16[528,256]{1,0:T(8,128)(2,1)S(1)} %collective-permute-done.8.f), channel_id=1, source_target_pairs={{0,32},{32,64},{64,96},{96,128},{128,160},{160,192},{192,224},{224... | collective-permute-start | bytes 811016 | tf_op jit(solution)/shard_map/ppermute | solution.py:594
  30.8 9.1 %collective-permute-start.12 = (bf16[528,256]{1,0:T(8,128)(2,1)S(1)}, bf16[528,256]{1,0:T(8,128)(2,1)S(1)}, u32[]{:S(2)}, u32[]{:S(2)}) collective-permute-start(bf16[528,256]{1,0:T(8,128)(2,1)S(1)} %collective-permute-done.9.b), channel_id=1, source_target_pairs={{0,224},{32,0},{64,32},{96,64},{128,96},{160,128},{192,160},{224,1... | collective-permute-start | bytes 811016 | tf_op jit(solution)/shard_map/ppermute | solution.py:594
  39.9 8.5 %collective-permute-start.13 = (bf16[528,256]{1,0:T(8,128)(2,1)S(1)}, bf16[528,256]{1,0:T(8,128)(2,1)S(1)}, u32[]{:S(2)}, u32[]{:S(2)}) collective-permute-start(bf16[528,256]{1,0:T(8,128)(2,1)S(1)} %collective-permute-done.11.f), channel_id=1, source_target_pairs={{0,32},{32,64},{64,96},{96,128},{128,160},{160,192},{192,224},{224... | collective-permute-start | bytes 811016 | tf_op jit(solution)/shard_map/ppermute | solution.py:594
  67.5 7.9 %collective-permute-start.18 = (bf16[256,256]{1,0:T(8,128)(2,1)S(1)}, bf16[256,256]{1,0:T(8,128)(2,1)S(1)}, u32[]{:S(2)}, u32[]{:S(2)}) collective-permute-start(bf16[256,256]{1,0:T(8,128)(2,1)S(1)} %get-tuple-element.131), channel_id=1, source_target_pairs={{0,1},{1,0},{2,3},{3,2},{4,5},{5,4},{6,7},{7,6},{8,9},{9,8},{10,11... | collective-permute-start | bytes 393224 | tf_op jit(solution)/shard_map/ppermute | solution.py:568
  81.4 23.1 %collective-permute-start.25 = (bf16[1056,2048]{1,0:T(8,128)(2,1)S(1)}, bf16[1056,2048]{1,0:T(8,128)(2,1)S(1)}, u32[]{:S(2)}, u32[]{:S(2)}) collective-permute-start(bf16[1056,2048]{1,0:T(8,128)(2,1)S(1)} %pad_maximum_fusion.own), channel_id=1, source_target_pairs={{0,8},{8,0},{1,9},{9,1},{2,10},{10,2},{3,11},{11,3},{4,12},{12,4},... | collective-permute-start | bytes 12976136 | tf_op jit(solution)/shard_map/ppermute | solution.py:637
  104.5 9.3 %collective-permute-start.29 = (bf16[512,256]{1,0:T(8,128)(2,1)S(1)}, bf16[512,256]{1,0:T(8,128)(2,1)S(1)}, u32[]{:S(2)}, u32[]{:S(2)}) collective-permute-start(bf16[512,256]{1,0:T(8,128)(2,1)S(1)} %bitcast.17), channel_id=1, source_target_pairs={{0,2},{1,3},{2,4},{3,5},{4,6},{5,7},{6,0},{7,1},{8,10},{9,11},{10,... | collective-permute-start | bytes 786440 | tf_op jit(solution)/shard_map/ppermute | solution.py:568
  104.5 12.1 %collective-permute-start.31 = (bf16[512,256]{1,0:T(8,128)(2,1)S(1)}, bf16[512,256]{1,0:T(8,128)(2,1)S(1)}, u32[]{:S(2)}, u32[]{:S(2)}) collective-permute-start(bf16[512,256]{1,0:T(8,128)(2,1)S(1)} %bitcast.18), channel_id=1, source_target_pairs={{0,7},{1,6},{2,1},{3,0},{4,3},{5,2},{6,5},{7,4},{8,15},{9,14},{10,... | collective-permute-start | bytes 786440 | tf_op jit(solution)/shard_map/ppermute | solution.py:568
  106.9 17.8 %collective-permute-start.26 = (bf16[512,256]{1,0:T(8,128)(2,1)S(1)}, bf16[512,256]{1,0:T(8,128)(2,1)S(1)}, u32[]{:S(2)}, u32[]{:S(2)}) collective-permute-start(bf16[512,256]{1,0:T(8,128)(2,1)S(1)} %bitcast.19), channel_id=1, source_target_pairs={{0,1},{1,0},{2,3},{3,2},{4,5},{5,4},{6,7},{7,6},{8,9},{9,8},{10,11... | collective-permute-start | bytes 786440 | tf_op jit(solution)/shard_map/ppermute | solution.py:568
  108.0 16.7 %collective-permute-start.27 = (bf16[512,256]{1,0:T(8,128)(2,1)S(1)}, bf16[512,256]{1,0:T(8,128)(2,1)S(1)}, u32[]{:S(2)}, u32[]{:S(2)}) collective-permute-start(bf16[512,256]{1,0:T(8,128)(2,1)S(1)} %bitcast.20), channel_id=1, source_target_pairs={{0,3},{1,2},{2,5},{3,4},{4,7},{5,6},{6,1},{7,0},{8,11},{9,10},{10,... | collective-permute-start | bytes 786440 | tf_op jit(solution)/shard_map/ppermute | solution.py:568
  109.6 15.1 %collective-permute-start.28 = (bf16[512,256]{1,0:T(8,128)(2,1)S(1)}, bf16[512,256]{1,0:T(8,128)(2,1)S(1)}, u32[]{:S(2)}, u32[]{:S(2)}) collective-permute-start(bf16[512,256]{1,0:T(8,128)(2,1)S(1)} %bitcast.21), channel_id=1, source_target_pairs={{0,6},{1,7},{2,0},{3,1},{4,2},{5,3},{6,4},{7,5},{8,14},{9,15},{10,... | collective-permute-start | bytes 786440 | tf_op jit(solution)/shard_map/ppermute | solution.py:568
  113.8 10.8 %collective-permute-start.30 = (bf16[512,256]{1,0:T(8,128)(2,1)S(1)}, bf16[512,256]{1,0:T(8,128)(2,1)S(1)}, u32[]{:S(2)}, u32[]{:S(2)}) collective-permute-start(bf16[512,256]{1,0:T(8,128)(2,1)S(1)} %collective-permute-done.29.b1), channel_id=1, source_target_pairs={{0,2},{1,3},{2,4},{3,5},{4,6},{5,7},{6,0},{7,1},{8,10},{9,11},{10,... | collective-permute-start | bytes 786440 | tf_op jit(solution)/shard_map/ppermute | solution.py:568
  116.6 8.1 %collective-permute-start.32 = (bf16[512,256]{1,0:T(8,128)(2,1)S(1)}, bf16[512,256]{1,0:T(8,128)(2,1)S(1)}, u32[]{:S(2)}, u32[]{:S(2)}) collective-permute-start(bf16[512,256]{1,0:T(8,128)(2,1)S(1)} %collective-permute-done.31.b2), channel_id=1, source_target_pairs={{0,6},{1,7},{2,0},{3,1},{4,2},{5,3},{6,4},{7,5},{8,14},{9,15},{10,... | collective-permute-start | bytes 786440 | tf_op jit(solution)/shard_map/ppermute | solution.py:568
  130.9 7.9 %collective-permute-start.33 = (bf16[512,256]{1,0:T(8,128)(2,1)S(1)}, bf16[512,256]{1,0:T(8,128)(2,1)S(1)}, u32[]{:S(2)}, u32[]{:S(2)}) collective-permute-start(bf16[512,256]{1,0:T(8,128)(2,1)S(1)} %get-tuple-element.153), channel_id=1, source_target_pairs={{0,2},{1,3},{2,4},{3,5},{4,6},{5,7},{6,0},{7,1},{8,10},{9,11},{10,... | collective-permute-start | bytes 786440 | tf_op jit(solution)/shard_map/ppermute | solution.py:568
  131.0 9.1 %collective-permute-start.34 = (bf16[512,256]{1,0:T(8,128)(2,1)S(1)}, bf16[512,256]{1,0:T(8,128)(2,1)S(1)}, u32[]{:S(2)}, u32[]{:S(2)}) collective-permute-start(bf16[512,256]{1,0:T(8,128)(2,1)S(1)} %get-tuple-element.154), channel_id=1, source_target_pairs={{0,6},{1,7},{2,0},{3,1},{4,2},{5,3},{6,4},{7,5},{8,14},{9,15},{10,... | collective-permute-start | bytes 786440 | tf_op jit(solution)/shard_map/ppermute | solution.py:568
  140.4 9.5 %collective-permute-start.38 = (bf16[512,256]{1,0:T(8,128)(2,1)S(1)}, bf16[512,256]{1,0:T(8,128)(2,1)S(1)}, u32[]{:S(2)}, u32[]{:S(2)}) collective-permute-start(bf16[512,256]{1,0:T(8,128)(2,1)S(1)} %get-tuple-element.165), channel_id=1, source_target_pairs={{0,2},{1,3},{2,4},{3,5},{4,6},{5,7},{6,0},{7,1},{8,10},{9,11},{10,... | collective-permute-start | bytes 786440 | tf_op jit(solution)/shard_map/ppermute | solution.py:568
  142.1 11.6 %collective-permute-start.39 = (bf16[512,256]{1,0:T(8,128)(2,1)S(1)}, bf16[512,256]{1,0:T(8,128)(2,1)S(1)}, u32[]{:S(2)}, u32[]{:S(2)}) collective-permute-start(bf16[512,256]{1,0:T(8,128)(2,1)S(1)} %get-tuple-element.166), channel_id=1, source_target_pairs={{0,7},{1,6},{2,1},{3,0},{4,3},{5,2},{6,5},{7,4},{8,15},{9,14},{10,... | collective-permute-start | bytes 786440 | tf_op jit(solution)/shard_map/ppermute | solution.py:568
  143.3 12.9 %collective-permute-start.36 = (bf16[512,256]{1,0:T(8,128)(2,1)S(1)}, bf16[512,256]{1,0:T(8,128)(2,1)S(1)}, u32[]{:S(2)}, u32[]{:S(2)}) collective-permute-start(bf16[512,256]{1,0:T(8,128)(2,1)S(1)} %get-tuple-element.159), channel_id=1, source_target_pairs={{0,3},{1,2},{2,5},{3,4},{4,7},{5,6},{6,1},{7,0},{8,11},{9,10},{10,... | collective-permute-start | bytes 786440 | tf_op jit(solution)/shard_map/ppermute | solution.py:568
  146.2 10.5 %collective-permute-start.37 = (bf16[512,256]{1,0:T(8,128)(2,1)S(1)}, bf16[512,256]{1,0:T(8,128)(2,1)S(1)}, u32[]{:S(2)}, u32[]{:S(2)}) collective-permute-start(bf16[512,256]{1,0:T(8,128)(2,1)S(1)} %get-tuple-element.160), channel_id=1, source_target_pairs={{0,6},{1,7},{2,0},{3,1},{4,2},{5,3},{6,4},{7,5},{8,14},{9,15},{10,... | collective-permute-start | bytes 786440 | tf_op jit(solution)/shard_map/ppermute | solution.py:568
  (24 other events, 295.7 us)

commit v3 on v2

--- a/solution.py
+++ b/solution.py
@@ -148,14 +148,14 @@
     )(own, got)
 
 
-def visit(q_s, f_s, m_s, l_s, acc_s, kv, masked):
+def visit(q_s, f_s, m_s, l_s, acc_s, kv, masked, wide):
     scale = 1.0 / math.sqrt(HEAD)
     if masked:
         lines = [jnp.broadcast_to(kv[r : r + 1, :].astype(F32), (HEAD, BLK)) for r in (2 * BLK, 2 * BLK + 1)]
         frames = jnp.concatenate([jnp.transpose(line)[:, :1] for line in lines], axis=0)
 
     def part(i, carry):
-        lanes = pl.ds(pl.multiple_of(i * BLK, BLK), BLK)
+        lanes = pl.ds(pl.multiple_of(i * wide, wide), wide)
         s = nt_dot(kv[: 2 * BLK, :HEAD], q_s[lanes, :]) * scale
         if masked:
             allowed = frames <= f_s[:, lanes]
@@ -171,10 +171,10 @@
         acc_s[:, lanes] = acc_s[:, lanes] * decay + tn_dot(kv[: 2 * BLK, HEAD:], p.astype(BF16))
         return carry
 
-    lax.fori_loop(0, 4, part, 0)
-
-
-def local_kernel(mine, theirs, kv, q_s, f_s, m_s, l_s, acc_s):
+    lax.fori_loop(0, 4 * BLK // wide, part, 0)
+
+
+def first_kernel(mine, theirs, own, f, b, q_s, f_s, m_s, l_s, acc_s, kv):
     for g, q in enumerate((mine, theirs)):
         q_s[g * 2 * BLK : (g + 1) * 2 * BLK, :] = q[: 2 * BLK, :]
         for i in range(4):
@@ -183,7 +183,26 @@
     m_s[...] = jnp.full_like(m_s, NEG)
     l_s[...] = jnp.zeros_like(l_s)
     acc_s[...] = jnp.zeros_like(acc_s)
-    visit(q_s, f_s, m_s, l_s, acc_s, kv, True)
+    z = lax.axis_index("z")
+    wanted = (z >= 0, z >= 1, (z == 7) | (lax.axis_index("yh") == 0))
+
+    def side(j, carry):
+        need = z < 0
+        for i, (block, want) in enumerate(zip((own, f, b), wanted)):
+
+            @pl.when((j == i) & want)
+            def _():
+                kv[...] = block[...]
+
+            need = need | ((j == i) & want)
+
+        @pl.when(need)
+        def _():
+            visit(q_s, f_s, m_s, l_s, acc_s, kv, True, 2 * BLK)
+
+        return carry
+
+    lax.fori_loop(0, 3, side, 0)
 
 
 STATE = (
@@ -200,16 +219,17 @@
     return pl.CostEstimate(flops=4 * work * HEAD, bytes_accessed=2 << 20, transcendentals=work)
 
 
-def local(mine, theirs, kv):
-    return pl.pallas_call(
-        local_kernel,
+def first(mine, theirs, own, f, b):
+    return pl.pallas_call(
+        first_kernel,
         out_shape=STATE,
-        in_specs=[VMEM] * 3,
+        in_specs=[VMEM] * 5,
         out_specs=(VMEM,) * 5,
-        cost_estimate=visit_cost(4),
+        scratch_shapes=[pltpu.VMEM(f.shape, BF16)],
+        cost_estimate=visit_cost(6),
         compiler_params=vmem(24),
-        name="local",
-    )(mine, theirs, kv)
+        name="first",
+    )(mine, theirs, own, f, b)
 
 
 def step_kernel(k, q_s, f_s, m_i, l_i, acc_i, f, b, m_s, l_s, acc_s, kv):
@@ -217,22 +237,19 @@
     m_s[...] = m_i[...]
     l_s[...] = l_i[...]
     acc_s[...] = acc_i[...]
-    wrapped = z + k >= 8
-    if k == 1:
-        wrapped = wrapped | (lax.axis_index("yh") == 0)
 
     def side(j, carry):
         @pl.when((j == 0) & (z >= k))
         def _():
             kv[...] = f[...]
 
-        @pl.when((j == 1) & wrapped)
+        @pl.when((j == 1) & (z + k >= 8))
         def _():
             kv[...] = b[...]
 
-        @pl.when(((j == 0) & (z >= k)) | ((j == 1) & wrapped))
+        @pl.when(((j == 0) & (z >= k)) | ((j == 1) & (z + k >= 8)))
         def _():
-            visit(q_s, f_s, m_s, l_s, acc_s, kv, k == 1)
+            visit(q_s, f_s, m_s, l_s, acc_s, kv, False, BLK)
 
         return carry
 
@@ -260,7 +277,7 @@
 
     @pl.when(lax.axis_index("z") >= 4)
     def _():
-        visit(q_s, f_s, m_s, l_s, acc_s, kv, False)
+        visit(q_s, f_s, m_s, l_s, acc_s, kv, False, 2 * BLK)
 
     for g, out in enumerate((mine, theirs)):
         lanes = slice(g * 2 * BLK, (g + 1) * 2 * BLK)
@@ -576,12 +593,10 @@
 def tp_scatter(pieces, waves):
     got = tp_shift(pieces[6], 1, 0), tp_shift(pieces[7], 3, 0)
     beside = tp_shift(pieces[3], *NEAR[3])
-    later = pieces[4:6]
     if waves:
-        *got, beside, a, b = lax.optimization_barrier((*got, beside, *later))
-        later = [a, b]
+        *got, beside = lax.optimization_barrier((*got, beside))
     sums = add_pairs(pieces[1], got[0], pieces[2], got[1])
-    straight = [tp_shift(p, *s) for p, s in zip(later, NEAR[4:6])]
+    straight = [tp_shift(p, *s) for p, s in zip(pieces[4:6], NEAR[4:6])]
     return [pieces[0], beside] + straight + [tp_shift(p, *s) for p, s in zip(sums, NEAR[1:3])]
 
 
@@ -601,7 +616,7 @@
     f, b = ring(kv, 1), ring(kv, -1)
     theirs = swap(q, 1, 0)
     f, b, theirs = lax.optimization_barrier((f, b, theirs))
-    state = local(q, theirs, kv)
+    state = None
     for k in range(1, 4):
         if k == 2:
             f, b, *held = lax.optimization_barrier((f, b, *state, *weights))
@@ -616,10 +631,12 @@
             way = jnp.where(lax.axis_index("c") == 0, f, b)
             hops = [(i * 2 + c, (i + (-1 if c else 1)) % 8 * 2 + c) for i in range(8) for c in range(2)]
             far = lax.ppermute(way, ("z", "c"), hops)
-        state = step(k, state, *here)
+        state = step(k, state, *here) if state else first(q, theirs, kv, *here)
+    far_weights = lax.ppermute(weights, "c", [(0, 1), (1, 0)])
     mine, theirs = last(state, far)
-    mine, other = merge(mine, swap(theirs, 1, 0))
-    return mine, swap(other, 0, 1), weights
+    theirs, far_weights = lax.optimization_barrier((swap(theirs, 1, 0), far_weights))
+    mine, other = merge(mine, theirs)
+    return mine, swap(other, 0, 1), weights, far_weights
 
 
 def shards(stream, frames, fidelity, wq, wk, wv, wo, gain, gate, up, down):
@@ -630,13 +647,10 @@
     gain = gain[None, :]
 
     expert_weights = (gate[0].T, up[0].T, down[0])
-    mine, other, own = attention(tp_gather(stream), wq, wk, wv, frames[None, :], expert_weights)
+    mine, other, own, far = attention(tp_gather(stream), wq, wk, wv, frames[None, :], expert_weights)
     mixed, rows = to_slots(tp_scatter(output(mine, other, wo), False), stream, slot)
 
-    sending, rows = lax.optimization_barrier((own, rows))
-    far = lax.ppermute(sending, "c", [(0, 1), (1, 0)])
     sent = lax.all_to_all(rows.reshape(EXPERTS, CAP, BLK), CHIPS, 0, 0, tiled=True)
-    sent, far = lax.optimization_barrier((sent, far))
     blocks = tp_gather(sent.reshape(EXPERTS * CAP, BLK))
     w1, w2, *early = expert_ready(blocks[:EARLY], gain, own, far)
     h, *lowered = expert_hidden(blocks[EARLY:], gain, w1, w2, *early)

time: 174 us -> 171 us (0.983)
  blocking collectives: 38.7 us -> 35.4 us
  starting transfers between devices: 54.6 us -> 52 us
  other arithmetic: 2.58 us -> 4.52 us
    ppermute x28, starting transfers between devices: 35.5 us -> 32.7 us  [tp_shift(): return lax.ppermute(a, TP, pairs)]
    ppermute x28, waiting for transfers between devices: 35.7 us -> 38.2 us  [tp_shift(): return lax.ppermute(a, TP, pairs)]
    all_to_all x1, blocking collectives: 23 us -> 20.6 us  [shards(): lax.all_to_all(rows.reshape(EXPERTS, CAP, BLK), CHIPS, 0, 0, tiled=True)]
    pallas_call x3 -> x2, Pallas kernels: 2.58 us -> 0.15 us  [step(): pl.pallas_call(functools.partial(step_kernel, k), out_shape=STATE[2:], in...]
    concatenate x1, other arithmetic: 0.4 us -> 2.34 us  [attention(): weights = jnp.concatenate(weights, axis=0)]
  transfers between devices with their start and end apart: 40 -> 40, of which waited for: 27 -> 25; matrix products, arithmetic and copies ran while one was open for 1% -> 3% of each run, Pallas kernels for 6% -> 6%
where the time goes in v3:
time: 171 us
  waiting for transfers between devices  59.3 us (35%)
  starting transfers between devices  52 us (30%)
  blocking collectives  35.4 us (21%)
  Pallas kernels  19.4 us (11%)
  other arithmetic  4.52 us (3%)
    ppermute x28, waiting for transfers between devices, tp_shift(): return lax.ppermute(a, TP, pairs)  38.2 us
    ppermute x28, starting transfers between devices, tp_shift(): return lax.ppermute(a, TP, pairs)  32.7 us
    all_to_all x1, blocking collectives, shards(): lax.all_to_all(rows.reshape(EXPERTS, CAP, BLK), CHIPS, 0, 0, tiled=True)  20.6 us
    all_to_all x1, blocking collectives, shards(): lax.all_to_all(summed.reshape(EXPERTS, CAP, BLK), CHIPS, 0, 0, tiled=True)  14.9 us
    ppermute x6, starting transfers between devices, ring(): return lax.ppermute(a, 'z', [(i, (i + step) % 8) for i in range(8)])  11.3 us
    ppermute x4, waiting for transfers between devices, swap(): return lax.ppermute(a, ('yh', 'c'), pairs)  10.4 us
    pallas_call x1, Pallas kernels, expert_hidden(): pl.pallas_call(hidden_kernel, out_shape=(jax.ShapeDtypeStruct((rows, WIDE...  6.21 us
    ppermute x1, waiting for transfers between devices, attention(): far = lax.ppermute(way, ('z', 'c'), hops)  6.16 us
  transfers between devices with their start and end apart: 40, of which 25 were waited for; matrix products, arithmetic and copies ran while one was open for 3% of the time, Pallas kernels for 6%

profile of v3, /device:TPU:6, one launch (start us, length us, event | category | flops | bytes accessed | tf_op | source)
XLA Modules:
  0.0 170.9 jit_solution(9988745949353702055)
XLA Ops:
  0.0 2.2 %collective-permute-start = (bf16[256,256]{1,0:T(8,128)(2,1)}, bf16[256,256]{1,0:T(8,128)(2,1)S(1)}, u32[]{:S(2)}, u32[]{:S(2)}) collective-permute-start(bf16[256,256]{1,0:T(8,128)(2,1)} %refs_6_.1), channel_id=1, source_target_pairs={{0,2},{1,3},{2,4},{3,5},{4,6},{5,7},{6,0},{7,1},{8,10},{9,11},{10,... | collective-permute-start | bytes 393224 | tf_op jit(solution)/shard_map/ppermute | solution.py:585
  3.5 2.9 %collective-permute-start.3 = (bf16[256,256]{1,0:T(8,128)(2,1)}, bf16[256,256]{1,0:T(8,128)(2,1)S(1)}, u32[]{:S(2)}, u32[]{:S(2)}) collective-permute-start(bf16[256,256]{1,0:T(8,128)(2,1)} %refs_6_.1), channel_id=1, source_target_pairs={{0,3},{1,2},{2,5},{3,4},{4,7},{5,6},{6,1},{7,0},{8,11},{9,10},{10,... | collective-permute-start | bytes 393224 | tf_op jit(solution)/shard_map/ppermute | solution.py:585
  6.5 3.1 %collective-permute-start.5 = (bf16[256,256]{1,0:T(8,128)(2,1)S(1)}, bf16[256,256]{1,0:T(8,128)(2,1)S(1)}, u32[]{:S(2)}, u32[]{:S(2)}) collective-permute-start(bf16[256,256]{1,0:T(8,128)(2,1)S(1)} %collective-permute-done.refs_1_), channel_id=1, source_target_pairs={{0,2},{1,3},{2,4},{3,5},{4,6},{5,7},{6,0},{7,1},{8,10},{9,11},{10,... | collective-permute-start | bytes 393224 | tf_op jit(solution)/shard_map/ppermute | solution.py:585
  19.9 4.0 %collective-permute-start.9 = (bf16[528,256]{1,0:T(8,128)(2,1)S(1)}, bf16[528,256]{1,0:T(8,128)(2,1)S(1)}, u32[]{:S(2)}, u32[]{:S(2)}) collective-permute-start(bf16[528,256]{1,0:T(8,128)(2,1)S(1)} %get-tuple-element.83.own), channel_id=1, source_target_pairs={{0,224},{32,0},{64,32},{96,64},{128,96},{160,128},{192,160},{224,1... | collective-permute-start | bytes 811016 | tf_op jit(solution)/shard_map/ppermute | solution.py:609
  24.0 2.9 %collective-permute-start.10 = (bf16[528,128]{1,0:T(8,128)(2,1)S(1)}, bf16[528,128]{1,0:T(8,128)(2,1)S(1)}, u32[]{:S(2)}, u32[]{:S(2)}) collective-permute-start(bf16[528,128]{1,0:T(8,128)(2,1)S(1)} %get-tuple-element.84.mine), channel_id=1, source_target_pairs={{0,16},{8,24},{16,0},{24,8},{1,17},{9,25},{17,1},{25,9},{2,18},{10... | collective-permute-start | bytes 405512 | tf_op jit(solution)/shard_map/ppermute | solution.py:605
  26.9 4.0 %collective-permute-done.10.theirs = bf16[528,128]{1,0:T(8,128)(2,1)S(1)} collective-permute-done((bf16[528,128]{1,0:T(8,128)(2,1)S(1)}, bf16[528,128]{1,0:T(8,128)(2,1)S(1)}, u32[]{:S(2)}, u32[]{:S(2)}) %collective-permute-start.10) | collective-permute-done | bytes 135200 | tf_op jit(solution)/shard_map/ppermute | solution.py:605
  30.8 3.2 %collective-permute-start.12 = (bf16[528,256]{1,0:T(8,128)(2,1)S(1)}, bf16[528,256]{1,0:T(8,128)(2,1)S(1)}, u32[]{:S(2)}, u32[]{:S(2)}) collective-permute-start(bf16[528,256]{1,0:T(8,128)(2,1)S(1)} %collective-permute-done.9.b), channel_id=1, source_target_pairs={{0,224},{32,0},{64,32},{96,64},{128,96},{160,128},{192,160},{224,1... | collective-permute-start | bytes 811016 | tf_op jit(solution)/shard_map/ppermute | solution.py:609
  34.1 3.8 %first.1 = (bf16[1024,128]{1,0:T(8,128)(2,1)S(1)}, f32[1,1024]{1,0:T(1,128)S(1)}, f32[1,1024]{1,0:T(1,128)S(1)}, f32[1,1024]{1,0:T(1,128)S(1)}, f32[128,1024]{1,0:T(8,128)S(1)}) custom-call(bf16[528,128]{1,0:T(8,128)(2,1)S(1)} %get-tuple-element.84.mine, bf16[528,128]{1,0:T(8,128)(2,1)S(1)} %collective-permute-done.10.theirs, ...), custom_call_target="tpu_custom_call" | custom-call | flops 805306368 | bytes 2097152 | tf_op jit(solution)/shard_map/first/pallas_call | solution.py:223
  43.1 2.3 %pad_maximum_fusion.own = bf16[1056,2048]{1,0:T(8,128)(2,1)} fusion(bf16[352,2048]{1,0:T(8,128)(2,1)S(1)} %bitcast.29, bf16[352,2048]{1,0:T(8,128)(2,1)S(1)} %bitcast.30, bf16[352,2048]{1,0:T(8,128)(2,1)S(1)} %bitcast.31), kind=kLoop, calls=%fused_computation | loop fusion | flops 12976128 | bytes 8650752 | tf_op jit(solution)/shard_map/concatenate | solution.py:624
  45.6 2.5 %collective-permute-done.13.f = bf16[528,256]{1,0:T(8,128)(2,1)S(1)} collective-permute-done((bf16[528,256]{1,0:T(8,128)(2,1)S(1)}, bf16[528,256]{1,0:T(8,128)(2,1)S(1)}, u32[]{:S(2)}, u32[]{:S(2)}) %collective-permute-start.13) | collective-permute-done | bytes 270368 | tf_op jit(solution)/shard_map/ppermute | solution.py:609
  50.1 6.2 %collective-permute-done.15.kv = bf16[528,256]{1,0:T(8,128)(2,1)S(1)} collective-permute-done((bf16[528,256]{1,0:T(8,128)(2,1)S(1)}, bf16[528,256]{1,0:T(8,128)(2,1)S(1)}, u32[]{:S(2)}, u32[]{:S(2)}) %collective-permute-start.15) | collective-permute-done | bytes 270368 | tf_op jit(solution)/shard_map/ppermute | solution.py:633
  56.4 3.0 %collective-permute-start.16 = (bf16[144,512]{1,0:T(8,128)(2,1)S(1)}, bf16[144,512]{1,0:T(8,128)(2,1)S(1)}, u32[]{:S(2)}, u32[]{:S(2)}) collective-permute-start(bf16[144,512]{1,0:T(8,128)(2,1)S(1)} %get-tuple-element.117), channel_id=1, source_target_pairs={{0,16},{8,24},{16,0},{24,8},{1,17},{9,25},{17,1},{25,9},{2,18},{10... | collective-permute-start | bytes 442376 | tf_op jit(solution)/shard_map/ppermute | solution.py:605
  59.4 3.7 %collective-permute-done.16.b = bf16[144,512]{1,0:T(8,128)(2,1)S(1)} collective-permute-done((bf16[144,512]{1,0:T(8,128)(2,1)S(1)}, bf16[144,512]{1,0:T(8,128)(2,1)S(1)}, u32[]{:S(2)}, u32[]{:S(2)}) %collective-permute-start.16) | collective-permute-done | bytes 147488 | tf_op jit(solution)/shard_map/ppermute | solution.py:605
  77.1 3.8 %collective-permute-done.25.refs_5_ = bf16[256,256]{1,0:T(8,128)(2,1)S(1)} collective-permute-done((bf16[256,256]{1,0:T(8,128)(2,1)S(1)}, bf16[256,256]{1,0:T(8,128)(2,1)S(1)}, u32[]{:S(2)}, u32[]{:S(2)}) %collective-permute-start.25) | collective-permute-done | bytes 131104 | tf_op jit(solution)/shard_map/ppermute | solution.py:585
  81.2 20.6 %all_to_all.10 = bf16[16,32,256]{2,1,0:T(8,128)(2,1)S(1)} all-to-all(bf16[16,32,256]{2,1,0:T(8,128)(2,1)S(1)} %bitcast.25), channel_id=1, replica_groups=mesh['z'=8,'yh'=2,'c'=2,'x'=4,'yl'=2] {'z','yh'}, dimensions={0} | all-to-all | bytes 524288 | tf_op jit(solution)/shard_map/all_to_all | solution.py:653
  101.8 2.1 %collective-permute-start.31 = (bf16[512,256]{1,0:T(8,128)(2,1)S(1)}, bf16[512,256]{1,0:T(8,128)(2,1)S(1)}, u32[]{:S(2)}, u32[]{:S(2)}) collective-permute-start(bf16[512,256]{1,0:T(8,128)(2,1)S(1)} %bitcast.18), channel_id=1, source_target_pairs={{0,7},{1,6},{2,1},{3,0},{4,3},{5,2},{6,5},{7,4},{8,15},{9,14},{10,... | collective-permute-start | bytes 786440 | tf_op jit(solution)/shard_map/ppermute | solution.py:585
  107.4 3.8 %collective-permute-done.29.b1 = bf16[512,256]{1,0:T(8,128)(2,1)S(1)} collective-permute-done((bf16[512,256]{1,0:T(8,128)(2,1)S(1)}, bf16[512,256]{1,0:T(8,128)(2,1)S(1)}, u32[]{:S(2)}, u32[]{:S(2)}) %collective-permute-start.29) | collective-permute-done | bytes 262176 | tf_op jit(solution)/shard_map/ppermute | solution.py:585
  114.2 3.6 %expert_ready.1 = (bf16[1536,2048]{1,0:T(8,128)(2,1)S(1)}, bf16[768,2048]{1,0:T(8,128)(2,1)S(1)}, bf16[512,768]{1,0:T(8,128)(2,1)S(1)}, f32[512,1]{1,0:T(8,128)S(1)}) custom-call(bf16[512,256]{1,0:T(8,128)(2,1)S(1)} %bitcast.22, bf16[512,256]{1,0:T(8,128)(2,1)S(1)} %collective-permute-done.29.b1, bf16[512,256]{1,0:T(8,128)(2,1)S(1)} %collective-permute-done.31.b2, ...), custom_call_target="tpu_custom_call" | custom-call | flops 1048576 | bytes 18874368 | tf_op jit(solution)/shard_map/expert_ready/pallas_call | solution.py:477
  120.7 6.2 %expert_hidden.1 = (bf16[512,768]{1,0:T(8,128)(2,1)S(1)}, bf16[512,256]{1,0:T(8,128)(2,1)S(1)}, bf16[512,256]{1,0:T(8,128)(2,1)S(1)}, bf16[512,256]{1,0:T(8,128)(2,1)S(1)}) custom-call(bf16[512,256]{1,0:T(8,128)(2,1)S(1)} %collective-permute-done.26.refs_0_, bf16[512,256]{1,0:T(8,128)(2,1)S(1)} %collective-permute-done.27.refs_1_, ...), custom_call_target="tpu_custom_call" | custom-call | flops 4026531840 | bytes 13631488 | tf_op jit(solution)/shard_map/expert_hidden/pallas_call | solution.py:530
  130.9 2.4 %collective-permute-start.36 = (bf16[512,256]{1,0:T(8,128)(2,1)S(1)}, bf16[512,256]{1,0:T(8,128)(2,1)S(1)}, u32[]{:S(2)}, u32[]{:S(2)}) collective-permute-start(bf16[512,256]{1,0:T(8,128)(2,1)S(1)} %get-tuple-element.145), channel_id=1, source_target_pairs={{0,3},{1,2},{2,5},{3,4},{4,7},{5,6},{6,1},{7,0},{8,11},{9,10},{10,... | collective-permute-start | bytes 786440 | tf_op jit(solution)/shard_map/ppermute | solution.py:585
  135.6 8.2 %collective-permute-done.35.refs_1_ = bf16[512,256]{1,0:T(8,128)(2,1)S(1)} collective-permute-done((bf16[512,256]{1,0:T(8,128)(2,1)S(1)}, bf16[512,256]{1,0:T(8,128)(2,1)S(1)}, u32[]{:S(2)}, u32[]{:S(2)}) %collective-permute-start.35) | collective-permute-done | bytes 262176 | tf_op jit(solution)/shard_map/ppermute | solution.py:585
  145.4 5.0 %collective-permute-done.38.refs_4_ = bf16[512,256]{1,0:T(8,128)(2,1)S(1)} collective-permute-done((bf16[512,256]{1,0:T(8,128)(2,1)S(1)}, bf16[512,256]{1,0:T(8,128)(2,1)S(1)}, u32[]{:S(2)}, u32[]{:S(2)}) %collective-permute-start.38) | collective-permute-done | bytes 262176 | tf_op jit(solution)/shard_map/ppermute | solution.py:585
  150.4 4.5 %collective-permute-done.39.refs_5_ = bf16[512,256]{1,0:T(8,128)(2,1)S(1)} collective-permute-done((bf16[512,256]{1,0:T(8,128)(2,1)S(1)}, bf16[512,256]{1,0:T(8,128)(2,1)S(1)}, u32[]{:S(2)}, u32[]{:S(2)}) %collective-permute-start.39) | collective-permute-done | bytes 262176 | tf_op jit(solution)/shard_map/ppermute | solution.py:585
  155.1 14.9 %all_to_all.11 = bf16[16,32,256]{2,1,0:T(8,128)(2,1)S(1)} all-to-all(bf16[16,32,256]{2,1,0:T(8,128)(2,1)S(1)} %bitcast.23), channel_id=1, replica_groups=mesh['z'=8,'yh'=2,'c'=2,'x'=4,'yl'=2] {'z','yh'}, dimensions={0} | all-to-all | bytes 524288 | tf_op jit(solution)/shard_map/all_to_all | solution.py:659
  (96 shorter events, 52.0 us)
Async XLA Ops:
  2.2 8.4 %collective-permute-start.1 = (bf16[256,256]{1,0:T(8,128)(2,1)}, bf16[256,256]{1,0:T(8,128)(2,1)S(1)}, u32[]{:S(2)}, u32[]{:S(2)}) collective-permute-start(bf16[256,256]{1,0:T(8,128)(2,1)} %refs_6_.1), channel_id=1, source_target_pairs={{0,7},{1,6},{2,1},{3,0},{4,3},{5,2},{6,5},{7,4},{8,15},{9,14},{10,... | collective-permute-start | bytes 393224 | tf_op jit(solution)/shard_map/ppermute | solution.py:585
  3.0 10.2 %collective-permute-start.2 = (bf16[256,256]{1,0:T(8,128)(2,1)}, bf16[256,256]{1,0:T(8,128)(2,1)S(1)}, u32[]{:S(2)}, u32[]{:S(2)}) collective-permute-start(bf16[256,256]{1,0:T(8,128)(2,1)} %refs_6_.1), channel_id=1, source_target_pairs={{0,1},{1,0},{2,3},{3,2},{4,5},{5,4},{6,7},{7,6},{8,9},{9,8},{10,11... | collective-permute-start | bytes 393224 | tf_op jit(solution)/shard_map/ppermute | solution.py:585
  3.5 9.8 %collective-permute-start.3 = (bf16[256,256]{1,0:T(8,128)(2,1)}, bf16[256,256]{1,0:T(8,128)(2,1)S(1)}, u32[]{:S(2)}, u32[]{:S(2)}) collective-permute-start(bf16[256,256]{1,0:T(8,128)(2,1)} %refs_6_.1), channel_id=1, source_target_pairs={{0,3},{1,2},{2,5},{3,4},{4,7},{5,6},{6,1},{7,0},{8,11},{9,10},{10,... | collective-permute-start | bytes 393224 | tf_op jit(solution)/shard_map/ppermute | solution.py:585
  6.4 7.7 %collective-permute-start.4 = (bf16[256,256]{1,0:T(8,128)(2,1)}, bf16[256,256]{1,0:T(8,128)(2,1)S(1)}, u32[]{:S(2)}, u32[]{:S(2)}) collective-permute-start(bf16[256,256]{1,0:T(8,128)(2,1)} %refs_6_.1), channel_id=1, source_target_pairs={{0,6},{1,7},{2,0},{3,1},{4,2},{5,3},{6,4},{7,5},{8,14},{9,15},{10,... | collective-permute-start | bytes 393224 | tf_op jit(solution)/shard_map/ppermute | solution.py:585
  6.5 8.7 %collective-permute-start.5 = (bf16[256,256]{1,0:T(8,128)(2,1)S(1)}, bf16[256,256]{1,0:T(8,128)(2,1)S(1)}, u32[]{:S(2)}, u32[]{:S(2)}) collective-permute-start(bf16[256,256]{1,0:T(8,128)(2,1)S(1)} %collective-permute-done.refs_1_), channel_id=1, source_target_pairs={{0,2},{1,3},{2,4},{3,5},{4,6},{5,7},{6,0},{7,1},{8,10},{9,11},{10,... | collective-permute-start | bytes 393224 | tf_op jit(solution)/shard_map/ppermute | solution.py:585
  19.1 11.7 %collective-permute-start.8 = (bf16[528,256]{1,0:T(8,128)(2,1)S(1)}, bf16[528,256]{1,0:T(8,128)(2,1)S(1)}, u32[]{:S(2)}, u32[]{:S(2)}) collective-permute-start(bf16[528,256]{1,0:T(8,128)(2,1)S(1)} %get-tuple-element.83.own), channel_id=1, source_target_pairs={{0,32},{32,64},{64,96},{96,128},{128,160},{160,192},{192,224},{224... | collective-permute-start | bytes 811016 | tf_op jit(solution)/shard_map/ppermute | solution.py:609
  19.9 10.9 %collective-permute-start.9 = (bf16[528,256]{1,0:T(8,128)(2,1)S(1)}, bf16[528,256]{1,0:T(8,128)(2,1)S(1)}, u32[]{:S(2)}, u32[]{:S(2)}) collective-permute-start(bf16[528,256]{1,0:T(8,128)(2,1)S(1)} %get-tuple-element.83.own), channel_id=1, source_target_pairs={{0,224},{32,0},{64,32},{96,64},{128,96},{160,128},{192,160},{224,1... | collective-permute-start | bytes 811016 | tf_op jit(solution)/shard_map/ppermute | solution.py:609
  30.8 9.1 %collective-permute-start.11 = (bf16[528,256]{1,0:T(8,128)(2,1)S(1)}, bf16[528,256]{1,0:T(8,128)(2,1)S(1)}, u32[]{:S(2)}, u32[]{:S(2)}) collective-permute-start(bf16[528,256]{1,0:T(8,128)(2,1)S(1)} %collective-permute-done.8.f), channel_id=1, source_target_pairs={{0,32},{32,64},{64,96},{96,128},{128,160},{160,192},{192,224},{224... | collective-permute-start | bytes 811016 | tf_op jit(solution)/shard_map/ppermute | solution.py:609
  30.8 9.1 %collective-permute-start.12 = (bf16[528,256]{1,0:T(8,128)(2,1)S(1)}, bf16[528,256]{1,0:T(8,128)(2,1)S(1)}, u32[]{:S(2)}, u32[]{:S(2)}) collective-permute-start(bf16[528,256]{1,0:T(8,128)(2,1)S(1)} %collective-permute-done.9.b), channel_id=1, source_target_pairs={{0,224},{32,0},{64,32},{96,64},{128,96},{160,128},{192,160},{224,1... | collective-permute-start | bytes 811016 | tf_op jit(solution)/shard_map/ppermute | solution.py:609
  39.9 8.1 %collective-permute-start.13 = (bf16[528,256]{1,0:T(8,128)(2,1)S(1)}, bf16[528,256]{1,0:T(8,128)(2,1)S(1)}, u32[]{:S(2)}, u32[]{:S(2)}) collective-permute-start(bf16[528,256]{1,0:T(8,128)(2,1)S(1)} %collective-permute-done.11.f), channel_id=1, source_target_pairs={{0,32},{32,64},{64,96},{96,128},{128,160},{160,192},{192,224},{224... | collective-permute-start | bytes 811016 | tf_op jit(solution)/shard_map/ppermute | solution.py:609
  48.2 14.9 %collective-permute-start.17 = (bf16[1056,2048]{1,0:T(8,128)(2,1)}, bf16[1056,2048]{1,0:T(8,128)(2,1)}, u32[]{:S(2)}, u32[]{:S(2)}) collective-permute-start(bf16[1056,2048]{1,0:T(8,128)(2,1)} %pad_maximum_fusion.own), channel_id=1, source_target_pairs={{0,8},{8,0},{1,9},{9,1},{2,10},{10,2},{3,11},{11,3},{4,12},{12,4},... | collective-permute-start | bytes 12976136 | tf_op jit(solution)/shard_map/ppermute | solution.py:635
  48.2 8.1 %collective-permute-start.15 = (bf16[528,256]{1,0:T(8,128)(2,1)S(1)}, bf16[528,256]{1,0:T(8,128)(2,1)S(1)}, u32[]{:S(2)}, u32[]{:S(2)}) collective-permute-start(bf16[528,256]{1,0:T(8,128)(2,1)S(1)} %broadcast_select_fusion), channel_id=1, source_target_pairs={{0,32},{8,232},{32,64},{40,8},{64,96},{72,40},{96,128},{104,72},{1... | collective-permute-start | bytes 811016 | tf_op jit(solution)/shard_map/ppermute | solution.py:633
  67.3 7.9 %collective-permute-start.19 = (bf16[256,256]{1,0:T(8,128)(2,1)S(1)}, bf16[256,256]{1,0:T(8,128)(2,1)S(1)}, u32[]{:S(2)}, u32[]{:S(2)}) collective-permute-start(bf16[256,256]{1,0:T(8,128)(2,1)S(1)} %get-tuple-element.123), channel_id=1, source_target_pairs={{0,1},{1,0},{2,3},{3,2},{4,5},{5,4},{6,7},{7,6},{8,9},{9,8},{10,11... | collective-permute-start | bytes 393224 | tf_op jit(solution)/shard_map/ppermute | solution.py:585
  101.8 9.4 %collective-permute-start.29 = (bf16[512,256]{1,0:T(8,128)(2,1)S(1)}, bf16[512,256]{1,0:T(8,128)(2,1)S(1)}, u32[]{:S(2)}, u32[]{:S(2)}) collective-permute-start(bf16[512,256]{1,0:T(8,128)(2,1)S(1)} %bitcast.17), channel_id=1, source_target_pairs={{0,2},{1,3},{2,4},{3,5},{4,6},{5,7},{6,0},{7,1},{8,10},{9,11},{10,... | collective-permute-start | bytes 786440 | tf_op jit(solution)/shard_map/ppermute | solution.py:585
  101.8 11.3 %collective-permute-start.31 = (bf16[512,256]{1,0:T(8,128)(2,1)S(1)}, bf16[512,256]{1,0:T(8,128)(2,1)S(1)}, u32[]{:S(2)}, u32[]{:S(2)}) collective-permute-start(bf16[512,256]{1,0:T(8,128)(2,1)S(1)} %bitcast.18), channel_id=1, source_target_pairs={{0,7},{1,6},{2,1},{3,0},{4,3},{5,2},{6,5},{7,4},{8,15},{9,14},{10,... | collective-permute-start | bytes 786440 | tf_op jit(solution)/shard_map/ppermute | solution.py:585
  103.9 14.9 %collective-permute-start.26 = (bf16[512,256]{1,0:T(8,128)(2,1)S(1)}, bf16[512,256]{1,0:T(8,128)(2,1)S(1)}, u32[]{:S(2)}, u32[]{:S(2)}) collective-permute-start(bf16[512,256]{1,0:T(8,128)(2,1)S(1)} %bitcast.19), channel_id=1, source_target_pairs={{0,1},{1,0},{2,3},{3,2},{4,5},{5,4},{6,7},{7,6},{8,9},{9,8},{10,11... | collective-permute-start | bytes 786440 | tf_op jit(solution)/shard_map/ppermute | solution.py:585
  105.3 13.5 %collective-permute-start.27 = (bf16[512,256]{1,0:T(8,128)(2,1)S(1)}, bf16[512,256]{1,0:T(8,128)(2,1)S(1)}, u32[]{:S(2)}, u32[]{:S(2)}) collective-permute-start(bf16[512,256]{1,0:T(8,128)(2,1)S(1)} %bitcast.20), channel_id=1, source_target_pairs={{0,3},{1,2},{2,5},{3,4},{4,7},{5,6},{6,1},{7,0},{8,11},{9,10},{10,... | collective-permute-start | bytes 786440 | tf_op jit(solution)/shard_map/ppermute | solution.py:585
  106.6 12.2 %collective-permute-start.28 = (bf16[512,256]{1,0:T(8,128)(2,1)S(1)}, bf16[512,256]{1,0:T(8,128)(2,1)S(1)}, u32[]{:S(2)}, u32[]{:S(2)}) collective-permute-start(bf16[512,256]{1,0:T(8,128)(2,1)S(1)} %bitcast.21), channel_id=1, source_target_pairs={{0,6},{1,7},{2,0},{3,1},{4,2},{5,3},{6,4},{7,5},{8,14},{9,15},{10,... | collective-permute-start | bytes 786440 | tf_op jit(solution)/shard_map/ppermute | solution.py:585
  127.0 8.7 %collective-permute-start.33 = (bf16[512,256]{1,0:T(8,128)(2,1)S(1)}, bf16[512,256]{1,0:T(8,128)(2,1)S(1)}, u32[]{:S(2)}, u32[]{:S(2)}) collective-permute-start(bf16[512,256]{1,0:T(8,128)(2,1)S(1)} %get-tuple-element.141), channel_id=1, source_target_pairs={{0,2},{1,3},{2,4},{3,5},{4,6},{5,7},{6,0},{7,1},{8,10},{9,11},{10,... | collective-permute-start | bytes 786440 | tf_op jit(solution)/shard_map/ppermute | solution.py:585
  127.0 8.6 %collective-permute-start.34 = (bf16[512,256]{1,0:T(8,128)(2,1)S(1)}, bf16[512,256]{1,0:T(8,128)(2,1)S(1)}, u32[]{:S(2)}, u32[]{:S(2)}) collective-permute-start(bf16[512,256]{1,0:T(8,128)(2,1)S(1)} %get-tuple-element.142), channel_id=1, source_target_pairs={{0,6},{1,7},{2,0},{3,1},{4,2},{5,3},{6,4},{7,5},{8,14},{9,15},{10,... | collective-permute-start | bytes 786440 | tf_op jit(solution)/shard_map/ppermute | solution.py:585
  129.1 14.7 %collective-permute-start.35 = (bf16[512,256]{1,0:T(8,128)(2,1)S(1)}, bf16[512,256]{1,0:T(8,128)(2,1)S(1)}, u32[]{:S(2)}, u32[]{:S(2)}) collective-permute-start(bf16[512,256]{1,0:T(8,128)(2,1)S(1)} %get-tuple-element.143), channel_id=1, source_target_pairs={{0,1},{1,0},{2,3},{3,2},{4,5},{5,4},{6,7},{7,6},{8,9},{9,8},{10,11... | collective-permute-start | bytes 786440 | tf_op jit(solution)/shard_map/ppermute | solution.py:585
  130.9 14.4 %collective-permute-start.36 = (bf16[512,256]{1,0:T(8,128)(2,1)S(1)}, bf16[512,256]{1,0:T(8,128)(2,1)S(1)}, u32[]{:S(2)}, u32[]{:S(2)}) collective-permute-start(bf16[512,256]{1,0:T(8,128)(2,1)S(1)} %get-tuple-element.145), channel_id=1, source_target_pairs={{0,3},{1,2},{2,5},{3,4},{4,7},{5,6},{6,1},{7,0},{8,11},{9,10},{10,... | collective-permute-start | bytes 786440 | tf_op jit(solution)/shard_map/ppermute | solution.py:585
  133.3 12.0 %collective-permute-start.37 = (bf16[512,256]{1,0:T(8,128)(2,1)S(1)}, bf16[512,256]{1,0:T(8,128)(2,1)S(1)}, u32[]{:S(2)}, u32[]{:S(2)}) collective-permute-start(bf16[512,256]{1,0:T(8,128)(2,1)S(1)} %get-tuple-element.146), channel_id=1, source_target_pairs={{0,6},{1,7},{2,0},{3,1},{4,2},{5,3},{6,4},{7,5},{8,14},{9,15},{10,... | collective-permute-start | bytes 786440 | tf_op jit(solution)/shard_map/ppermute | solution.py:585
  145.4 9.5 %collective-permute-start.39 = (bf16[512,256]{1,0:T(8,128)(2,1)S(1)}, bf16[512,256]{1,0:T(8,128)(2,1)S(1)}, u32[]{:S(2)}, u32[]{:S(2)}) collective-permute-start(bf16[512,256]{1,0:T(8,128)(2,1)S(1)} %get-tuple-element.152), channel_id=1, source_target_pairs={{0,7},{1,6},{2,1},{3,0},{4,3},{5,2},{6,5},{7,4},{8,15},{9,14},{10,... | collective-permute-start | bytes 786440 | tf_op jit(solution)/shard_map/ppermute | solution.py:585
  (24 other events, 326.4 us)

commit v4 on v3

--- a/solution.py
+++ b/solution.py
@@ -18,7 +18,7 @@
 SEQ = ("z", "yh", "c")
 CHIPS = ("z", "yh")
 TP = ("x", "yl")
-NEAR = ((0, 0), (1, 0), (3, 1), (0, 1), (1, 1), (3, 0))
+NEAR = ((0, 0), (1, 0), (3, 1), (0, 1), (3, 0), (1, 1))
 FAR = ((2, 0), (2, 1))
 F32 = jnp.float32
 BF16 = jnp.bfloat16
@@ -615,14 +615,12 @@
     kv, q = join(own, swap(other, 0, 1))
     f, b = ring(kv, 1), ring(kv, -1)
     theirs = swap(q, 1, 0)
-    f, b, theirs = lax.optimization_barrier((f, b, theirs))
+    weights, kv = lax.optimization_barrier((weights, kv))
+    weights = jnp.concatenate(weights, axis=0)
+    f, b, theirs, weights = lax.optimization_barrier((f, b, theirs, weights))
     state = None
     for k in range(1, 4):
-        if k == 2:
-            f, b, *held = lax.optimization_barrier((f, b, *state, *weights))
-            state, weights = held[:5], held[5:]
-            weights = jnp.concatenate(weights, axis=0)
-        if k == 3:
+        if k > 1:
             f, b, weights, *state = lax.optimization_barrier((f, b, weights, *state))
         here = f, b
         if k < 3:

time: 171 us -> 170 us (level)
  waiting for transfers between devices: 59.3 us -> 52.4 us
  starting transfers between devices: 52 us -> 57.8 us
    ppermute x28, waiting for transfers between devices: 38.2 us -> 32.6 us  [tp_shift(): return lax.ppermute(a, TP, pairs)]
    ppermute x28, starting transfers between devices: 32.7 us -> 38.2 us  [tp_shift(): return lax.ppermute(a, TP, pairs)]
    ppermute x4, waiting for transfers between devices: 10.4 us -> 7.21 us  [swap(): return lax.ppermute(a, ('yh', 'c'), pairs)]
    ppermute x6, waiting for transfers between devices: 4.62 us -> 6.83 us  [ring(): return lax.ppermute(a, 'z', [(i, (i + step) % 8) for i in range(8)])]
  transfers between devices with their start and end apart: 40 -> 40, of which waited for: 25 -> 22; matrix products, arithmetic and copies ran while one was open for 3% -> 3% of each run, Pallas kernels for 6% -> 6%
where the time goes in v4:
time: 170 us
  starting transfers between devices  57.8 us (34%)
  waiting for transfers between devices  52.4 us (31%)
  blocking collectives  35.7 us (21%)
  Pallas kernels  19.4 us (11%)
  other arithmetic  4.52 us (3%)
    ppermute x28, starting transfers between devices, tp_shift(): return lax.ppermute(a, TP, pairs)  38.2 us
    ppermute x28, waiting for transfers between devices, tp_shift(): return lax.ppermute(a, TP, pairs)  32.6 us
    all_to_all x1, blocking collectives, shards(): lax.all_to_all(rows.reshape(EXPERTS, CAP, BLK), CHIPS, 0, 0, tiled=True)  20.9 us
    all_to_all x1, blocking collectives, shards(): lax.all_to_all(summed.reshape(EXPERTS, CAP, BLK), CHIPS, 0, 0, tiled=True)  14.8 us
    ppermute x6, starting transfers between devices, ring(): return lax.ppermute(a, 'z', [(i, (i + step) % 8) for i in range(8)])  10.8 us
    ppermute x4, waiting for transfers between devices, swap(): return lax.ppermute(a, ('yh', 'c'), pairs)  7.21 us
    ppermute x4, starting transfers between devices, swap(): return lax.ppermute(a, ('yh', 'c'), pairs)  7.05 us
    ppermute x6, waiting for transfers between devices, ring(): return lax.ppermute(a, 'z', [(i, (i + step) % 8) for i in range(8)])  6.83 us
  transfers between devices with their start and end apart: 40, of which 22 were waited for; matrix products, arithmetic and copies ran while one was open for 3% of the time, Pallas kernels for 6%

profile of v4, /device:TPU:6, one launch (start us, length us, event | category | flops | bytes accessed | tf_op | source)
XLA Modules:
  0.0 170.2 jit_solution(16495127257617911988)
XLA Ops:
  4.3 3.4 %collective-permute-start.4 = (bf16[256,256]{1,0:T(8,128)(2,1)}, bf16[256,256]{1,0:T(8,128)(2,1)S(1)}, u32[]{:S(2)}, u32[]{:S(2)}) collective-permute-start(bf16[256,256]{1,0:T(8,128)(2,1)} %refs_6_.1), channel_id=1, source_target_pairs={{0,3},{1,2},{2,5},{3,4},{4,7},{5,6},{6,1},{7,0},{8,11},{9,10},{10,... | collective-permute-start | bytes 393224 | tf_op jit(solution)/shard_map/ppermute | solution.py:585
  14.5 2.3 %collective-permute-done.6.b1 = bf16[256,256]{1,0:T(8,128)(2,1)S(1)} collective-permute-done((bf16[256,256]{1,0:T(8,128)(2,1)S(1)}, bf16[256,256]{1,0:T(8,128)(2,1)S(1)}, u32[]{:S(2)}, u32[]{:S(2)}) %collective-permute-start.6) | collective-permute-done | bytes 131104 | tf_op jit(solution)/shard_map/ppermute | solution.py:585
  19.4 4.0 %collective-permute-start.9 = (bf16[528,256]{1,0:T(8,128)(2,1)S(1)}, bf16[528,256]{1,0:T(8,128)(2,1)S(1)}, u32[]{:S(2)}, u32[]{:S(2)}) collective-permute-start(bf16[528,256]{1,0:T(8,128)(2,1)S(1)} %get-tuple-element.95.own), channel_id=1, source_target_pairs={{0,224},{32,0},{64,32},{96,64},{128,96},{160,128},{192,160},{224,1... | collective-permute-start | bytes 811016 | tf_op jit(solution)/shard_map/ppermute | solution.py:609
  23.5 3.4 %collective-permute-start.10 = (bf16[528,128]{1,0:T(8,128)(2,1)S(1)}, bf16[528,128]{1,0:T(8,128)(2,1)S(1)}, u32[]{:S(2)}, u32[]{:S(2)}) collective-permute-start(bf16[528,128]{1,0:T(8,128)(2,1)S(1)} %get-tuple-element.87.mine), channel_id=1, source_target_pairs={{0,16},{8,24},{16,0},{24,8},{1,17},{9,25},{17,1},{25,9},{2,18},{10... | collective-permute-start | bytes 405512 | tf_op jit(solution)/shard_map/ppermute | solution.py:605
  26.9 2.3 %pad_maximum_fusion.own = bf16[1056,2048]{1,0:T(8,128)(2,1)} fusion(bf16[352,2048]{1,0:T(8,128)(2,1)S(1)} %bitcast.29, bf16[352,2048]{1,0:T(8,128)(2,1)S(1)} %bitcast.30, bf16[352,2048]{1,0:T(8,128)(2,1)S(1)} %bitcast.31), kind=kLoop, calls=%fused_computation | loop fusion | flops 12976128 | bytes 8650752 | tf_op jit(solution)/shard_map/concatenate | solution.py:619
  30.5 3.2 %collective-permute-start.12 = (bf16[528,256]{1,0:T(8,128)(2,1)S(1)}, bf16[528,256]{1,0:T(8,128)(2,1)S(1)}, u32[]{:S(2)}, u32[]{:S(2)}) collective-permute-start(bf16[528,256]{1,0:T(8,128)(2,1)S(1)} %collective-permute-done.9.b), channel_id=1, source_target_pairs={{0,224},{32,0},{64,32},{96,64},{128,96},{160,128},{192,160},{224,1... | collective-permute-start | bytes 811016 | tf_op jit(solution)/shard_map/ppermute | solution.py:609
  33.7 3.8 %first.1 = (bf16[1024,128]{1,0:T(8,128)(2,1)S(1)}, f32[1,1024]{1,0:T(1,128)S(1)}, f32[1,1024]{1,0:T(1,128)S(1)}, f32[1,1024]{1,0:T(1,128)S(1)}, f32[128,1024]{1,0:T(8,128)S(1)}) custom-call(bf16[528,128]{1,0:T(8,128)(2,1)S(1)} %get-tuple-element.87.mine, bf16[528,128]{1,0:T(8,128)(2,1)S(1)} %collective-permute-done.10.theirs, ...), custom_call_target="tpu_custom_call" | custom-call | flops 805306368 | bytes 2097152 | tf_op jit(solution)/shard_map/first/pallas_call | solution.py:223
  42.7 4.7 %collective-permute-done.13.f = bf16[528,256]{1,0:T(8,128)(2,1)S(1)} collective-permute-done((bf16[528,256]{1,0:T(8,128)(2,1)S(1)}, bf16[528,256]{1,0:T(8,128)(2,1)S(1)}, u32[]{:S(2)}, u32[]{:S(2)}) %collective-permute-start.13) | collective-permute-done | bytes 270368 | tf_op jit(solution)/shard_map/ppermute | solution.py:609
  49.6 5.8 %collective-permute-done.15.kv = bf16[528,256]{1,0:T(8,128)(2,1)S(1)} collective-permute-done((bf16[528,256]{1,0:T(8,128)(2,1)S(1)}, bf16[528,256]{1,0:T(8,128)(2,1)S(1)}, u32[]{:S(2)}, u32[]{:S(2)}) %collective-permute-start.15) | collective-permute-done | bytes 270368 | tf_op jit(solution)/shard_map/ppermute | solution.py:631
  55.6 3.5 %collective-permute-start.16 = (bf16[144,512]{1,0:T(8,128)(2,1)S(1)}, bf16[144,512]{1,0:T(8,128)(2,1)S(1)}, u32[]{:S(2)}, u32[]{:S(2)}) collective-permute-start(bf16[144,512]{1,0:T(8,128)(2,1)S(1)} %get-tuple-element.123), channel_id=1, source_target_pairs={{0,16},{8,24},{16,0},{24,8},{1,17},{9,25},{17,1},{25,9},{2,18},{10... | collective-permute-start | bytes 442376 | tf_op jit(solution)/shard_map/ppermute | solution.py:605
  59.0 3.3 %collective-permute-done.16.b = bf16[144,512]{1,0:T(8,128)(2,1)S(1)} collective-permute-done((bf16[144,512]{1,0:T(8,128)(2,1)S(1)}, bf16[144,512]{1,0:T(8,128)(2,1)S(1)}, u32[]{:S(2)}, u32[]{:S(2)}) %collective-permute-start.16) | collective-permute-done | bytes 147488 | tf_op jit(solution)/shard_map/ppermute | solution.py:605
  68.7 2.8 %collective-permute-start.21 = (bf16[256,256]{1,0:T(8,128)(2,1)S(1)}, bf16[256,256]{1,0:T(8,128)(2,1)S(1)}, u32[]{:S(2)}, u32[]{:S(2)}) collective-permute-start(bf16[256,256]{1,0:T(8,128)(2,1)S(1)} %get-tuple-element.131), channel_id=1, source_target_pairs={{0,3},{1,2},{2,5},{3,4},{4,7},{5,6},{6,1},{7,0},{8,11},{9,10},{10,... | collective-permute-start | bytes 393224 | tf_op jit(solution)/shard_map/ppermute | solution.py:585
  72.4 3.5 %collective-permute-start.25 = (bf16[256,256]{1,0:T(8,128)(2,1)S(1)}, bf16[256,256]{1,0:T(8,128)(2,1)S(1)}, u32[]{:S(2)}, u32[]{:S(2)}) collective-permute-start(bf16[256,256]{1,0:T(8,128)(2,1)S(1)} %get-tuple-element.137), channel_id=1, source_target_pairs={{0,7},{1,6},{2,1},{3,0},{4,3},{5,2},{6,5},{7,4},{8,15},{9,14},{10,... | collective-permute-start | bytes 393224 | tf_op jit(solution)/shard_map/ppermute | solution.py:585
  76.9 2.6 %collective-permute-done.25.refs_5_ = bf16[256,256]{1,0:T(8,128)(2,1)S(1)} collective-permute-done((bf16[256,256]{1,0:T(8,128)(2,1)S(1)}, bf16[256,256]{1,0:T(8,128)(2,1)S(1)}, u32[]{:S(2)}, u32[]{:S(2)}) %collective-permute-start.25) | collective-permute-done | bytes 131104 | tf_op jit(solution)/shard_map/ppermute | solution.py:585
  79.8 20.9 %all_to_all.10 = bf16[16,32,256]{2,1,0:T(8,128)(2,1)S(1)} all-to-all(bf16[16,32,256]{2,1,0:T(8,128)(2,1)S(1)} %bitcast.25), channel_id=1, replica_groups=mesh['z'=8,'yh'=2,'c'=2,'x'=4,'yl'=2] {'z','yh'}, dimensions={0} | all-to-all | bytes 524288 | tf_op jit(solution)/shard_map/all_to_all | solution.py:651
  104.6 3.4 %collective-permute-start.28 = (bf16[512,256]{1,0:T(8,128)(2,1)S(1)}, bf16[512,256]{1,0:T(8,128)(2,1)S(1)}, u32[]{:S(2)}, u32[]{:S(2)}) collective-permute-start(bf16[512,256]{1,0:T(8,128)(2,1)S(1)} %bitcast.21), channel_id=1, source_target_pairs={{0,3},{1,2},{2,5},{3,4},{4,7},{5,6},{6,1},{7,0},{8,11},{9,10},{10,... | collective-permute-start | bytes 786440 | tf_op jit(solution)/shard_map/ppermute | solution.py:585
  108.0 2.6 %collective-permute-done.29.b1 = bf16[512,256]{1,0:T(8,128)(2,1)S(1)} collective-permute-done((bf16[512,256]{1,0:T(8,128)(2,1)S(1)}, bf16[512,256]{1,0:T(8,128)(2,1)S(1)}, u32[]{:S(2)}, u32[]{:S(2)}) %collective-permute-start.29) | collective-permute-done | bytes 262176 | tf_op jit(solution)/shard_map/ppermute | solution.py:585
  112.7 3.6 %expert_ready.1 = (bf16[1536,2048]{1,0:T(8,128)(2,1)S(1)}, bf16[768,2048]{1,0:T(8,128)(2,1)S(1)}, bf16[512,768]{1,0:T(8,128)(2,1)S(1)}, f32[512,1]{1,0:T(8,128)S(1)}) custom-call(bf16[512,256]{1,0:T(8,128)(2,1)S(1)} %bitcast.22, bf16[512,256]{1,0:T(8,128)(2,1)S(1)} %collective-permute-done.29.b1, bf16[512,256]{1,0:T(8,128)(2,1)S(1)} %collective-permute-done.31.b2, ...), custom_call_target="tpu_custom_call" | custom-call | flops 1048576 | bytes 18874368 | tf_op jit(solution)/shard_map/expert_ready/pallas_call | solution.py:477
  120.3 6.2 %expert_hidden.1 = (bf16[512,768]{1,0:T(8,128)(2,1)S(1)}, bf16[512,256]{1,0:T(8,128)(2,1)S(1)}, bf16[512,256]{1,0:T(8,128)(2,1)S(1)}, bf16[512,256]{1,0:T(8,128)(2,1)S(1)}) custom-call(bf16[512,256]{1,0:T(8,128)(2,1)S(1)} %collective-permute-done.26.refs_0_, bf16[512,256]{1,0:T(8,128)(2,1)S(1)} %collective-permute-done.27.refs_1_, ...), custom_call_target="tpu_custom_call" | custom-call | flops 4026531840 | bytes 13631488 | tf_op jit(solution)/shard_map/expert_hidden/pallas_call | solution.py:530
  130.3 4.5 %collective-permute-start.37 = (bf16[512,256]{1,0:T(8,128)(2,1)S(1)}, bf16[512,256]{1,0:T(8,128)(2,1)S(1)}, u32[]{:S(2)}, u32[]{:S(2)}) collective-permute-start(bf16[512,256]{1,0:T(8,128)(2,1)S(1)} %get-tuple-element.152), channel_id=1, source_target_pairs={{0,3},{1,2},{2,5},{3,4},{4,7},{5,6},{6,1},{7,0},{8,11},{9,10},{10,... | collective-permute-start | bytes 786440 | tf_op jit(solution)/shard_map/ppermute | solution.py:585
  137.1 5.7 %collective-permute-done.35.refs_1_ = bf16[512,256]{1,0:T(8,128)(2,1)S(1)} collective-permute-done((bf16[512,256]{1,0:T(8,128)(2,1)S(1)}, bf16[512,256]{1,0:T(8,128)(2,1)S(1)}, u32[]{:S(2)}, u32[]{:S(2)}) %collective-permute-start.35) | collective-permute-done | bytes 262176 | tf_op jit(solution)/shard_map/ppermute | solution.py:585
  145.2 4.2 %collective-permute-done.38.refs_4_ = bf16[512,256]{1,0:T(8,128)(2,1)S(1)} collective-permute-done((bf16[512,256]{1,0:T(8,128)(2,1)S(1)}, bf16[512,256]{1,0:T(8,128)(2,1)S(1)}, u32[]{:S(2)}, u32[]{:S(2)}) %collective-permute-start.38) | collective-permute-done | bytes 262176 | tf_op jit(solution)/shard_map/ppermute | solution.py:585
  149.4 4.8 %collective-permute-done.39.refs_5_ = bf16[512,256]{1,0:T(8,128)(2,1)S(1)} collective-permute-done((bf16[512,256]{1,0:T(8,128)(2,1)S(1)}, bf16[512,256]{1,0:T(8,128)(2,1)S(1)}, u32[]{:S(2)}, u32[]{:S(2)}) %collective-permute-start.39) | collective-permute-done | bytes 262176 | tf_op jit(solution)/shard_map/ppermute | solution.py:585
  154.4 14.8 %all_to_all.11 = bf16[16,32,256]{2,1,0:T(8,128)(2,1)S(1)} all-to-all(bf16[16,32,256]{2,1,0:T(8,128)(2,1)S(1)} %bitcast.23), channel_id=1, replica_groups=mesh['z'=8,'yh'=2,'c'=2,'x'=4,'yl'=2] {'z','yh'}, dimensions={0} | all-to-all | bytes 524288 | tf_op jit(solution)/shard_map/all_to_all | solution.py:657
  (96 shorter events, 50.5 us)
Async XLA Ops:
  0.0 7.7 %collective-permute-start = (bf16[256,256]{1,0:T(8,128)(2,1)}, bf16[256,256]{1,0:T(8,128)(2,1)S(1)}, u32[]{:S(2)}, u32[]{:S(2)}) collective-permute-start(bf16[256,256]{1,0:T(8,128)(2,1)} %refs_6_.1), channel_id=1, source_target_pairs={{0,2},{1,3},{2,4},{3,5},{4,6},{5,7},{6,0},{7,1},{8,10},{9,11},{10,... | collective-permute-start | bytes 393224 | tf_op jit(solution)/shard_map/ppermute | solution.py:585
  2.2 8.4 %collective-permute-start.1 = (bf16[256,256]{1,0:T(8,128)(2,1)}, bf16[256,256]{1,0:T(8,128)(2,1)S(1)}, u32[]{:S(2)}, u32[]{:S(2)}) collective-permute-start(bf16[256,256]{1,0:T(8,128)(2,1)} %refs_6_.1), channel_id=1, source_target_pairs={{0,7},{1,6},{2,1},{3,0},{4,3},{5,2},{6,5},{7,4},{8,15},{9,14},{10,... | collective-permute-start | bytes 393224 | tf_op jit(solution)/shard_map/ppermute | solution.py:585
  3.0 10.2 %collective-permute-start.2 = (bf16[256,256]{1,0:T(8,128)(2,1)}, bf16[256,256]{1,0:T(8,128)(2,1)S(1)}, u32[]{:S(2)}, u32[]{:S(2)}) collective-permute-start(bf16[256,256]{1,0:T(8,128)(2,1)} %refs_6_.1), channel_id=1, source_target_pairs={{0,1},{1,0},{2,3},{3,2},{4,5},{5,4},{6,7},{7,6},{8,9},{9,8},{10,11... | collective-permute-start | bytes 393224 | tf_op jit(solution)/shard_map/ppermute | solution.py:585
  3.5 9.8 %collective-permute-start.3 = (bf16[256,256]{1,0:T(8,128)(2,1)}, bf16[256,256]{1,0:T(8,128)(2,1)S(1)}, u32[]{:S(2)}, u32[]{:S(2)}) collective-permute-start(bf16[256,256]{1,0:T(8,128)(2,1)} %refs_6_.1), channel_id=1, source_target_pairs={{0,6},{1,7},{2,0},{3,1},{4,2},{5,3},{6,4},{7,5},{8,14},{9,15},{10,... | collective-permute-start | bytes 393224 | tf_op jit(solution)/shard_map/ppermute | solution.py:585
  4.3 8.9 %collective-permute-start.4 = (bf16[256,256]{1,0:T(8,128)(2,1)}, bf16[256,256]{1,0:T(8,128)(2,1)S(1)}, u32[]{:S(2)}, u32[]{:S(2)}) collective-permute-start(bf16[256,256]{1,0:T(8,128)(2,1)} %refs_6_.1), channel_id=1, source_target_pairs={{0,3},{1,2},{2,5},{3,4},{4,7},{5,6},{6,1},{7,0},{8,11},{9,10},{10,... | collective-permute-start | bytes 393224 | tf_op jit(solution)/shard_map/ppermute | solution.py:585
  19.1 11.3 %collective-permute-start.8 = (bf16[528,256]{1,0:T(8,128)(2,1)S(1)}, bf16[528,256]{1,0:T(8,128)(2,1)S(1)}, u32[]{:S(2)}, u32[]{:S(2)}) collective-permute-start(bf16[528,256]{1,0:T(8,128)(2,1)S(1)} %get-tuple-element.95.own), channel_id=1, source_target_pairs={{0,32},{32,64},{64,96},{96,128},{128,160},{160,192},{192,224},{224... | collective-permute-start | bytes 811016 | tf_op jit(solution)/shard_map/ppermute | solution.py:609
  19.4 11.0 %collective-permute-start.9 = (bf16[528,256]{1,0:T(8,128)(2,1)S(1)}, bf16[528,256]{1,0:T(8,128)(2,1)S(1)}, u32[]{:S(2)}, u32[]{:S(2)}) collective-permute-start(bf16[528,256]{1,0:T(8,128)(2,1)S(1)} %get-tuple-element.95.own), channel_id=1, source_target_pairs={{0,224},{32,0},{64,32},{96,64},{128,96},{160,128},{192,160},{224,1... | collective-permute-start | bytes 811016 | tf_op jit(solution)/shard_map/ppermute | solution.py:609
  30.5 8.9 %collective-permute-start.11 = (bf16[528,256]{1,0:T(8,128)(2,1)S(1)}, bf16[528,256]{1,0:T(8,128)(2,1)S(1)}, u32[]{:S(2)}, u32[]{:S(2)}) collective-permute-start(bf16[528,256]{1,0:T(8,128)(2,1)S(1)} %collective-permute-done.8.f), channel_id=1, source_target_pairs={{0,32},{32,64},{64,96},{96,128},{128,160},{160,192},{192,224},{224... | collective-permute-start | bytes 811016 | tf_op jit(solution)/shard_map/ppermute | solution.py:609
  30.5 8.9 %collective-permute-start.12 = (bf16[528,256]{1,0:T(8,128)(2,1)S(1)}, bf16[528,256]{1,0:T(8,128)(2,1)S(1)}, u32[]{:S(2)}, u32[]{:S(2)}) collective-permute-start(bf16[528,256]{1,0:T(8,128)(2,1)S(1)} %collective-permute-done.9.b), channel_id=1, source_target_pairs={{0,224},{32,0},{64,32},{96,64},{128,96},{160,128},{192,160},{224,1... | collective-permute-start | bytes 811016 | tf_op jit(solution)/shard_map/ppermute | solution.py:609
  39.4 8.0 %collective-permute-start.13 = (bf16[528,256]{1,0:T(8,128)(2,1)S(1)}, bf16[528,256]{1,0:T(8,128)(2,1)S(1)}, u32[]{:S(2)}, u32[]{:S(2)}) collective-permute-start(bf16[528,256]{1,0:T(8,128)(2,1)S(1)} %collective-permute-done.11.f), channel_id=1, source_target_pairs={{0,32},{32,64},{64,96},{96,128},{128,160},{160,192},{192,224},{224... | collective-permute-start | bytes 811016 | tf_op jit(solution)/shard_map/ppermute | solution.py:609
  47.7 14.6 %collective-permute-start.17 = (bf16[1056,2048]{1,0:T(8,128)(2,1)}, bf16[1056,2048]{1,0:T(8,128)(2,1)}, u32[]{:S(2)}, u32[]{:S(2)}) collective-permute-start(bf16[1056,2048]{1,0:T(8,128)(2,1)} %pad_maximum_fusion.own), channel_id=1, source_target_pairs={{0,8},{8,0},{1,9},{9,1},{2,10},{10,2},{3,11},{11,3},{4,12},{12,4},... | collective-permute-start | bytes 12976136 | tf_op jit(solution)/shard_map/ppermute | solution.py:633
  47.7 7.7 %collective-permute-start.15 = (bf16[528,256]{1,0:T(8,128)(2,1)S(1)}, bf16[528,256]{1,0:T(8,128)(2,1)S(1)}, u32[]{:S(2)}, u32[]{:S(2)}) collective-permute-start(bf16[528,256]{1,0:T(8,128)(2,1)S(1)} %broadcast_select_fusion), channel_id=1, source_target_pairs={{0,32},{8,232},{32,64},{40,8},{64,96},{72,40},{96,128},{104,72},{1... | collective-permute-start | bytes 811016 | tf_op jit(solution)/shard_map/ppermute | solution.py:631
  66.5 9.4 %collective-permute-start.19 = (bf16[256,256]{1,0:T(8,128)(2,1)S(1)}, bf16[256,256]{1,0:T(8,128)(2,1)S(1)}, u32[]{:S(2)}, u32[]{:S(2)}) collective-permute-start(bf16[256,256]{1,0:T(8,128)(2,1)S(1)} %get-tuple-element.129), channel_id=1, source_target_pairs={{0,1},{1,0},{2,3},{3,2},{4,5},{5,4},{6,7},{7,6},{8,9},{9,8},{10,11... | collective-permute-start | bytes 393224 | tf_op jit(solution)/shard_map/ppermute | solution.py:585
  100.7 9.9 %collective-permute-start.29 = (bf16[512,256]{1,0:T(8,128)(2,1)S(1)}, bf16[512,256]{1,0:T(8,128)(2,1)S(1)}, u32[]{:S(2)}, u32[]{:S(2)}) collective-permute-start(bf16[512,256]{1,0:T(8,128)(2,1)S(1)} %bitcast.17), channel_id=1, source_target_pairs={{0,2},{1,3},{2,4},{3,5},{4,6},{5,7},{6,0},{7,1},{8,10},{9,11},{10,... | collective-permute-start | bytes 786440 | tf_op jit(solution)/shard_map/ppermute | solution.py:585
  102.4 10.3 %collective-permute-start.31 = (bf16[512,256]{1,0:T(8,128)(2,1)S(1)}, bf16[512,256]{1,0:T(8,128)(2,1)S(1)}, u32[]{:S(2)}, u32[]{:S(2)}) collective-permute-start(bf16[512,256]{1,0:T(8,128)(2,1)S(1)} %bitcast.18), channel_id=1, source_target_pairs={{0,7},{1,6},{2,1},{3,0},{4,3},{5,2},{6,5},{7,4},{8,15},{9,14},{10,... | collective-permute-start | bytes 786440 | tf_op jit(solution)/shard_map/ppermute | solution.py:585
  103.3 14.8 %collective-permute-start.26 = (bf16[512,256]{1,0:T(8,128)(2,1)S(1)}, bf16[512,256]{1,0:T(8,128)(2,1)S(1)}, u32[]{:S(2)}, u32[]{:S(2)}) collective-permute-start(bf16[512,256]{1,0:T(8,128)(2,1)S(1)} %bitcast.19), channel_id=1, source_target_pairs={{0,1},{1,0},{2,3},{3,2},{4,5},{5,4},{6,7},{7,6},{8,9},{9,8},{10,11... | collective-permute-start | bytes 786440 | tf_op jit(solution)/shard_map/ppermute | solution.py:585
  104.2 13.9 %collective-permute-start.27 = (bf16[512,256]{1,0:T(8,128)(2,1)S(1)}, bf16[512,256]{1,0:T(8,128)(2,1)S(1)}, u32[]{:S(2)}, u32[]{:S(2)}) collective-permute-start(bf16[512,256]{1,0:T(8,128)(2,1)S(1)} %bitcast.20), channel_id=1, source_target_pairs={{0,6},{1,7},{2,0},{3,1},{4,2},{5,3},{6,4},{7,5},{8,14},{9,15},{10,... | collective-permute-start | bytes 786440 | tf_op jit(solution)/shard_map/ppermute | solution.py:585
  104.6 13.5 %collective-permute-start.28 = (bf16[512,256]{1,0:T(8,128)(2,1)S(1)}, bf16[512,256]{1,0:T(8,128)(2,1)S(1)}, u32[]{:S(2)}, u32[]{:S(2)}) collective-permute-start(bf16[512,256]{1,0:T(8,128)(2,1)S(1)} %bitcast.21), channel_id=1, source_target_pairs={{0,3},{1,2},{2,5},{3,4},{4,7},{5,6},{6,1},{7,0},{8,11},{9,10},{10,... | collective-permute-start | bytes 786440 | tf_op jit(solution)/shard_map/ppermute | solution.py:585
  126.5 9.1 %collective-permute-start.33 = (bf16[512,256]{1,0:T(8,128)(2,1)S(1)}, bf16[512,256]{1,0:T(8,128)(2,1)S(1)}, u32[]{:S(2)}, u32[]{:S(2)}) collective-permute-start(bf16[512,256]{1,0:T(8,128)(2,1)S(1)} %get-tuple-element.147), channel_id=1, source_target_pairs={{0,2},{1,3},{2,4},{3,5},{4,6},{5,7},{6,0},{7,1},{8,10},{9,11},{10,... | collective-permute-start | bytes 786440 | tf_op jit(solution)/shard_map/ppermute | solution.py:585
  127.0 10.2 %collective-permute-start.34 = (bf16[512,256]{1,0:T(8,128)(2,1)S(1)}, bf16[512,256]{1,0:T(8,128)(2,1)S(1)}, u32[]{:S(2)}, u32[]{:S(2)}) collective-permute-start(bf16[512,256]{1,0:T(8,128)(2,1)S(1)} %get-tuple-element.148), channel_id=1, source_target_pairs={{0,6},{1,7},{2,0},{3,1},{4,2},{5,3},{6,4},{7,5},{8,14},{9,15},{10,... | collective-permute-start | bytes 786440 | tf_op jit(solution)/shard_map/ppermute | solution.py:585
  128.6 14.2 %collective-permute-start.35 = (bf16[512,256]{1,0:T(8,128)(2,1)S(1)}, bf16[512,256]{1,0:T(8,128)(2,1)S(1)}, u32[]{:S(2)}, u32[]{:S(2)}) collective-permute-start(bf16[512,256]{1,0:T(8,128)(2,1)S(1)} %get-tuple-element.149), channel_id=1, source_target_pairs={{0,1},{1,0},{2,3},{3,2},{4,5},{5,4},{6,7},{7,6},{8,9},{9,8},{10,11... | collective-permute-start | bytes 786440 | tf_op jit(solution)/shard_map/ppermute | solution.py:585
  130.2 15.0 %collective-permute-start.36 = (bf16[512,256]{1,0:T(8,128)(2,1)S(1)}, bf16[512,256]{1,0:T(8,128)(2,1)S(1)}, u32[]{:S(2)}, u32[]{:S(2)}) collective-permute-start(bf16[512,256]{1,0:T(8,128)(2,1)S(1)} %get-tuple-element.151), channel_id=1, source_target_pairs={{0,6},{1,7},{2,0},{3,1},{4,2},{5,3},{6,4},{7,5},{8,14},{9,15},{10,... | collective-permute-start | bytes 786440 | tf_op jit(solution)/shard_map/ppermute | solution.py:585
  130.3 14.9 %collective-permute-start.37 = (bf16[512,256]{1,0:T(8,128)(2,1)S(1)}, bf16[512,256]{1,0:T(8,128)(2,1)S(1)}, u32[]{:S(2)}, u32[]{:S(2)}) collective-permute-start(bf16[512,256]{1,0:T(8,128)(2,1)S(1)} %get-tuple-element.152), channel_id=1, source_target_pairs={{0,3},{1,2},{2,5},{3,4},{4,7},{5,6},{6,1},{7,0},{8,11},{9,10},{10,... | collective-permute-start | bytes 786440 | tf_op jit(solution)/shard_map/ppermute | solution.py:585
  145.2 9.0 %collective-permute-start.39 = (bf16[512,256]{1,0:T(8,128)(2,1)S(1)}, bf16[512,256]{1,0:T(8,128)(2,1)S(1)}, u32[]{:S(2)}, u32[]{:S(2)}) collective-permute-start(bf16[512,256]{1,0:T(8,128)(2,1)S(1)} %get-tuple-element.158), channel_id=1, source_target_pairs={{0,7},{1,6},{2,1},{3,0},{4,3},{5,2},{6,5},{7,4},{8,15},{9,14},{10,... | collective-permute-start | bytes 786440 | tf_op jit(solution)/shard_map/ppermute | solution.py:585
  (24 other events, 307.4 us)

commit v5 on v4

--- a/solution.py
+++ b/solution.py
@@ -594,7 +594,7 @@
     got = tp_shift(pieces[6], 1, 0), tp_shift(pieces[7], 3, 0)
     beside = tp_shift(pieces[3], *NEAR[3])
     if waves:
-        *got, beside = lax.optimization_barrier((*got, beside))
+        beside, *got = lax.optimization_barrier((beside, *got))
     sums = add_pairs(pieces[1], got[0], pieces[2], got[1])
     straight = [tp_shift(p, *s) for p, s in zip(pieces[4:6], NEAR[4:6])]
     return [pieces[0], beside] + straight + [tp_shift(p, *s) for p, s in zip(sums, NEAR[1:3])]

time: 170 us -> 163 us (0.959)
  waiting for transfers between devices: 52.4 us -> 45.1 us
    ppermute x28, waiting for transfers between devices: 32.6 us -> 25.2 us  [tp_shift(): return lax.ppermute(a, TP, pairs)]
  transfers between devices with their start and end apart: 40 -> 40, of which waited for: 22 -> 23; matrix products, arithmetic and copies ran while one was open for 3% -> 3% of each run, Pallas kernels for 6% -> 6%
where the time goes in v5:
time: 163 us
  starting transfers between devices  57.6 us (35%)
  waiting for transfers between devices  45.1 us (28%)
  blocking collectives  35.7 us (22%)
  Pallas kernels  19.4 us (12%)
  other arithmetic  4.52 us (3%)
    ppermute x28, starting transfers between devices, tp_shift(): return lax.ppermute(a, TP, pairs)  37.9 us
    ppermute x28, waiting for transfers between devices, tp_shift(): return lax.ppermute(a, TP, pairs)  25.2 us
    all_to_all x1, blocking collectives, shards(): lax.all_to_all(rows.reshape(EXPERTS, CAP, BLK), CHIPS, 0, 0, tiled=True)  20.9 us
    all_to_all x1, blocking collectives, shards(): lax.all_to_all(summed.reshape(EXPERTS, CAP, BLK), CHIPS, 0, 0, tiled=True)  14.9 us
    ppermute x6, starting transfers between devices, ring(): return lax.ppermute(a, 'z', [(i, (i + step) % 8) for i in range(8)])  10.8 us
    ppermute x4, waiting for transfers between devices, swap(): return lax.ppermute(a, ('yh', 'c'), pairs)  7.21 us
    ppermute x4, starting transfers between devices, swap(): return lax.ppermute(a, ('yh', 'c'), pairs)  7.05 us
    ppermute x6, waiting for transfers between devices, ring(): return lax.ppermute(a, 'z', [(i, (i + step) % 8) for i in range(8)])  6.83 us
  transfers between devices with their start and end apart: 40, of which 23 were waited for; matrix products, arithmetic and copies ran while one was open for 3% of the time, Pallas kernels for 6%

profile of v5, /device:TPU:6, one launch (start us, length us, event | category | flops | bytes accessed | tf_op | source)
XLA Modules:
  0.0 162.6 jit_solution(3649064594523377991)
XLA Ops:
  0.0 2.2 %collective-permute-start = (bf16[256,256]{1,0:T(8,128)(2,1)}, bf16[256,256]{1,0:T(8,128)(2,1)S(1)}, u32[]{:S(2)}, u32[]{:S(2)}) collective-permute-start(bf16[256,256]{1,0:T(8,128)(2,1)} %refs_6_.1), channel_id=1, source_target_pairs={{0,2},{1,3},{2,4},{3,5},{4,6},{5,7},{6,0},{7,1},{8,10},{9,11},{10,... | collective-permute-start | bytes 393224 | tf_op jit(solution)/shard_map/ppermute | solution.py:585
  4.3 3.4 %collective-permute-start.4 = (bf16[256,256]{1,0:T(8,128)(2,1)}, bf16[256,256]{1,0:T(8,128)(2,1)S(1)}, u32[]{:S(2)}, u32[]{:S(2)}) collective-permute-start(bf16[256,256]{1,0:T(8,128)(2,1)} %refs_6_.1), channel_id=1, source_target_pairs={{0,3},{1,2},{2,5},{3,4},{4,7},{5,6},{6,1},{7,0},{8,11},{9,10},{10,... | collective-permute-start | bytes 393224 | tf_op jit(solution)/shard_map/ppermute | solution.py:585
  14.5 2.3 %collective-permute-done.6.b1 = bf16[256,256]{1,0:T(8,128)(2,1)S(1)} collective-permute-done((bf16[256,256]{1,0:T(8,128)(2,1)S(1)}, bf16[256,256]{1,0:T(8,128)(2,1)S(1)}, u32[]{:S(2)}, u32[]{:S(2)}) %collective-permute-start.6) | collective-permute-done | bytes 131104 | tf_op jit(solution)/shard_map/ppermute | solution.py:585
  19.4 4.0 %collective-permute-start.9 = (bf16[528,256]{1,0:T(8,128)(2,1)S(1)}, bf16[528,256]{1,0:T(8,128)(2,1)S(1)}, u32[]{:S(2)}, u32[]{:S(2)}) collective-permute-start(bf16[528,256]{1,0:T(8,128)(2,1)S(1)} %get-tuple-element.95.own), channel_id=1, source_target_pairs={{0,224},{32,0},{64,32},{96,64},{128,96},{160,128},{192,160},{224,1... | collective-permute-start | bytes 811016 | tf_op jit(solution)/shard_map/ppermute | solution.py:609
  23.5 3.4 %collective-permute-start.10 = (bf16[528,128]{1,0:T(8,128)(2,1)S(1)}, bf16[528,128]{1,0:T(8,128)(2,1)S(1)}, u32[]{:S(2)}, u32[]{:S(2)}) collective-permute-start(bf16[528,128]{1,0:T(8,128)(2,1)S(1)} %get-tuple-element.87.mine), channel_id=1, source_target_pairs={{0,16},{8,24},{16,0},{24,8},{1,17},{9,25},{17,1},{25,9},{2,18},{10... | collective-permute-start | bytes 405512 | tf_op jit(solution)/shard_map/ppermute | solution.py:605
  26.9 2.3 %pad_maximum_fusion.own = bf16[1056,2048]{1,0:T(8,128)(2,1)} fusion(bf16[352,2048]{1,0:T(8,128)(2,1)S(1)} %bitcast.29, bf16[352,2048]{1,0:T(8,128)(2,1)S(1)} %bitcast.30, bf16[352,2048]{1,0:T(8,128)(2,1)S(1)} %bitcast.31), kind=kLoop, calls=%fused_computation | loop fusion | flops 12976128 | bytes 8650752 | tf_op jit(solution)/shard_map/concatenate | solution.py:619
  30.5 3.2 %collective-permute-start.12 = (bf16[528,256]{1,0:T(8,128)(2,1)S(1)}, bf16[528,256]{1,0:T(8,128)(2,1)S(1)}, u32[]{:S(2)}, u32[]{:S(2)}) collective-permute-start(bf16[528,256]{1,0:T(8,128)(2,1)S(1)} %collective-permute-done.9.b), channel_id=1, source_target_pairs={{0,224},{32,0},{64,32},{96,64},{128,96},{160,128},{192,160},{224,1... | collective-permute-start | bytes 811016 | tf_op jit(solution)/shard_map/ppermute | solution.py:609
  33.7 3.8 %first.1 = (bf16[1024,128]{1,0:T(8,128)(2,1)S(1)}, f32[1,1024]{1,0:T(1,128)S(1)}, f32[1,1024]{1,0:T(1,128)S(1)}, f32[1,1024]{1,0:T(1,128)S(1)}, f32[128,1024]{1,0:T(8,128)S(1)}) custom-call(bf16[528,128]{1,0:T(8,128)(2,1)S(1)} %get-tuple-element.87.mine, bf16[528,128]{1,0:T(8,128)(2,1)S(1)} %collective-permute-done.10.theirs, ...), custom_call_target="tpu_custom_call" | custom-call | flops 805306368 | bytes 2097152 | tf_op jit(solution)/shard_map/first/pallas_call | solution.py:223
  42.7 4.7 %collective-permute-done.13.f = bf16[528,256]{1,0:T(8,128)(2,1)S(1)} collective-permute-done((bf16[528,256]{1,0:T(8,128)(2,1)S(1)}, bf16[528,256]{1,0:T(8,128)(2,1)S(1)}, u32[]{:S(2)}, u32[]{:S(2)}) %collective-permute-start.13) | collective-permute-done | bytes 270368 | tf_op jit(solution)/shard_map/ppermute | solution.py:609
  49.6 5.8 %collective-permute-done.15.kv = bf16[528,256]{1,0:T(8,128)(2,1)S(1)} collective-permute-done((bf16[528,256]{1,0:T(8,128)(2,1)S(1)}, bf16[528,256]{1,0:T(8,128)(2,1)S(1)}, u32[]{:S(2)}, u32[]{:S(2)}) %collective-permute-start.15) | collective-permute-done | bytes 270368 | tf_op jit(solution)/shard_map/ppermute | solution.py:631
  55.6 3.5 %collective-permute-start.16 = (bf16[144,512]{1,0:T(8,128)(2,1)S(1)}, bf16[144,512]{1,0:T(8,128)(2,1)S(1)}, u32[]{:S(2)}, u32[]{:S(2)}) collective-permute-start(bf16[144,512]{1,0:T(8,128)(2,1)S(1)} %get-tuple-element.123), channel_id=1, source_target_pairs={{0,16},{8,24},{16,0},{24,8},{1,17},{9,25},{17,1},{25,9},{2,18},{10... | collective-permute-start | bytes 442376 | tf_op jit(solution)/shard_map/ppermute | solution.py:605
  59.0 3.3 %collective-permute-done.16.b = bf16[144,512]{1,0:T(8,128)(2,1)S(1)} collective-permute-done((bf16[144,512]{1,0:T(8,128)(2,1)S(1)}, bf16[144,512]{1,0:T(8,128)(2,1)S(1)}, u32[]{:S(2)}, u32[]{:S(2)}) %collective-permute-start.16) | collective-permute-done | bytes 147488 | tf_op jit(solution)/shard_map/ppermute | solution.py:605
  68.7 2.8 %collective-permute-start.21 = (bf16[256,256]{1,0:T(8,128)(2,1)S(1)}, bf16[256,256]{1,0:T(8,128)(2,1)S(1)}, u32[]{:S(2)}, u32[]{:S(2)}) collective-permute-start(bf16[256,256]{1,0:T(8,128)(2,1)S(1)} %get-tuple-element.131), channel_id=1, source_target_pairs={{0,3},{1,2},{2,5},{3,4},{4,7},{5,6},{6,1},{7,0},{8,11},{9,10},{10,... | collective-permute-start | bytes 393224 | tf_op jit(solution)/shard_map/ppermute | solution.py:585
  72.4 3.5 %collective-permute-start.25 = (bf16[256,256]{1,0:T(8,128)(2,1)S(1)}, bf16[256,256]{1,0:T(8,128)(2,1)S(1)}, u32[]{:S(2)}, u32[]{:S(2)}) collective-permute-start(bf16[256,256]{1,0:T(8,128)(2,1)S(1)} %get-tuple-element.137), channel_id=1, source_target_pairs={{0,7},{1,6},{2,1},{3,0},{4,3},{5,2},{6,5},{7,4},{8,15},{9,14},{10,... | collective-permute-start | bytes 393224 | tf_op jit(solution)/shard_map/ppermute | solution.py:585
  76.9 2.6 %collective-permute-done.25.refs_5_ = bf16[256,256]{1,0:T(8,128)(2,1)S(1)} collective-permute-done((bf16[256,256]{1,0:T(8,128)(2,1)S(1)}, bf16[256,256]{1,0:T(8,128)(2,1)S(1)}, u32[]{:S(2)}, u32[]{:S(2)}) %collective-permute-start.25) | collective-permute-done | bytes 131104 | tf_op jit(solution)/shard_map/ppermute | solution.py:585
  79.8 20.9 %all_to_all.10 = bf16[16,32,256]{2,1,0:T(8,128)(2,1)S(1)} all-to-all(bf16[16,32,256]{2,1,0:T(8,128)(2,1)S(1)} %bitcast.25), channel_id=1, replica_groups=mesh['z'=8,'yh'=2,'c'=2,'x'=4,'yl'=2] {'z','yh'}, dimensions={0} | all-to-all | bytes 524288 | tf_op jit(solution)/shard_map/all_to_all | solution.py:651
  104.6 3.4 %collective-permute-start.28 = (bf16[512,256]{1,0:T(8,128)(2,1)S(1)}, bf16[512,256]{1,0:T(8,128)(2,1)S(1)}, u32[]{:S(2)}, u32[]{:S(2)}) collective-permute-start(bf16[512,256]{1,0:T(8,128)(2,1)S(1)} %bitcast.21), channel_id=1, source_target_pairs={{0,3},{1,2},{2,5},{3,4},{4,7},{5,6},{6,1},{7,0},{8,11},{9,10},{10,... | collective-permute-start | bytes 786440 | tf_op jit(solution)/shard_map/ppermute | solution.py:585
  108.0 2.6 %collective-permute-done.29.b1 = bf16[512,256]{1,0:T(8,128)(2,1)S(1)} collective-permute-done((bf16[512,256]{1,0:T(8,128)(2,1)S(1)}, bf16[512,256]{1,0:T(8,128)(2,1)S(1)}, u32[]{:S(2)}, u32[]{:S(2)}) %collective-permute-start.29) | collective-permute-done | bytes 262176 | tf_op jit(solution)/shard_map/ppermute | solution.py:585
  112.7 3.6 %expert_ready.1 = (bf16[1536,2048]{1,0:T(8,128)(2,1)S(1)}, bf16[768,2048]{1,0:T(8,128)(2,1)S(1)}, bf16[512,768]{1,0:T(8,128)(2,1)S(1)}, f32[512,1]{1,0:T(8,128)S(1)}) custom-call(bf16[512,256]{1,0:T(8,128)(2,1)S(1)} %bitcast.22, bf16[512,256]{1,0:T(8,128)(2,1)S(1)} %collective-permute-done.29.b1, bf16[512,256]{1,0:T(8,128)(2,1)S(1)} %collective-permute-done.31.b2, ...), custom_call_target="tpu_custom_call" | custom-call | flops 1048576 | bytes 18874368 | tf_op jit(solution)/shard_map/expert_ready/pallas_call | solution.py:477
  120.3 6.2 %expert_hidden.1 = (bf16[512,768]{1,0:T(8,128)(2,1)S(1)}, bf16[512,256]{1,0:T(8,128)(2,1)S(1)}, bf16[512,256]{1,0:T(8,128)(2,1)S(1)}, bf16[512,256]{1,0:T(8,128)(2,1)S(1)}) custom-call(bf16[512,256]{1,0:T(8,128)(2,1)S(1)} %collective-permute-done.26.refs_0_, bf16[512,256]{1,0:T(8,128)(2,1)S(1)} %collective-permute-done.27.refs_1_, ...), custom_call_target="tpu_custom_call" | custom-call | flops 4026531840 | bytes 13631488 | tf_op jit(solution)/shard_map/expert_hidden/pallas_call | solution.py:530
  130.3 4.5 %collective-permute-start.37 = (bf16[512,256]{1,0:T(8,128)(2,1)S(1)}, bf16[512,256]{1,0:T(8,128)(2,1)S(1)}, u32[]{:S(2)}, u32[]{:S(2)}) collective-permute-start(bf16[512,256]{1,0:T(8,128)(2,1)S(1)} %get-tuple-element.152), channel_id=1, source_target_pairs={{0,3},{1,2},{2,5},{3,4},{4,7},{5,6},{6,1},{7,0},{8,11},{9,10},{10,... | collective-permute-start | bytes 786440 | tf_op jit(solution)/shard_map/ppermute | solution.py:585
  139.9 2.5 %collective-permute-done.36.refs_2_ = bf16[512,256]{1,0:T(8,128)(2,1)S(1)} collective-permute-done((bf16[512,256]{1,0:T(8,128)(2,1)S(1)}, bf16[512,256]{1,0:T(8,128)(2,1)S(1)}, u32[]{:S(2)}, u32[]{:S(2)}) %collective-permute-start.36) | collective-permute-done | bytes 262176 | tf_op jit(solution)/shard_map/ppermute | solution.py:585
  144.4 2.2 %collective-permute-done.39.refs_5_ = bf16[512,256]{1,0:T(8,128)(2,1)S(1)} collective-permute-done((bf16[512,256]{1,0:T(8,128)(2,1)S(1)}, bf16[512,256]{1,0:T(8,128)(2,1)S(1)}, u32[]{:S(2)}, u32[]{:S(2)}) %collective-permute-start.39) | collective-permute-done | bytes 262176 | tf_op jit(solution)/shard_map/ppermute | solution.py:585
  146.8 14.9 %all_to_all.11 = bf16[16,32,256]{2,1,0:T(8,128)(2,1)S(1)} all-to-all(bf16[16,32,256]{2,1,0:T(8,128)(2,1)S(1)} %bitcast.23), channel_id=1, replica_groups=mesh['z'=8,'yh'=2,'c'=2,'x'=4,'yl'=2] {'z','yh'}, dimensions={0} | all-to-all | bytes 524288 | tf_op jit(solution)/shard_map/all_to_all | solution.py:657
  (96 shorter events, 50.7 us)
Async XLA Ops:
  0.0 7.7 %collective-permute-start = (bf16[256,256]{1,0:T(8,128)(2,1)}, bf16[256,256]{1,0:T(8,128)(2,1)S(1)}, u32[]{:S(2)}, u32[]{:S(2)}) collective-permute-start(bf16[256,256]{1,0:T(8,128)(2,1)} %refs_6_.1), channel_id=1, source_target_pairs={{0,2},{1,3},{2,4},{3,5},{4,6},{5,7},{6,0},{7,1},{8,10},{9,11},{10,... | collective-permute-start | bytes 393224 | tf_op jit(solution)/shard_map/ppermute | solution.py:585
  2.2 8.4 %collective-permute-start.1 = (bf16[256,256]{1,0:T(8,128)(2,1)}, bf16[256,256]{1,0:T(8,128)(2,1)S(1)}, u32[]{:S(2)}, u32[]{:S(2)}) collective-permute-start(bf16[256,256]{1,0:T(8,128)(2,1)} %refs_6_.1), channel_id=1, source_target_pairs={{0,7},{1,6},{2,1},{3,0},{4,3},{5,2},{6,5},{7,4},{8,15},{9,14},{10,... | collective-permute-start | bytes 393224 | tf_op jit(solution)/shard_map/ppermute | solution.py:585
  3.0 10.2 %collective-permute-start.2 = (bf16[256,256]{1,0:T(8,128)(2,1)}, bf16[256,256]{1,0:T(8,128)(2,1)S(1)}, u32[]{:S(2)}, u32[]{:S(2)}) collective-permute-start(bf16[256,256]{1,0:T(8,128)(2,1)} %refs_6_.1), channel_id=1, source_target_pairs={{0,1},{1,0},{2,3},{3,2},{4,5},{5,4},{6,7},{7,6},{8,9},{9,8},{10,11... | collective-permute-start | bytes 393224 | tf_op jit(solution)/shard_map/ppermute | solution.py:585
  3.5 9.8 %collective-permute-start.3 = (bf16[256,256]{1,0:T(8,128)(2,1)}, bf16[256,256]{1,0:T(8,128)(2,1)S(1)}, u32[]{:S(2)}, u32[]{:S(2)}) collective-permute-start(bf16[256,256]{1,0:T(8,128)(2,1)} %refs_6_.1), channel_id=1, source_target_pairs={{0,6},{1,7},{2,0},{3,1},{4,2},{5,3},{6,4},{7,5},{8,14},{9,15},{10,... | collective-permute-start | bytes 393224 | tf_op jit(solution)/shard_map/ppermute | solution.py:585
  4.3 8.9 %collective-permute-start.4 = (bf16[256,256]{1,0:T(8,128)(2,1)}, bf16[256,256]{1,0:T(8,128)(2,1)S(1)}, u32[]{:S(2)}, u32[]{:S(2)}) collective-permute-start(bf16[256,256]{1,0:T(8,128)(2,1)} %refs_6_.1), channel_id=1, source_target_pairs={{0,3},{1,2},{2,5},{3,4},{4,7},{5,6},{6,1},{7,0},{8,11},{9,10},{10,... | collective-permute-start | bytes 393224 | tf_op jit(solution)/shard_map/ppermute | solution.py:585
  19.1 11.3 %collective-permute-start.8 = (bf16[528,256]{1,0:T(8,128)(2,1)S(1)}, bf16[528,256]{1,0:T(8,128)(2,1)S(1)}, u32[]{:S(2)}, u32[]{:S(2)}) collective-permute-start(bf16[528,256]{1,0:T(8,128)(2,1)S(1)} %get-tuple-element.95.own), channel_id=1, source_target_pairs={{0,32},{32,64},{64,96},{96,128},{128,160},{160,192},{192,224},{224... | collective-permute-start | bytes 811016 | tf_op jit(solution)/shard_map/ppermute | solution.py:609
  19.4 11.0 %collective-permute-start.9 = (bf16[528,256]{1,0:T(8,128)(2,1)S(1)}, bf16[528,256]{1,0:T(8,128)(2,1)S(1)}, u32[]{:S(2)}, u32[]{:S(2)}) collective-permute-start(bf16[528,256]{1,0:T(8,128)(2,1)S(1)} %get-tuple-element.95.own), channel_id=1, source_target_pairs={{0,224},{32,0},{64,32},{96,64},{128,96},{160,128},{192,160},{224,1... | collective-permute-start | bytes 811016 | tf_op jit(solution)/shard_map/ppermute | solution.py:609
  30.5 8.9 %collective-permute-start.11 = (bf16[528,256]{1,0:T(8,128)(2,1)S(1)}, bf16[528,256]{1,0:T(8,128)(2,1)S(1)}, u32[]{:S(2)}, u32[]{:S(2)}) collective-permute-start(bf16[528,256]{1,0:T(8,128)(2,1)S(1)} %collective-permute-done.8.f), channel_id=1, source_target_pairs={{0,32},{32,64},{64,96},{96,128},{128,160},{160,192},{192,224},{224... | collective-permute-start | bytes 811016 | tf_op jit(solution)/shard_map/ppermute | solution.py:609
  30.5 8.9 %collective-permute-start.12 = (bf16[528,256]{1,0:T(8,128)(2,1)S(1)}, bf16[528,256]{1,0:T(8,128)(2,1)S(1)}, u32[]{:S(2)}, u32[]{:S(2)}) collective-permute-start(bf16[528,256]{1,0:T(8,128)(2,1)S(1)} %collective-permute-done.9.b), channel_id=1, source_target_pairs={{0,224},{32,0},{64,32},{96,64},{128,96},{160,128},{192,160},{224,1... | collective-permute-start | bytes 811016 | tf_op jit(solution)/shard_map/ppermute | solution.py:609
  39.4 8.0 %collective-permute-start.13 = (bf16[528,256]{1,0:T(8,128)(2,1)S(1)}, bf16[528,256]{1,0:T(8,128)(2,1)S(1)}, u32[]{:S(2)}, u32[]{:S(2)}) collective-permute-start(bf16[528,256]{1,0:T(8,128)(2,1)S(1)} %collective-permute-done.11.f), channel_id=1, source_target_pairs={{0,32},{32,64},{64,96},{96,128},{128,160},{160,192},{192,224},{224... | collective-permute-start | bytes 811016 | tf_op jit(solution)/shard_map/ppermute | solution.py:609
  47.7 14.6 %collective-permute-start.17 = (bf16[1056,2048]{1,0:T(8,128)(2,1)}, bf16[1056,2048]{1,0:T(8,128)(2,1)}, u32[]{:S(2)}, u32[]{:S(2)}) collective-permute-start(bf16[1056,2048]{1,0:T(8,128)(2,1)} %pad_maximum_fusion.own), channel_id=1, source_target_pairs={{0,8},{8,0},{1,9},{9,1},{2,10},{10,2},{3,11},{11,3},{4,12},{12,4},... | collective-permute-start | bytes 12976136 | tf_op jit(solution)/shard_map/ppermute | solution.py:633
  47.7 7.7 %collective-permute-start.15 = (bf16[528,256]{1,0:T(8,128)(2,1)S(1)}, bf16[528,256]{1,0:T(8,128)(2,1)S(1)}, u32[]{:S(2)}, u32[]{:S(2)}) collective-permute-start(bf16[528,256]{1,0:T(8,128)(2,1)S(1)} %broadcast_select_fusion), channel_id=1, source_target_pairs={{0,32},{8,232},{32,64},{40,8},{64,96},{72,40},{96,128},{104,72},{1... | collective-permute-start | bytes 811016 | tf_op jit(solution)/shard_map/ppermute | solution.py:631
  66.5 9.4 %collective-permute-start.19 = (bf16[256,256]{1,0:T(8,128)(2,1)S(1)}, bf16[256,256]{1,0:T(8,128)(2,1)S(1)}, u32[]{:S(2)}, u32[]{:S(2)}) collective-permute-start(bf16[256,256]{1,0:T(8,128)(2,1)S(1)} %get-tuple-element.129), channel_id=1, source_target_pairs={{0,1},{1,0},{2,3},{3,2},{4,5},{5,4},{6,7},{7,6},{8,9},{9,8},{10,11... | collective-permute-start | bytes 393224 | tf_op jit(solution)/shard_map/ppermute | solution.py:585
  100.7 9.9 %collective-permute-start.29 = (bf16[512,256]{1,0:T(8,128)(2,1)S(1)}, bf16[512,256]{1,0:T(8,128)(2,1)S(1)}, u32[]{:S(2)}, u32[]{:S(2)}) collective-permute-start(bf16[512,256]{1,0:T(8,128)(2,1)S(1)} %bitcast.17), channel_id=1, source_target_pairs={{0,2},{1,3},{2,4},{3,5},{4,6},{5,7},{6,0},{7,1},{8,10},{9,11},{10,... | collective-permute-start | bytes 786440 | tf_op jit(solution)/shard_map/ppermute | solution.py:585
  102.4 10.3 %collective-permute-start.31 = (bf16[512,256]{1,0:T(8,128)(2,1)S(1)}, bf16[512,256]{1,0:T(8,128)(2,1)S(1)}, u32[]{:S(2)}, u32[]{:S(2)}) collective-permute-start(bf16[512,256]{1,0:T(8,128)(2,1)S(1)} %bitcast.18), channel_id=1, source_target_pairs={{0,7},{1,6},{2,1},{3,0},{4,3},{5,2},{6,5},{7,4},{8,15},{9,14},{10,... | collective-permute-start | bytes 786440 | tf_op jit(solution)/shard_map/ppermute | solution.py:585
  103.3 14.8 %collective-permute-start.26 = (bf16[512,256]{1,0:T(8,128)(2,1)S(1)}, bf16[512,256]{1,0:T(8,128)(2,1)S(1)}, u32[]{:S(2)}, u32[]{:S(2)}) collective-permute-start(bf16[512,256]{1,0:T(8,128)(2,1)S(1)} %bitcast.19), channel_id=1, source_target_pairs={{0,1},{1,0},{2,3},{3,2},{4,5},{5,4},{6,7},{7,6},{8,9},{9,8},{10,11... | collective-permute-start | bytes 786440 | tf_op jit(solution)/shard_map/ppermute | solution.py:585
  104.2 13.9 %collective-permute-start.27 = (bf16[512,256]{1,0:T(8,128)(2,1)S(1)}, bf16[512,256]{1,0:T(8,128)(2,1)S(1)}, u32[]{:S(2)}, u32[]{:S(2)}) collective-permute-start(bf16[512,256]{1,0:T(8,128)(2,1)S(1)} %bitcast.20), channel_id=1, source_target_pairs={{0,6},{1,7},{2,0},{3,1},{4,2},{5,3},{6,4},{7,5},{8,14},{9,15},{10,... | collective-permute-start | bytes 786440 | tf_op jit(solution)/shard_map/ppermute | solution.py:585
  104.6 13.5 %collective-permute-start.28 = (bf16[512,256]{1,0:T(8,128)(2,1)S(1)}, bf16[512,256]{1,0:T(8,128)(2,1)S(1)}, u32[]{:S(2)}, u32[]{:S(2)}) collective-permute-start(bf16[512,256]{1,0:T(8,128)(2,1)S(1)} %bitcast.21), channel_id=1, source_target_pairs={{0,3},{1,2},{2,5},{3,4},{4,7},{5,6},{6,1},{7,0},{8,11},{9,10},{10,... | collective-permute-start | bytes 786440 | tf_op jit(solution)/shard_map/ppermute | solution.py:585
  126.5 9.1 %collective-permute-start.33 = (bf16[512,256]{1,0:T(8,128)(2,1)S(1)}, bf16[512,256]{1,0:T(8,128)(2,1)S(1)}, u32[]{:S(2)}, u32[]{:S(2)}) collective-permute-start(bf16[512,256]{1,0:T(8,128)(2,1)S(1)} %get-tuple-element.147), channel_id=1, source_target_pairs={{0,1},{1,0},{2,3},{3,2},{4,5},{5,4},{6,7},{7,6},{8,9},{9,8},{10,11... | collective-permute-start | bytes 786440 | tf_op jit(solution)/shard_map/ppermute | solution.py:585
  126.7 9.2 %collective-permute-start.34 = (bf16[512,256]{1,0:T(8,128)(2,1)S(1)}, bf16[512,256]{1,0:T(8,128)(2,1)S(1)}, u32[]{:S(2)}, u32[]{:S(2)}) collective-permute-start(bf16[512,256]{1,0:T(8,128)(2,1)S(1)} %get-tuple-element.148), channel_id=1, source_target_pairs={{0,2},{1,3},{2,4},{3,5},{4,6},{5,7},{6,0},{7,1},{8,10},{9,11},{10,... | collective-permute-start | bytes 786440 | tf_op jit(solution)/shard_map/ppermute | solution.py:585
  127.4 10.4 %collective-permute-start.35 = (bf16[512,256]{1,0:T(8,128)(2,1)S(1)}, bf16[512,256]{1,0:T(8,128)(2,1)S(1)}, u32[]{:S(2)}, u32[]{:S(2)}) collective-permute-start(bf16[512,256]{1,0:T(8,128)(2,1)S(1)} %get-tuple-element.149), channel_id=1, source_target_pairs={{0,6},{1,7},{2,0},{3,1},{4,2},{5,3},{6,4},{7,5},{8,14},{9,15},{10,... | collective-permute-start | bytes 786440 | tf_op jit(solution)/shard_map/ppermute | solution.py:585
  130.2 12.2 %collective-permute-start.36 = (bf16[512,256]{1,0:T(8,128)(2,1)S(1)}, bf16[512,256]{1,0:T(8,128)(2,1)S(1)}, u32[]{:S(2)}, u32[]{:S(2)}) collective-permute-start(bf16[512,256]{1,0:T(8,128)(2,1)S(1)} %get-tuple-element.151), channel_id=1, source_target_pairs={{0,6},{1,7},{2,0},{3,1},{4,2},{5,3},{6,4},{7,5},{8,14},{9,15},{10,... | collective-permute-start | bytes 786440 | tf_op jit(solution)/shard_map/ppermute | solution.py:585
  130.3 12.1 %collective-permute-start.37 = (bf16[512,256]{1,0:T(8,128)(2,1)S(1)}, bf16[512,256]{1,0:T(8,128)(2,1)S(1)}, u32[]{:S(2)}, u32[]{:S(2)}) collective-permute-start(bf16[512,256]{1,0:T(8,128)(2,1)S(1)} %get-tuple-element.152), channel_id=1, source_target_pairs={{0,3},{1,2},{2,5},{3,4},{4,7},{5,6},{6,1},{7,0},{8,11},{9,10},{10,... | collective-permute-start | bytes 786440 | tf_op jit(solution)/shard_map/ppermute | solution.py:585
  138.0 8.6 %collective-permute-start.39 = (bf16[512,256]{1,0:T(8,128)(2,1)S(1)}, bf16[512,256]{1,0:T(8,128)(2,1)S(1)}, u32[]{:S(2)}, u32[]{:S(2)}) collective-permute-start(bf16[512,256]{1,0:T(8,128)(2,1)S(1)} %get-tuple-element.158), channel_id=1, source_target_pairs={{0,7},{1,6},{2,1},{3,0},{4,3},{5,2},{6,5},{7,4},{8,15},{9,14},{10,... | collective-permute-start | bytes 786440 | tf_op jit(solution)/shard_map/ppermute | solution.py:585
  (24 other events, 307.4 us)
